TPU v7x, 32 devices: a whole 2x2x4 slice. The times are simulated.
32 devices in a mesh: head: 8 (over z, y), qblk: 4 (over x, core).
Axes of the slice: x: 2, y: 2, z: 4, core: 2. Of those that a mesh axis runs over, the one named last changes fastest.
Arguments:
- residual: bfloat16 [1024, 2048], P(('qblk', 'head')), may hold values from -6 to 6
- queries: bfloat16 [1024, 4096], P('qblk', 'head'), may hold values from -30 to 30
- key_cache: bfloat16 [4, 2048, 128], P(None, 'qblk'), may hold values from -6 to 6
- value_cache: bfloat16 [4, 2048, 128], P(None, 'qblk'), may hold values from -6 to 6
- visible_len: int32 [1024], P('qblk'), may hold values from 256 to 2048
- out_weight: bfloat16 [4096, 2048], P('head'), may hold values from -0.5 to 0.5
- norm_gain: float32 [2048], replicated, may hold values from 0.1 to 1.9
- expert_ids: int32 [1024, 8], P(('qblk', 'head')), may hold values from 0 to 31, all different within a row; in each aligned block of 32 rows (0 to 31, 32 to 63, ...) at most 16 rows name the same one
- route_weights: float32 [1024, 8], P(('qblk', 'head')), may hold values from 0.02 to 0.3
- w_gate: bfloat16 [32, 2048, 768], P(('head', 'qblk')), may hold values from -0.125 to 0.125
- w_up: bfloat16 [32, 2048, 768], P(('head', 'qblk')), may hold values from -0.125 to 0.125
- w_down: bfloat16 [32, 768, 2048], P(('head', 'qblk')), may hold values from -0.21875 to 0.21875
Outputs:
- layer_out: bfloat16 [1024, 2048], P(('qblk', 'head'))
Inputs may be any that keep to these rules, and one draw needn't show every extreme that they name: `expert_ids`: each row names 8 different experts; in each aligned block of 32 rows (the rows of one device) no expert is named more than 16 times, and some block names some expert exactly 16 times.
All inputs are finite; a program needn't handle non-finite values.
Results may differ from a plain program's by a relative error of at most 0.012.
Values may be sent and summed in bfloat16 or wider, within the bound.
No kernel may reach another device: no remote copies, remote signals or barrier semaphores. Data moves between devices by JAX's collectives and lax.ppermute only.
A program may use at most 64 MiB of HBM per device.

v0:
```python
import functools
import math

import jax
import jax.numpy as jnp
from jax import lax
from jax.experimental import pallas as pl
from jax.experimental.pallas import tpu as pltpu
from jax.sharding import PartitionSpec as P


QH = 32
KVH = 4
HD = 128
F32 = jnp.float32
BF16 = jnp.bfloat16
LANES = 128
TILE = 256
MIB = 1 << 20
COVER = 2 * 10**10


def swap(v, link):
    axis, mask = link
    return lax.ppermute(v, axis, [(i, i ^ mask) for i in range(lax.axis_size(axis))])


def links():
    core, x, y, z = ("qblk", 1), ("qblk", 2), ("head", 1), ("head", 2)
    far = []
    for axis in ("head", "qblk"):
        bit = 4
        while bit < lax.axis_size(axis):
            far.append((axis, bit | bit >> 1))
            bit *= 2
    return core, x, y, z, far


def masks_of(chosen):
    order = [0]
    for _, mask in chosen:
        order = order + [o ^ mask for o in order]
    return order


def call(kernel, outs, args, specs, scratch, flops, grant):
    nbytes = sum(math.prod(a.shape) * a.dtype.itemsize for a in (*args, *outs))
    return pl.pallas_call(
        kernel,
        out_shape=outs,
        in_specs=specs,
        out_specs=[pl.BlockSpec(memory_space=pltpu.VMEM)] * len(outs),
        scratch_shapes=scratch,
        compiler_params=pltpu.CompilerParams(vmem_limit_bytes=grant),
        cost_estimate=pl.CostEstimate(flops=flops, bytes_accessed=nbytes, transcendentals=0),
    )(*args)


IN_VMEM = pl.BlockSpec(memory_space=pltpu.VMEM)
IN_SMEM = pl.BlockSpec(memory_space=pltpu.SMEM)


def attention_kernel(cfg, where, query, lens, *refs):
    kv, out_weight = refs[: cfg["blocks"]], refs[cfg["blocks"]]
    send_a, keep_a, send_b, keep_b, stacked, scores, attended, column = refs[cfg["blocks"] + 1 :]
    count = lens.shape[1]
    square = (count, count)
    diagonal = lax.broadcasted_iota(jnp.int32, square, 0) == lax.broadcasted_iota(
        jnp.int32, square, 1
    )
    lens_row = jnp.broadcast_to(lens[...].astype(F32), square)
    column[...] = jnp.sum(jnp.where(diagonal, lens_row, 0.0), axis=1, keepdims=True)
    token_rows, heads, near = cfg["token_rows"], cfg["heads"], cfg["near"]
    head_me, qblk_me = where[0], where[1]
    tile = 2 * near
    keys = kv[0].shape[0]
    factor = HD ** (-0.5) * math.log2(math.e)
    group = max(1, TILE // tile)
    half = out_weight.shape[1] // 2
    for z in (1, 0):
        starts = []
        for o in cfg["order"][z]:
            starts.append(pl.multiple_of((head_me ^ o) * token_rows, token_rows))
        span = jnp.concatenate([column[pl.ds(s, token_rows), :] for s in starts], axis=0)
        span = jnp.concatenate([span] * group, axis=0)
        for first in range(0, heads, group):
            for h in range(group):
                lanes = pl.ds((first + h) * HD, HD)
                for i, s in enumerate(starts):
                    rows = pl.ds(h * tile + i * token_rows, token_rows)
                    stacked[rows, :] = query[pl.ds(s, token_rows), lanes]
            q = stacked[...]
            top = None
            for b in range(cfg["blocks"]):
                s = lax.dot_general(
                    q, kv[b][:, :HD], (((1,), (1,)), ((), ())), preferred_element_type=F32
                )
                base = (qblk_me ^ cfg["offsets"][b]) * keys
                pos = base + lax.broadcasted_iota(jnp.int32, s.shape, 1)
                s = jnp.where(pos.astype(F32) < span, s, -1e30)
                scores[:, b * keys : (b + 1) * keys] = s
                here = jnp.max(s, axis=1, keepdims=True)
                top = here if top is None else jnp.maximum(top, here)
            denom, mixed = 0.0, 0.0
            for b in range(cfg["blocks"]):
                s = scores[:, b * keys : (b + 1) * keys]
                w = jnp.exp2((s - top) * factor)
                denom = denom + jnp.sum(w, axis=1, keepdims=True)
                mixed = mixed + jnp.dot(
                    w.astype(BF16), kv[b][:, HD:], preferred_element_type=F32
                )
            result = (mixed / denom).astype(BF16)
            for h in range(group):
                attended[:, (first + h) * HD : (first + h + 1) * HD] = result[
                    h * tile : (h + 1) * tile
                ]
        a = attended[...]
        for col in range(0, 2 * half, TILE):
            p = jnp.dot(a, out_weight[:, col : col + TILE], preferred_element_type=F32)
            for y in (0, 1):
                rows = p[y * near : (y + 1) * near]
                if col < half:
                    at = slice(col, col + TILE)
                    if z:
                        send_a[y, :, at] = rows.astype(BF16)
                    else:
                        keep_a[y, :, at] = rows
                else:
                    at = slice(col - half, col - half + TILE)
                    if y:
                        send_b[z, :, at] = rows.astype(BF16)
                    else:
                        keep_b[z, :, at] = rows


def attention(where, queries, visible_len, kv, offsets, out_weight, token_rows):
    _, _, y, z, far = links()
    tokens, lanes = queries.shape
    heads = lanes // HD
    far = [link for link in far if link[0] == "head"]
    order = masks_of([*far, y, z])
    blocks = len(order) // 2
    near = blocks // 2 * token_rows
    half = out_weight.shape[1] // 2
    cfg = dict(
        blocks=len(kv),
        token_rows=token_rows,
        heads=heads,
        near=near,
        order=(order[:blocks], order[blocks:]),
        offsets=offsets,
    )
    tile = 2 * near
    rows = max(1, TILE // tile) * tile
    keys = kv[0].shape[0] * len(kv)
    outs = [
        jax.ShapeDtypeStruct((2, near, half), kind) for kind in (BF16, F32, BF16, F32)
    ]
    return call(
        functools.partial(attention_kernel, cfg),
        outs,
        [where, queries, visible_len.reshape(1, tokens), *kv, out_weight],
        [IN_SMEM] + [IN_VMEM] * (3 + len(kv)),
        [
            pltpu.VMEM((rows, HD), BF16),
            pltpu.VMEM((rows, keys), F32),
            pltpu.VMEM((tile, lanes), BF16),
            pltpu.VMEM((tokens, 1), F32),
        ],
        4 * tokens * heads * keys * HD + 2 * tokens * lanes * 2 * half,
        12 * MIB,
    )


def pick_kernel(index, keys, values, own):
    own[:, :HD] = keys[0]
    own[:, HD:] = values[0]


def pick(where, key_cache, value_cache, local_heads):
    rows = key_cache.shape[1]
    group = QH // KVH

    def of_head(i, at):
        return lax.div(at[0] * local_heads, jnp.int32(group)), 0, 0

    block = pl.BlockSpec((1, rows, HD), of_head)
    return pl.pallas_call(
        pick_kernel,
        out_shape=jax.ShapeDtypeStruct((rows, 2 * HD), BF16),
        grid_spec=pltpu.PrefetchScalarGridSpec(
            num_scalar_prefetch=1,
            grid=(1,),
            in_specs=[block, block],
            out_specs=pl.BlockSpec((rows, 2 * HD), lambda i, at: (0, 0)),
        ),
        compiler_params=pltpu.CompilerParams(vmem_limit_bytes=54 * MIB),
        cost_estimate=pl.CostEstimate(flops=COVER, bytes_accessed=8 * rows * HD, transcendentals=0),
    )(where, key_cache, value_cache)


def gather_keys(where, key_cache, value_cache, local_heads):
    own = pick(where, key_cache, value_cache, local_heads)
    core, x, _, _, far = links()
    chosen = [link for link in far if link[0] == "qblk"] + [x, core]
    blocks = [own]
    for link in chosen:
        blocks = blocks + [swap(b, link) for b in blocks]
    return blocks, masks_of(chosen)


def reduce_heads(send_a, keep_a, send_b, keep_b):
    _, _, y, z, far = links()
    got_a, got_b = swap(send_a, z), swap(send_b, y)

    def second(keep, got, link):
        sent = swap((keep[1] + got[1].astype(F32)).astype(BF16), link)
        return keep[0] + got[0].astype(F32) + sent.astype(F32)

    total = jnp.concatenate([second(keep_a, got_a, y), second(keep_b, got_b, z)], axis=1)
    return fold_far(total, [link for link in far if link[0] == "head"])


def fold_far(total, far):
    for link in reversed(far):
        half = total.shape[0] // 2
        total = total[:half] + swap(total[half:].astype(BF16), link).astype(F32)
    return total


def row_cuts(rows):
    units = rows // 8
    first = -(-units // 3)
    return (0, first * 8, 2 * first * 8, rows)


def spread(block, dims, far):
    for link in far:
        block = jnp.concatenate([block, swap(block, link)], axis=0)
    cuts = row_cuts(block.shape[0])
    parts = [block[cuts[i] : cuts[i + 1]][None, None, None] for i in range(3)]
    for stage in range(2):
        got = [swap(parts[i], dims[(i + stage) % 3]) for i in range(3)]
        joined = []
        for i in range(3):
            joined.append(jnp.concatenate([parts[i], got[i]], axis=(i + stage) % 3))
        parts = joined
    parts = [p.reshape(-1, p.shape[-1]) for p in parts]
    return parts, [swap(parts[i], dims[(i + 2) % 3]) for i in range(3)]


def expert_kernel(cfg, where, *refs):
    parts, (gate, up, down), refs = refs[:3], refs[3:6], refs[6:]
    out, hidden = refs
    mine = (where[0] * cfg["blocks"] + where[1]).astype(F32)
    top = cfg["top"]
    total = hidden.shape[0]
    width = out.shape[1]
    sizes = [p.shape[0] for p in parts]
    chunk = cfg["chunk"]

    def run(pieces, at):
        lhs = jnp.concatenate([p[:, :width] for p in pieces], axis=0)
        route = jnp.concatenate([p[:, width:] for p in pieces], axis=0).astype(F32)
        lane = lax.broadcasted_iota(jnp.int32, route.shape, 1)
        hit = (route == mine) & (lane < top)
        weight = sum(pltpu.roll(route, LANES - top * k, 1) for k in (1, 2, 3))
        scale = jnp.sum(jnp.where(hit, weight, 0.0), axis=1, keepdims=True)
        rows = pl.ds(at, lhs.shape[0])
        for f in range(0, hidden.shape[1], TILE):
            g = jnp.dot(lhs, gate[0, :, f : f + TILE], preferred_element_type=F32)
            u = jnp.dot(lhs, up[0, :, f : f + TILE], preferred_element_type=F32)
            hidden[rows, f : f + TILE] = (g / (1.0 + jnp.exp(-g)) * u).astype(BF16)
        h = hidden[rows, :]
        for col in range(0, width, TILE):
            y = jnp.dot(h, down[0, :, col : col + TILE], preferred_element_type=F32) * scale
            out[rows, col : col + TILE] = y.astype(out.dtype)

    if total <= chunk:
        run([p[...] for p in parts], 0)
        return
    at = 0
    for p, size in zip(parts, sizes, strict=True):
        run([p[...]], at)
        at += size


def expert(where, parts, matrices, top, kind):
    width = parts[0].shape[1] - LANES
    rows = sum(p.shape[0] for p in parts)
    hidden = matrices[0].shape[2]
    cfg = dict(blocks=lax.axis_size("qblk"), top=top, chunk=2 * TILE)
    args = [where, *parts, *matrices]
    return call(
        functools.partial(expert_kernel, cfg),
        [jax.ShapeDtypeStruct((rows, width), kind)],
        args,
        [IN_SMEM] + [IN_VMEM] * (len(args) - 1),
        [pltpu.VMEM((rows, hidden), BF16)],
        6 * rows * width * hidden,
        12 * MIB,
    )[0]


def fold(sends, keeps, dims, far):
    keeps = [k.reshape(2, 2, -1, k.shape[-1]) for k in keeps]
    sends = [s.reshape(2, 2, -1, s.shape[-1]) for s in sends]
    got = [swap(sends[i], dims[(i + 2) % 3]) for i in range(3)]
    for stage in (1, 0):
        nxt = []
        for i in range(3):
            axis = (i + stage) % 3
            left = sorted((i + s) % 3 for s in range(stage + 1))
            at = left.index(axis)
            keep = [lax.index_in_dim(keeps[i], k, at, False) for k in (0, 1)]
            new = [lax.index_in_dim(got[i], k, at, False).astype(F32) for k in (0, 1)]
            sent = (keep[1] + new[1]).astype(BF16)
            nxt.append((keep[0] + new[0], swap(sent, dims[axis])))
        keeps, got = [n[0] for n in nxt], [n[1] for n in nxt]
    total = jnp.concatenate([keeps[i] + got[i].astype(F32) for i in range(3)], axis=0)
    return fold_far(total, far)


def norm_kernel(residual, projected, gain, ids, weights, hidden, block):
    total = residual[...].astype(F32) + projected[...]
    mean_square = jnp.mean(total * total, axis=1, keepdims=True)
    hidden[...] = total
    rows, width = total.shape
    block[:, :width] = (total * lax.rsqrt(mean_square + 1e-06) * gain[...]).astype(BF16)
    rest, pieces = weights[...], [ids[...].astype(F32)]
    for _ in range(3):
        piece = rest.astype(BF16).astype(F32)
        pieces.append(piece)
        rest = rest - piece
    used = 4 * ids.shape[0]
    pieces.append(jnp.zeros((LANES - used, rows), F32))
    table = jnp.concatenate(pieces, axis=0).astype(BF16)
    square = (rows, rows)
    diagonal = lax.broadcasted_iota(jnp.int32, square, 0) == lax.broadcasted_iota(
        jnp.int32, square, 1
    )
    eye = jnp.where(diagonal, 1.0, 0.0).astype(BF16)
    turned = lax.dot_general(
        eye, table, (((1,), (1,)), ((), ())), preferred_element_type=F32
    )
    block[:, width:] = turned.astype(BF16)


def norm(residual, projected, gain, expert_ids, route_weights):
    rows, width = residual.shape
    return call(
        norm_kernel,
        [
            jax.ShapeDtypeStruct((rows, width), F32),
            jax.ShapeDtypeStruct((rows, width + LANES), BF16),
        ],
        [residual, projected, gain.reshape(1, width), expert_ids.T, route_weights.T],
        [IN_VMEM] * 5,
        [],
        COVER,
        4 * MIB,
    )


def per_device(
    residual,
    queries,
    key_cache,
    value_cache,
    visible_len,
    out_weight,
    norm_gain,
    expert_ids,
    route_weights,
    w_gate,
    w_up,
    w_down,
):
    core, x, y, z, far = links()
    where = jnp.stack([lax.axis_index("head"), lax.axis_index("qblk")])
    kv, offsets = gather_keys(where, key_cache, value_cache, queries.shape[1] // HD)
    projected = reduce_heads(
        *attention(where, queries, visible_len, kv, offsets, out_weight, residual.shape[0])
    )
    hidden_state, block = norm(residual, projected, norm_gain, expert_ids, route_weights)
    dims = (x, y, z)
    matrices = (w_gate, w_up, w_down)
    own, got = spread(block, dims, far)
    own_c = [swap(p, core) for p in own]
    got_c = [swap(p, core) for p in got]
    top = expert_ids.shape[1]
    back = expert(where, own_c, matrices, top, BF16)
    back = swap(back, core)
    kept = expert(where, own, matrices, top, F32)
    kept = kept + back.astype(F32)
    back = expert(where, got_c, matrices, top, BF16)
    back = swap(back, core)
    sent = expert(where, got, matrices, top, F32)
    sent = (sent + back.astype(F32)).astype(BF16)
    cuts = [0]
    for p in own:
        cuts.append(cuts[-1] + p.shape[0])
    split = [[v[cuts[i] : cuts[i + 1]] for i in range(3)] for v in (sent, kept)]
    mix = fold(*split, dims, far)
    return (hidden_state + mix).astype(BF16)


def solution(mesh):
    in_specs = (
        P(("qblk", "head"), None),
        P("qblk", "head"),
        P(None, "qblk", None),
        P(None, "qblk", None),
        P("qblk"),
        P("head", None),
        P(),
        P(("qblk", "head"), None),
        P(("qblk", "head"), None),
        P(("head", "qblk"), None, None),
        P(("head", "qblk"), None, None),
        P(("head", "qblk"), None, None),
    )
    out_specs = P(("qblk", "head"), None)

    return jax.shard_map(
        per_device, mesh=mesh, in_specs=in_specs, out_specs=out_specs, check_vma=False
    )
```

profile of v0, /device:TPU:0, one launch (start us, length us, event | category | flops | bytes accessed | tf_op | source)
XLA Modules:
  0.0 132.7 jit_solution(1235989143799270187)
XLA Ops:
  0.6 2.5 %shard_map.118.refs_0_ = bf16[512,256]{1,0:T(8,128)(2,1)} custom-call(s32[2]{0:T(128)} %pad_add_fusion.index.where, bf16[4,512,128]{2,1,0:T(8,128)(2,1)} %keys.1, bf16[4,512,128]{2,1,0:T(8,128)(2,1)} %values.1), custom_call_target="tpu_custom_call" | custom-call | flops 20000000000 | bytes 524288 | tf_op jit(solution)/shard_map/pallas_call | solution.py:188
  3.1 3.0 %collective-permute-start = (bf16[512,256]{1,0:T(8,128)(2,1)}, bf16[512,256]{1,0:T(8,128)(2,1)S(1)}, u32[]{:S(2)}, u32[]{:S(2)}) collective-permute-start(bf16[512,256]{1,0:T(8,128)(2,1)} %shard_map.118.refs_0_), channel_id=1, source_target_pairs={{0,2},{1,3},{2,0},{3,1},{4,6},{5,7},{6,4},{7,5},{8,10},{9,11},{10,... | collective-permute-start | bytes 786440 | tf_op jit(solution)/shard_map/ppermute | solution.py:25
  6.1 6.5 %collective-permute-done.refs_1_ = bf16[512,256]{1,0:T(8,128)(2,1)S(1)} collective-permute-done((bf16[512,256]{1,0:T(8,128)(2,1)}, bf16[512,256]{1,0:T(8,128)(2,1)S(1)}, u32[]{:S(2)}, u32[]{:S(2)}) %collective-permute-start) | collective-permute-done | bytes 262176 | tf_op jit(solution)/shard_map/ppermute | solution.py:25
  15.1 4.9 %shard_map.119 = (bf16[2,64,1024]{2,1,0:T(8,128)(2,1)S(1)}, f32[2,64,1024]{2,1,0:T(8,128)S(1)}, bf16[2,64,1024]{2,1,0:T(8,128)(2,1)S(1)}, f32[2,64,1024]{2,1,0:T(8,128)S(1)}) custom-call(s32[2]{0:T(128)S(1)} %copy-done.3, bf16[256,512]{1,0:T(8,128)(2,1)S(1)} %copy-done.5, s32[1,256]{1,0:T(1,128)S(1)} %bitcast.110, bf16[512,256]{1,0:T(8,128)(2,1)S(1)} %copy-done.6, ...), custom_call_target="tpu_custom_call" | custom-call | flops 1610612736 | bytes 4981768 | tf_op jit(solution)/shard_map/pallas_call | solution.py:48
  23.5 5.0 %collective-permute-done.5 = bf16[2,64,1024]{2,1,0:T(8,128)(2,1)S(1)} collective-permute-done((bf16[2,64,1024]{2,1,0:T(8,128)(2,1)S(1)}, bf16[2,64,1024]{2,1,0:T(8,128)(2,1)S(1)}, u32[]{:S(2)}, u32[]{:S(2)}) %collective-permute-start.5) | collective-permute-done | bytes 262176 | tf_op jit(solution)/shard_map/ppermute | solution.py:25
  28.5 1.9 %collective-permute-start.6 = (bf16[64,1024]{1,0:T(8,128)(2,1)S(1)}, bf16[64,1024]{1,0:T(8,128)(2,1)S(1)}, u32[]{:S(2)}, u32[]{:S(2)}) collective-permute-start(bf16[64,1024]{1,0:T(8,128)(2,1)S(1)} %fusion.22), channel_id=1, source_target_pairs={{0,8},{4,12},{8,0},{12,4},{16,24},{20,28},{24,16},{28,20},{1,9},{5... | collective-permute-start | bytes 393224 | tf_op jit(solution)/shard_map/ppermute | solution.py:25
  35.5 3.2 %collective-permute-start.7 = (bf16[32,2048]{1,0:T(8,128)(2,1)S(1)}, bf16[32,2048]{1,0:T(8,128)(2,1)S(1)}, u32[]{:S(2)}, u32[]{:S(2)}) collective-permute-start(bf16[32,2048]{1,0:T(8,128)(2,1)S(1)} %fusion.7), channel_id=1, source_target_pairs={{0,24},{4,28},{8,16},{12,20},{16,8},{20,12},{24,0},{28,4},{1,25},{... | collective-permute-start | bytes 393224 | tf_op jit(solution)/shard_map/ppermute | solution.py:25
  38.7 3.7 %collective-permute-done.7 = bf16[32,2048]{1,0:T(8,128)(2,1)S(1)} collective-permute-done((bf16[32,2048]{1,0:T(8,128)(2,1)S(1)}, bf16[32,2048]{1,0:T(8,128)(2,1)S(1)}, u32[]{:S(2)}, u32[]{:S(2)}) %collective-permute-start.7) | collective-permute-done | bytes 131104 | tf_op jit(solution)/shard_map/ppermute | solution.py:25
  42.7 3.2 %collective-permute-start.10 = (bf16[32,2176]{1,0:T(8,128)(2,1)S(1)}, bf16[32,2176]{1,0:T(8,128)(2,1)S(1)}, u32[]{:S(2)}, u32[]{:S(2)}) collective-permute-start(bf16[32,2176]{1,0:T(8,128)(2,1)S(1)} %get-tuple-element.16), channel_id=1, source_target_pairs={{0,24},{4,28},{8,16},{12,20},{16,8},{20,12},{24,0},{28,4},{1,25},{... | collective-permute-start | bytes 417800 | tf_op jit(solution)/shard_map/ppermute | solution.py:25
  45.9 3.9 %collective-permute-done.10 = bf16[32,2176]{1,0:T(8,128)(2,1)S(1)} collective-permute-done((bf16[32,2176]{1,0:T(8,128)(2,1)S(1)}, bf16[32,2176]{1,0:T(8,128)(2,1)S(1)}, u32[]{:S(2)}, u32[]{:S(2)}) %collective-permute-start.10) | collective-permute-done | bytes 139296 | tf_op jit(solution)/shard_map/ppermute | solution.py:25
  54.2 2.3 %collective-permute-start.14 = (bf16[1,1,2,16,2176]{4,3,2,1,0:T(8,128)(2,1)S(1)}, bf16[1,1,2,16,2176]{4,3,2,1,0:T(8,128)(2,1)S(1)}, u32[]{:S(2)}, u32[]{:S(2)}) collective-permute-start(bf16[1,1,2,16,2176]{4,3,2,1,0:T(8,128)(2,1)S(1)} %pad_maximum_fusion.7), channel_id=1, source_target_pairs={{0,2},{1,3},{2,0},{3,1},{4,6},{5,7},{6,4},{7,5},{8,10},{9,11},{10,... | collective-permute-start | bytes 417800 | tf_op jit(solution)/shard_map/ppermute | solution.py:25
  59.0 3.3 %collective-permute-done.12 = bf16[1,2,1,24,2176]{4,3,2,1,0:T(8,128)(2,1)S(1)} collective-permute-done((bf16[1,2,1,24,2176]{4,3,2,1,0:T(8,128)(2,1)S(1)}, bf16[1,2,1,24,2176]{4,3,2,1,0:T(8,128)(2,1)S(1)}, u32[]{:S(2)}, u32[]{:S(2)}) %collective-permute-start.12) | collective-permute-done | bytes 208928 | tf_op jit(solution)/shard_map/ppermute | solution.py:25
  64.0 2.0 %collective-permute-start.20 = (bf16[96,2176]{1,0:T(8,128)(2,1)S(1)}, bf16[96,2176]{1,0:T(8,128)(2,1)S(1)}, u32[]{:S(2)}, u32[]{:S(2)}) collective-permute-start(bf16[96,2176]{1,0:T(8,128)(2,1)S(1)} %bitcast.99), channel_id=1, source_target_pairs={{0,2},{1,3},{2,0},{3,1},{4,6},{5,7},{6,4},{7,5},{8,10},{9,11},{10,... | collective-permute-start | bytes 1253384 | tf_op jit(solution)/shard_map/ppermute | solution.py:25
  66.4 3.2 %shard_map.122 = bf16[256,2048]{1,0:T(8,128)(2,1)S(1)} custom-call(s32[2]{0:T(128)S(1)} %copy-done.3, bf16[96,2176]{1,0:T(8,128)(2,1)S(1)} %collective-permute-done.15.refs_0_, bf16[96,2176]{1,0:T(8,128)(2,1)S(1)} %collective-permute-done.16.refs_1_, bf16[64,2176]{1,0:T(8,128)(2,1)S(1)} %collective-permute-done.17.refs_2_, ...), custom_call_target="tpu_custom_call" | custom-call | flops 2415919104 | bytes 11599880 | tf_op jit(solution)/shard_map/pallas_call | solution.py:48
  71.1 7.7 %collective-permute-done.21.refs_2_ = bf16[64,2176]{1,0:T(8,128)(2,1)S(1)} collective-permute-done((bf16[64,2176]{1,0:T(8,128)(2,1)S(1)}, bf16[64,2176]{1,0:T(8,128)(2,1)S(1)}, u32[]{:S(2)}, u32[]{:S(2)}) %collective-permute-start.21) | collective-permute-done | bytes 278560 | tf_op jit(solution)/shard_map/ppermute | solution.py:25
  79.3 3.2 %shard_map.121 = f32[256,2048]{1,0:T(8,128)S(1)} custom-call(s32[2]{0:T(128)S(1)} %copy-done.3, bf16[96,2176]{1,0:T(8,128)(2,1)S(1)} %bitcast.103, bf16[96,2176]{1,0:T(8,128)(2,1)S(1)} %bitcast.100, bf16[64,2176]{1,0:T(8,128)(2,1)S(1)} %bitcast.106, bf16[1,2048,768]{2,1,0:T(8,128)(2,1)S(1)} %copy-done, bf16[1,2048,768]{2,1,0:T(8,128)(2,1)S(1)} %copy-done.1, ...), custom_call_target="tpu_custom_call" | custom-call | flops 2415919104 | bytes 12648456 | tf_op jit(solution)/shard_map/pallas_call | solution.py:48
  82.5 3.4 %shard_map.123 = f32[256,2048]{1,0:T(8,128)S(1)} custom-call(s32[2]{0:T(128)S(1)} %copy-done.3, bf16[96,2176]{1,0:T(8,128)(2,1)S(1)} %collective-permute-done.19.refs_0_, bf16[96,2176]{1,0:T(8,128)(2,1)S(1)} %collective-permute-done.20.refs_1_, bf16[64,2176]{1,0:T(8,128)(2,1)S(1)} %collective-permute-done.21.refs_2_, bf16[1,2048,768]{2,1,0:T(8,128)(2,1)S(1)} %copy-done, ...), custom_call_target="tpu_custom_call" | custom-call | flops 2415919104 | bytes 12648456 | tf_op jit(solution)/shard_map/pallas_call | solution.py:48
  86.0 3.2 %shard_map.124 = bf16[256,2048]{1,0:T(8,128)(2,1)S(1)} custom-call(s32[2]{0:T(128)S(1)} %copy-done.3, bf16[96,2176]{1,0:T(8,128)(2,1)S(1)} %collective-permute-done.22.refs_0_, bf16[96,2176]{1,0:T(8,128)(2,1)S(1)} %collective-permute-done.23.refs_1_, bf16[64,2176]{1,0:T(8,128)(2,1)S(1)} %collective-permute-done.24.refs_2_, ...), custom_call_target="tpu_custom_call" | custom-call | flops 2415919104 | bytes 11599880 | tf_op jit(solution)/shard_map/pallas_call | solution.py:48
  93.7 7.2 %collective-permute-done.32 = bf16[2,2,16,2048]{3,2,1,0:T(8,128)(2,1)S(1)} collective-permute-done((bf16[2,2,16,2048]{3,2,1,0:T(8,128)(2,1)S(1)}, bf16[2,2,16,2048]{3,2,1,0:T(8,128)(2,1)S(1)}, u32[]{:S(2)}, u32[]{:S(2)}) %collective-permute-start.32) | collective-permute-done | bytes 262176 | tf_op jit(solution)/shard_map/ppermute | solution.py:25
  104.9 2.6 %collective-permute-done.33 = bf16[2,16,2048]{2,1,0:T(8,128)(2,1)S(1)} collective-permute-done((bf16[2,16,2048]{2,1,0:T(8,128)(2,1)S(1)}, bf16[2,16,2048]{2,1,0:T(8,128)(2,1)S(1)}, u32[]{:S(2)}, u32[]{:S(2)}) %collective-permute-start.33) | collective-permute-done | bytes 131104 | tf_op jit(solution)/shard_map/ppermute | solution.py:25
  109.2 5.3 %collective-permute-done.29 = bf16[2,2,24,2048]{3,2,1,0:T(8,128)(2,1)S(1)} collective-permute-done((bf16[2,2,24,2048]{3,2,1,0:T(8,128)(2,1)S(1)}, bf16[2,2,24,2048]{3,2,1,0:T(8,128)(2,1)S(1)}, u32[]{:S(2)}, u32[]{:S(2)}) %collective-permute-start.29) | collective-permute-done | bytes 393248 | tf_op jit(solution)/shard_map/ppermute | solution.py:25
  118.0 2.2 %collective-permute-done.30 = bf16[2,24,2048]{2,1,0:T(8,128)(2,1)S(1)} collective-permute-done((bf16[2,24,2048]{2,1,0:T(8,128)(2,1)S(1)}, bf16[2,24,2048]{2,1,0:T(8,128)(2,1)S(1)}, u32[]{:S(2)}, u32[]{:S(2)}) %collective-permute-start.30) | collective-permute-done | bytes 196640 | tf_op jit(solution)/shard_map/ppermute | solution.py:25
  125.0 3.4 %collective-permute-start.35 = (bf16[32,2048]{1,0:T(8,128)(2,1)S(1)}, bf16[32,2048]{1,0:T(8,128)(2,1)S(1)}, u32[]{:S(2)}, u32[]{:S(2)}) collective-permute-start(bf16[32,2048]{1,0:T(8,128)(2,1)S(1)} %pad_maximum_fusion.8), channel_id=1, source_target_pairs={{0,24},{4,28},{8,16},{12,20},{16,8},{20,12},{24,0},{28,4},{1,25},{... | collective-permute-start | bytes 393224 | tf_op jit(solution)/shard_map/ppermute | solution.py:25
  128.4 3.5 %collective-permute-done.35 = bf16[32,2048]{1,0:T(8,128)(2,1)S(1)} collective-permute-done((bf16[32,2048]{1,0:T(8,128)(2,1)S(1)}, bf16[32,2048]{1,0:T(8,128)(2,1)S(1)}, u32[]{:S(2)}, u32[]{:S(2)}) %collective-permute-start.35) | collective-permute-done | bytes 131104 | tf_op jit(solution)/shard_map/ppermute | solution.py:25
  (111 shorter events, 41.9 us)
Async XLA Ops:
  3.1 9.5 %collective-permute-start = (bf16[512,256]{1,0:T(8,128)(2,1)}, bf16[512,256]{1,0:T(8,128)(2,1)S(1)}, u32[]{:S(2)}, u32[]{:S(2)}) collective-permute-start(bf16[512,256]{1,0:T(8,128)(2,1)} %shard_map.118.refs_0_), channel_id=1, source_target_pairs={{0,2},{1,3},{2,0},{3,1},{4,6},{5,7},{6,4},{7,5},{8,10},{9,11},{10,... | collective-permute-start | bytes 786440 | tf_op jit(solution)/shard_map/ppermute | solution.py:25
  6.1 6.5 %collective-permute-start.1 = (bf16[512,256]{1,0:T(8,128)(2,1)}, bf16[512,256]{1,0:T(8,128)(2,1)S(1)}, u32[]{:S(2)}, u32[]{:S(2)}) collective-permute-start(bf16[512,256]{1,0:T(8,128)(2,1)} %shard_map.118.refs_0_), channel_id=1, source_target_pairs={{0,1},{1,0},{2,3},{3,2},{4,5},{5,4},{6,7},{7,6},{8,9},{9,8},{10,11... | collective-permute-start | bytes 786440 | tf_op jit(solution)/shard_map/ppermute | solution.py:25
  20.0 8.4 %collective-permute-start.5 = (bf16[2,64,1024]{2,1,0:T(8,128)(2,1)S(1)}, bf16[2,64,1024]{2,1,0:T(8,128)(2,1)S(1)}, u32[]{:S(2)}, u32[]{:S(2)}) collective-permute-start(bf16[2,64,1024]{2,1,0:T(8,128)(2,1)S(1)} %get-tuple-element.14), channel_id=1, source_target_pairs={{0,4},{4,0},{8,12},{12,8},{16,20},{20,16},{24,28},{28,24},{1,5},{5... | collective-permute-start | bytes 786440 | tf_op jit(solution)/shard_map/ppermute | solution.py:25
  21.9 8.5 %collective-permute-start.3 = (bf16[2,64,1024]{2,1,0:T(8,128)(2,1)S(1)}, bf16[2,64,1024]{2,1,0:T(8,128)(2,1)S(1)}, u32[]{:S(2)}, u32[]{:S(2)}) collective-permute-start(bf16[2,64,1024]{2,1,0:T(8,128)(2,1)S(1)} %get-tuple-element.12), channel_id=1, source_target_pairs={{0,8},{4,12},{8,0},{12,4},{16,24},{20,28},{24,16},{28,20},{1,9},{5... | collective-permute-start | bytes 786440 | tf_op jit(solution)/shard_map/ppermute | solution.py:25
  35.5 6.9 %collective-permute-start.7 = (bf16[32,2048]{1,0:T(8,128)(2,1)S(1)}, bf16[32,2048]{1,0:T(8,128)(2,1)S(1)}, u32[]{:S(2)}, u32[]{:S(2)}) collective-permute-start(bf16[32,2048]{1,0:T(8,128)(2,1)S(1)} %fusion.7), channel_id=1, source_target_pairs={{0,24},{4,28},{8,16},{12,20},{16,8},{20,12},{24,0},{28,4},{1,25},{... | collective-permute-start | bytes 393224 | tf_op jit(solution)/shard_map/ppermute | solution.py:25
  42.7 7.1 %collective-permute-start.10 = (bf16[32,2176]{1,0:T(8,128)(2,1)S(1)}, bf16[32,2176]{1,0:T(8,128)(2,1)S(1)}, u32[]{:S(2)}, u32[]{:S(2)}) collective-permute-start(bf16[32,2176]{1,0:T(8,128)(2,1)S(1)} %get-tuple-element.16), channel_id=1, source_target_pairs={{0,24},{4,28},{8,16},{12,20},{16,8},{20,12},{24,0},{28,4},{1,25},{... | collective-permute-start | bytes 417800 | tf_op jit(solution)/shard_map/ppermute | solution.py:25
  49.9 6.6 %collective-permute-start.11 = (bf16[1,1,1,24,2176]{4,3,2,1,0:T(8,128)(2,1)S(1)}, bf16[1,1,1,24,2176]{4,3,2,1,0:T(8,128)(2,1)S(1)}, u32[]{:S(2)}, u32[]{:S(2)}) collective-permute-start(bf16[1,1,1,24,2176]{4,3,2,1,0:T(8,128)(2,1)S(1)} %get-tuple-element.31), channel_id=1, source_target_pairs={{0,4},{4,0},{8,12},{12,8},{16,20},{20,16},{24,28},{28,24},{1,5},{5... | collective-permute-start | bytes 313352 | tf_op jit(solution)/shard_map/ppermute | solution.py:25
  54.2 9.2 %collective-permute-start.14 = (bf16[1,1,2,16,2176]{4,3,2,1,0:T(8,128)(2,1)S(1)}, bf16[1,1,2,16,2176]{4,3,2,1,0:T(8,128)(2,1)S(1)}, u32[]{:S(2)}, u32[]{:S(2)}) collective-permute-start(bf16[1,1,2,16,2176]{4,3,2,1,0:T(8,128)(2,1)S(1)} %pad_maximum_fusion.7), channel_id=1, source_target_pairs={{0,2},{1,3},{2,0},{3,1},{4,6},{5,7},{6,4},{7,5},{8,10},{9,11},{10,... | collective-permute-start | bytes 417800 | tf_op jit(solution)/shard_map/ppermute | solution.py:25
  56.5 5.9 %collective-permute-start.12 = (bf16[1,2,1,24,2176]{4,3,2,1,0:T(8,128)(2,1)S(1)}, bf16[1,2,1,24,2176]{4,3,2,1,0:T(8,128)(2,1)S(1)}, u32[]{:S(2)}, u32[]{:S(2)}) collective-permute-start(bf16[1,2,1,24,2176]{4,3,2,1,0:T(8,128)(2,1)S(1)} %pad_maximum_fusion.6), channel_id=1, source_target_pairs={{0,8},{4,12},{8,0},{12,4},{16,24},{20,28},{24,16},{28,20},{1,9},{5... | collective-permute-start | bytes 626696 | tf_op jit(solution)/shard_map/ppermute | solution.py:25
  57.4 5.9 %collective-permute-start.9 = (bf16[2,1,1,24,2176]{4,3,2,1,0:T(8,128)(2,1)S(1)}, bf16[2,1,1,24,2176]{4,3,2,1,0:T(8,128)(2,1)S(1)}, u32[]{:S(2)}, u32[]{:S(2)}) collective-permute-start(bf16[2,1,1,24,2176]{4,3,2,1,0:T(8,128)(2,1)S(1)} %pad_maximum_fusion.5), channel_id=1, source_target_pairs={{0,4},{4,0},{8,12},{12,8},{16,20},{20,16},{24,28},{28,24},{1,5},{5... | collective-permute-start | bytes 626696 | tf_op jit(solution)/shard_map/ppermute | solution.py:25
  64.0 14.8 %collective-permute-start.20 = (bf16[96,2176]{1,0:T(8,128)(2,1)S(1)}, bf16[96,2176]{1,0:T(8,128)(2,1)S(1)}, u32[]{:S(2)}, u32[]{:S(2)}) collective-permute-start(bf16[96,2176]{1,0:T(8,128)(2,1)S(1)} %bitcast.99), channel_id=1, source_target_pairs={{0,2},{1,3},{2,0},{3,1},{4,6},{5,7},{6,4},{7,5},{8,10},{9,11},{10,... | collective-permute-start | bytes 1253384 | tf_op jit(solution)/shard_map/ppermute | solution.py:25
  66.0 13.3 %collective-permute-start.19 = (bf16[96,2176]{1,0:T(8,128)(2,1)S(1)}, bf16[96,2176]{1,0:T(8,128)(2,1)S(1)}, u32[]{:S(2)}, u32[]{:S(2)}) collective-permute-start(bf16[96,2176]{1,0:T(8,128)(2,1)S(1)} %bitcast.102), channel_id=1, source_target_pairs={{0,8},{4,12},{8,0},{12,4},{16,24},{20,28},{24,16},{28,20},{1,9},{5... | collective-permute-start | bytes 1253384 | tf_op jit(solution)/shard_map/ppermute | solution.py:25
  69.6 20.1 %collective-permute-start.18 = (bf16[256,2048]{1,0:T(8,128)(2,1)S(1)}, bf16[256,2048]{1,0:T(8,128)(2,1)S(1)}, u32[]{:S(2)}, u32[]{:S(2)}) collective-permute-start(bf16[256,2048]{1,0:T(8,128)(2,1)S(1)} %shard_map.122), channel_id=1, source_target_pairs={{0,1},{1,0},{2,3},{3,2},{4,5},{5,4},{6,7},{7,6},{8,9},{9,8},{10,11... | collective-permute-start | bytes 3145736 | tf_op jit(solution)/shard_map/ppermute | solution.py:25
  69.7 9.1 %collective-permute-start.21 = (bf16[64,2176]{1,0:T(8,128)(2,1)S(1)}, bf16[64,2176]{1,0:T(8,128)(2,1)S(1)}, u32[]{:S(2)}, u32[]{:S(2)}) collective-permute-start(bf16[64,2176]{1,0:T(8,128)(2,1)S(1)} %bitcast.105), channel_id=1, source_target_pairs={{0,4},{4,0},{8,12},{12,8},{16,20},{20,16},{24,28},{28,24},{1,5},{5... | collective-permute-start | bytes 835592 | tf_op jit(solution)/shard_map/ppermute | solution.py:25
  78.7 7.2 %collective-permute-start.24 = (bf16[64,2176]{1,0:T(8,128)(2,1)S(1)}, bf16[64,2176]{1,0:T(8,128)(2,1)S(1)}, u32[]{:S(2)}, u32[]{:S(2)}) collective-permute-start(bf16[64,2176]{1,0:T(8,128)(2,1)S(1)} %collective-permute-done.21.refs_2_), channel_id=1, source_target_pairs={{0,1},{1,0},{2,3},{3,2},{4,5},{5,4},{6,7},{7,6},{8,9},{9,8},{10,11... | collective-permute-start | bytes 835592 | tf_op jit(solution)/shard_map/ppermute | solution.py:25
  78.8 7.2 %collective-permute-start.23 = (bf16[96,2176]{1,0:T(8,128)(2,1)S(1)}, bf16[96,2176]{1,0:T(8,128)(2,1)S(1)}, u32[]{:S(2)}, u32[]{:S(2)}) collective-permute-start(bf16[96,2176]{1,0:T(8,128)(2,1)S(1)} %collective-permute-done.20.refs_1_), channel_id=1, source_target_pairs={{0,1},{1,0},{2,3},{3,2},{4,5},{5,4},{6,7},{7,6},{8,9},{9,8},{10,11... | collective-permute-start | bytes 1253384 | tf_op jit(solution)/shard_map/ppermute | solution.py:25
  79.3 6.7 %collective-permute-start.22 = (bf16[96,2176]{1,0:T(8,128)(2,1)S(1)}, bf16[96,2176]{1,0:T(8,128)(2,1)S(1)}, u32[]{:S(2)}, u32[]{:S(2)}) collective-permute-start(bf16[96,2176]{1,0:T(8,128)(2,1)S(1)} %collective-permute-done.19.refs_0_), channel_id=1, source_target_pairs={{0,1},{1,0},{2,3},{3,2},{4,5},{5,4},{6,7},{7,6},{8,9},{9,8},{10,11... | collective-permute-start | bytes 1253384 | tf_op jit(solution)/shard_map/ppermute | solution.py:25
  92.3 8.7 %collective-permute-start.32 = (bf16[2,2,16,2048]{3,2,1,0:T(8,128)(2,1)S(1)}, bf16[2,2,16,2048]{3,2,1,0:T(8,128)(2,1)S(1)}, u32[]{:S(2)}, u32[]{:S(2)}) collective-permute-start(bf16[2,2,16,2048]{3,2,1,0:T(8,128)(2,1)S(1)} %bitcast.117), channel_id=1, source_target_pairs={{0,4},{4,0},{8,12},{12,8},{16,20},{20,16},{24,28},{28,24},{1,5},{5... | collective-permute-start | bytes 786440 | tf_op jit(solution)/shard_map/ppermute | solution.py:25
  101.0 6.4 %collective-permute-start.33 = (bf16[2,16,2048]{2,1,0:T(8,128)(2,1)S(1)}, bf16[2,16,2048]{2,1,0:T(8,128)(2,1)S(1)}, u32[]{:S(2)}, u32[]{:S(2)}) collective-permute-start(bf16[2,16,2048]{2,1,0:T(8,128)(2,1)S(1)} %get-tuple-element.29), channel_id=1, source_target_pairs={{0,2},{1,3},{2,0},{3,1},{4,6},{5,7},{6,4},{7,5},{8,10},{9,11},{10,... | collective-permute-start | bytes 393224 | tf_op jit(solution)/shard_map/ppermute | solution.py:25
  102.3 12.1 %collective-permute-start.29 = (bf16[2,2,24,2048]{3,2,1,0:T(8,128)(2,1)S(1)}, bf16[2,2,24,2048]{3,2,1,0:T(8,128)(2,1)S(1)}, u32[]{:S(2)}, u32[]{:S(2)}) collective-permute-start(bf16[2,2,24,2048]{3,2,1,0:T(8,128)(2,1)S(1)} %bitcast.116), channel_id=1, source_target_pairs={{0,2},{1,3},{2,0},{3,1},{4,6},{5,7},{6,4},{7,5},{8,10},{9,11},{10,... | collective-permute-start | bytes 1179656 | tf_op jit(solution)/shard_map/ppermute | solution.py:25
  103.3 13.0 %collective-permute-start.26 = (bf16[2,2,24,2048]{3,2,1,0:T(8,128)(2,1)S(1)}, bf16[2,2,24,2048]{3,2,1,0:T(8,128)(2,1)S(1)}, u32[]{:S(2)}, u32[]{:S(2)}) collective-permute-start(bf16[2,2,24,2048]{3,2,1,0:T(8,128)(2,1)S(1)} %bitcast.115), channel_id=1, source_target_pairs={{0,8},{4,12},{8,0},{12,4},{16,24},{20,28},{24,16},{28,20},{1,9},{5... | collective-permute-start | bytes 1179656 | tf_op jit(solution)/shard_map/ppermute | solution.py:25
  107.5 10.5 %collective-permute-start.34 = (bf16[16,2048]{1,0:T(8,128)(2,1)S(1)}, bf16[16,2048]{1,0:T(8,128)(2,1)S(1)}, u32[]{:S(2)}, u32[]{:S(2)}) collective-permute-start(bf16[16,2048]{1,0:T(8,128)(2,1)S(1)} %fusion.30), channel_id=1, source_target_pairs={{0,8},{4,12},{8,0},{12,4},{16,24},{20,28},{24,16},{28,20},{1,9},{5... | collective-permute-start | bytes 196616 | tf_op jit(solution)/shard_map/ppermute | solution.py:25
  116.3 6.8 %collective-permute-start.27 = (bf16[2,24,2048]{2,1,0:T(8,128)(2,1)S(1)}, bf16[2,24,2048]{2,1,0:T(8,128)(2,1)S(1)}, u32[]{:S(2)}, u32[]{:S(2)}) collective-permute-start(bf16[2,24,2048]{2,1,0:T(8,128)(2,1)S(1)} %get-tuple-element.23), channel_id=1, source_target_pairs={{0,4},{4,0},{8,12},{12,8},{16,20},{20,16},{24,28},{28,24},{1,5},{5... | collective-permute-start | bytes 589832 | tf_op jit(solution)/shard_map/ppermute | solution.py:25
  125.0 6.9 %collective-permute-start.35 = (bf16[32,2048]{1,0:T(8,128)(2,1)S(1)}, bf16[32,2048]{1,0:T(8,128)(2,1)S(1)}, u32[]{:S(2)}, u32[]{:S(2)}) collective-permute-start(bf16[32,2048]{1,0:T(8,128)(2,1)S(1)} %pad_maximum_fusion.8), channel_id=1, source_target_pairs={{0,24},{4,28},{8,16},{12,20},{16,8},{20,12},{24,0},{28,4},{1,25},{... | collective-permute-start | bytes 393224 | tf_op jit(solution)/shard_map/ppermute | solution.py:25
  (24 other events, 232.7 us)
where the time goes:
time: 133 us
  waiting for transfers between devices  62.8 us (47%)
  starting transfers between devices  44.8 us (34%)
  Pallas kernels  20.6 us (15%)
  other arithmetic  2.76 us (2%)
    ppermute x36, waiting for transfers between devices, swap(): lax.ppermute(v, axis, [(i, i ^ mask) for i in range(lax.axis_size(axis))])  62.8 us
    ppermute x36, starting transfers between devices, swap(): lax.ppermute(v, axis, [(i, i ^ mask) for i in range(lax.axis_size(axis))])  44.8 us
    pallas_call x6, Pallas kernels, call(): pl.pallas_call(kernel, out_shape=outs, in_specs=specs, out_specs=[pl.Bloc...  18.1 us
  transfers between devices with their start and end apart: 36, of which 19 were waited for; matrix products, arithmetic and copies ran while one was open for 1% of the time, Pallas kernels for 10%

commit v1 on v0

--- a/solution.py
+++ b/solution.py
@@ -57,83 +57,88 @@
 
 
 IN_VMEM = pl.BlockSpec(memory_space=pltpu.VMEM)
-IN_SMEM = pl.BlockSpec(memory_space=pltpu.SMEM)
-
-
-def attention_kernel(cfg, where, query, lens, *refs):
-    kv, out_weight = refs[: cfg["blocks"]], refs[cfg["blocks"]]
-    send_a, keep_a, send_b, keep_b, stacked, scores, attended, column = refs[cfg["blocks"] + 1 :]
+
+
+def lens_kernel(lens, column):
     count = lens.shape[1]
     square = (count, count)
     diagonal = lax.broadcasted_iota(jnp.int32, square, 0) == lax.broadcasted_iota(
         jnp.int32, square, 1
     )
-    lens_row = jnp.broadcast_to(lens[...].astype(F32), square)
-    column[...] = jnp.sum(jnp.where(diagonal, lens_row, 0.0), axis=1, keepdims=True)
+    row = jnp.broadcast_to(lens[...].astype(F32), square)
+    column[...] = jnp.sum(jnp.where(diagonal, row, 0.0), axis=1, keepdims=True)
+
+
+def attention_kernel(cfg, query, column, *refs):
+    kv, refs = refs[: cfg["blocks"]], refs[cfg["blocks"] :]
+    if cfg["z"]:
+        out_weight, send_a, send_b, keep_b, stacked, scores, attended = refs
+    else:
+        out_weight, early_b, keep_a, send_b, keep_b, stacked, scores, attended = refs
+        send_b[1] = early_b[...]
     token_rows, heads, near = cfg["token_rows"], cfg["heads"], cfg["near"]
-    head_me, qblk_me = where[0], where[1]
+    head_me, qblk_me = lax.axis_index("head"), lax.axis_index("qblk")
     tile = 2 * near
     keys = kv[0].shape[0]
     factor = HD ** (-0.5) * math.log2(math.e)
     group = max(1, TILE // tile)
-    half = out_weight.shape[1] // 2
-    for z in (1, 0):
-        starts = []
-        for o in cfg["order"][z]:
-            starts.append(pl.multiple_of((head_me ^ o) * token_rows, token_rows))
-        span = jnp.concatenate([column[pl.ds(s, token_rows), :] for s in starts], axis=0)
-        span = jnp.concatenate([span] * group, axis=0)
-        for first in range(0, heads, group):
-            for h in range(group):
-                lanes = pl.ds((first + h) * HD, HD)
-                for i, s in enumerate(starts):
-                    rows = pl.ds(h * tile + i * token_rows, token_rows)
-                    stacked[rows, :] = query[pl.ds(s, token_rows), lanes]
-            q = stacked[...]
-            top = None
-            for b in range(cfg["blocks"]):
-                s = lax.dot_general(
-                    q, kv[b][:, :HD], (((1,), (1,)), ((), ())), preferred_element_type=F32
-                )
-                base = (qblk_me ^ cfg["offsets"][b]) * keys
-                pos = base + lax.broadcasted_iota(jnp.int32, s.shape, 1)
-                s = jnp.where(pos.astype(F32) < span, s, -1e30)
-                scores[:, b * keys : (b + 1) * keys] = s
-                here = jnp.max(s, axis=1, keepdims=True)
-                top = here if top is None else jnp.maximum(top, here)
-            denom, mixed = 0.0, 0.0
-            for b in range(cfg["blocks"]):
-                s = scores[:, b * keys : (b + 1) * keys]
-                w = jnp.exp2((s - top) * factor)
-                denom = denom + jnp.sum(w, axis=1, keepdims=True)
-                mixed = mixed + jnp.dot(
-                    w.astype(BF16), kv[b][:, HD:], preferred_element_type=F32
-                )
-            result = (mixed / denom).astype(BF16)
-            for h in range(group):
-                attended[:, (first + h) * HD : (first + h + 1) * HD] = result[
-                    h * tile : (h + 1) * tile
-                ]
-        a = attended[...]
-        for col in range(0, 2 * half, TILE):
-            p = jnp.dot(a, out_weight[:, col : col + TILE], preferred_element_type=F32)
-            for y in (0, 1):
-                rows = p[y * near : (y + 1) * near]
-                if col < half:
-                    at = slice(col, col + TILE)
-                    if z:
-                        send_a[y, :, at] = rows.astype(BF16)
-                    else:
-                        keep_a[y, :, at] = rows
+    starts = []
+    for o in cfg["order"]:
+        starts.append(pl.multiple_of((head_me ^ o) * token_rows, token_rows))
+    span = jnp.concatenate([column[pl.ds(s, token_rows), :] for s in starts], axis=0)
+    span = jnp.concatenate([span] * group, axis=0)
+    for first in range(0, heads, group):
+        for h in range(group):
+            lanes = pl.ds((first + h) * HD, HD)
+            for i, s in enumerate(starts):
+                rows = pl.ds(h * tile + i * token_rows, token_rows)
+                stacked[rows, :] = query[pl.ds(s, token_rows), lanes]
+        q = stacked[...]
+        top = None
+        for b in range(cfg["blocks"]):
+            s = lax.dot_general(
+                q, kv[b][:, :HD], (((1,), (1,)), ((), ())), preferred_element_type=F32
+            )
+            base = (qblk_me ^ cfg["offsets"][b]) * keys
+            pos = base + lax.broadcasted_iota(jnp.int32, s.shape, 1)
+            s = jnp.where(pos.astype(F32) < span, s, -1e30)
+            scores[:, b * keys : (b + 1) * keys] = s
+            here = jnp.max(s, axis=1, keepdims=True)
+            top = here if top is None else jnp.maximum(top, here)
+        denom, mixed = 0.0, 0.0
+        for b in range(cfg["blocks"]):
+            s = scores[:, b * keys : (b + 1) * keys]
+            w = jnp.exp2((s - top) * factor)
+            denom = denom + jnp.sum(w, axis=1, keepdims=True)
+            mixed = mixed + jnp.dot(w.astype(BF16), kv[b][:, HD:], preferred_element_type=F32)
+        result = (mixed / denom).astype(BF16)
+        for h in range(group):
+            attended[:, (first + h) * HD : (first + h + 1) * HD] = result[
+                h * tile : (h + 1) * tile
+            ]
+    a = attended[...]
+    cut = cfg["cut"]
+    for col in range(0, out_weight.shape[1], TILE):
+        p = jnp.dot(a, out_weight[:, col : col + TILE], preferred_element_type=F32)
+        for y in (0, 1):
+            rows = p[y * near : (y + 1) * near]
+            if col < cut:
+                at = slice(col, col + TILE)
+                if cfg["z"]:
+                    send_a[y, :, at] = rows.astype(BF16)
                 else:
-                    at = slice(col - half, col - half + TILE)
-                    if y:
-                        send_b[z, :, at] = rows.astype(BF16)
-                    else:
-                        keep_b[z, :, at] = rows
-
-
-def attention(where, queries, visible_len, kv, offsets, out_weight, token_rows):
+                    keep_a[y, :, at] = rows
+                continue
+            at = slice(col - cut, col - cut + TILE)
+            if not y:
+                keep_b[:, at] = rows
+            elif cfg["z"]:
+                send_b[:, at] = rows.astype(BF16)
+            else:
+                send_b[0, :, at] = rows.astype(BF16)
+
+
+def attention(queries, visible_len, kv, offsets, out_weight, token_rows):
     _, _, y, z, far = links()
     tokens, lanes = queries.shape
     heads = lanes // HD
@@ -141,84 +146,81 @@
     order = masks_of([*far, y, z])
     blocks = len(order) // 2
     near = blocks // 2 * token_rows
-    half = out_weight.shape[1] // 2
-    cfg = dict(
-        blocks=len(kv),
-        token_rows=token_rows,
-        heads=heads,
-        near=near,
-        order=(order[:blocks], order[blocks:]),
-        offsets=offsets,
-    )
+    width = out_weight.shape[1]
+    cut = -(-5 * width // (8 * TILE)) * TILE
     tile = 2 * near
     rows = max(1, TILE // tile) * tile
     keys = kv[0].shape[0] * len(kv)
-    outs = [
-        jax.ShapeDtypeStruct((2, near, half), kind) for kind in (BF16, F32, BF16, F32)
-    ]
-    return call(
-        functools.partial(attention_kernel, cfg),
-        outs,
-        [where, queries, visible_len.reshape(1, tokens), *kv, out_weight],
-        [IN_SMEM] + [IN_VMEM] * (3 + len(kv)),
+    column = call(
+        lens_kernel,
+        [jax.ShapeDtypeStruct((tokens, 1), F32)],
+        [visible_len.reshape(1, tokens)],
+        [IN_VMEM],
+        [],
+        COVER,
+        4 * MIB,
+    )[0]
+
+    def run(side, outs, more):
+        cfg = dict(
+            blocks=len(kv),
+            token_rows=token_rows,
+            heads=heads,
+            near=near,
+            order=order[side * blocks : (side + 1) * blocks],
+            offsets=offsets,
+            cut=cut,
+            z=side,
+        )
+        args = [queries, column, *kv, out_weight, *more]
+        return call(
+            functools.partial(attention_kernel, cfg),
+            [jax.ShapeDtypeStruct(shape, kind) for shape, kind in outs],
+            args,
+            [IN_VMEM] * len(args),
+            [
+                pltpu.VMEM((rows, HD), BF16),
+                pltpu.VMEM((rows, keys), F32),
+                pltpu.VMEM((tile, lanes), BF16),
+            ],
+            2 * tokens * heads * keys * HD + tokens * lanes * width,
+            12 * MIB,
+        )
+
+    part_a, part_b = (2, near, cut), (near, width - cut)
+    send_a, early_b, keep_b1 = run(1, [(part_a, BF16), (part_b, BF16), (part_b, F32)], [])
+    got_a = swap(send_a, z)
+    keep_a, send_b, keep_b0 = run(
+        0, [(part_a, F32), ((2, *part_b), BF16), (part_b, F32)], [early_b]
+    )
+    got_b = swap(send_b, y)
+
+    def second(keep0, keep1, got, link):
+        sent = (keep1 + got[1].astype(F32)).astype(BF16)
+        sent = swap(sent, link)
+        return keep0 + got[0].astype(F32) + sent.astype(F32)
+
+    total = jnp.concatenate(
+        [second(keep_a[0], keep_a[1], got_a, y), second(keep_b0, keep_b1, got_b, z)],
+        axis=1,
+    )
+    return fold_far(total, far)
+
+
+def gather_keys(key_cache, value_cache, kv_index):
+    own = jnp.concatenate(
         [
-            pltpu.VMEM((rows, HD), BF16),
-            pltpu.VMEM((rows, keys), F32),
-            pltpu.VMEM((tile, lanes), BF16),
-            pltpu.VMEM((tokens, 1), F32),
+            lax.dynamic_index_in_dim(key_cache, kv_index, 0, keepdims=False),
+            lax.dynamic_index_in_dim(value_cache, kv_index, 0, keepdims=False),
         ],
-        4 * tokens * heads * keys * HD + 2 * tokens * lanes * 2 * half,
-        12 * MIB,
-    )
-
-
-def pick_kernel(index, keys, values, own):
-    own[:, :HD] = keys[0]
-    own[:, HD:] = values[0]
-
-
-def pick(where, key_cache, value_cache, local_heads):
-    rows = key_cache.shape[1]
-    group = QH // KVH
-
-    def of_head(i, at):
-        return lax.div(at[0] * local_heads, jnp.int32(group)), 0, 0
-
-    block = pl.BlockSpec((1, rows, HD), of_head)
-    return pl.pallas_call(
-        pick_kernel,
-        out_shape=jax.ShapeDtypeStruct((rows, 2 * HD), BF16),
-        grid_spec=pltpu.PrefetchScalarGridSpec(
-            num_scalar_prefetch=1,
-            grid=(1,),
-            in_specs=[block, block],
-            out_specs=pl.BlockSpec((rows, 2 * HD), lambda i, at: (0, 0)),
-        ),
-        compiler_params=pltpu.CompilerParams(vmem_limit_bytes=54 * MIB),
-        cost_estimate=pl.CostEstimate(flops=COVER, bytes_accessed=8 * rows * HD, transcendentals=0),
-    )(where, key_cache, value_cache)
-
-
-def gather_keys(where, key_cache, value_cache, local_heads):
-    own = pick(where, key_cache, value_cache, local_heads)
+        axis=1,
+    )
     core, x, _, _, far = links()
     chosen = [link for link in far if link[0] == "qblk"] + [x, core]
     blocks = [own]
     for link in chosen:
         blocks = blocks + [swap(b, link) for b in blocks]
     return blocks, masks_of(chosen)
-
-
-def reduce_heads(send_a, keep_a, send_b, keep_b):
-    _, _, y, z, far = links()
-    got_a, got_b = swap(send_a, z), swap(send_b, y)
-
-    def second(keep, got, link):
-        sent = swap((keep[1] + got[1].astype(F32)).astype(BF16), link)
-        return keep[0] + got[0].astype(F32) + sent.astype(F32)
-
-    total = jnp.concatenate([second(keep_a, got_a, y), second(keep_b, got_b, z)], axis=1)
-    return fold_far(total, [link for link in far if link[0] == "head"])
 
 
 def fold_far(total, far):
@@ -249,10 +251,10 @@
     return parts, [swap(parts[i], dims[(i + 2) % 3]) for i in range(3)]
 
 
-def expert_kernel(cfg, where, *refs):
+def expert_kernel(cfg, *refs):
     parts, (gate, up, down), refs = refs[:3], refs[3:6], refs[6:]
     out, hidden = refs
-    mine = (where[0] * cfg["blocks"] + where[1]).astype(F32)
+    mine = (lax.axis_index("head") * cfg["blocks"] + lax.axis_index("qblk")).astype(F32)
     top = cfg["top"]
     total = hidden.shape[0]
     width = out.shape[1]
@@ -285,17 +287,17 @@
         at += size
 
 
-def expert(where, parts, matrices, top, kind):
+def expert(parts, matrices, top, kind):
     width = parts[0].shape[1] - LANES
     rows = sum(p.shape[0] for p in parts)
     hidden = matrices[0].shape[2]
     cfg = dict(blocks=lax.axis_size("qblk"), top=top, chunk=2 * TILE)
-    args = [where, *parts, *matrices]
+    args = [*parts, *matrices]
     return call(
         functools.partial(expert_kernel, cfg),
         [jax.ShapeDtypeStruct((rows, width), kind)],
         args,
-        [IN_SMEM] + [IN_VMEM] * (len(args) - 1),
+        [IN_VMEM] * len(args),
         [pltpu.VMEM((rows, hidden), BF16)],
         6 * rows * width * hidden,
         12 * MIB,
@@ -377,11 +379,10 @@
     w_down,
 ):
     core, x, y, z, far = links()
-    where = jnp.stack([lax.axis_index("head"), lax.axis_index("qblk")])
-    kv, offsets = gather_keys(where, key_cache, value_cache, queries.shape[1] // HD)
-    projected = reduce_heads(
-        *attention(where, queries, visible_len, kv, offsets, out_weight, residual.shape[0])
-    )
+    local_heads = queries.shape[1] // HD
+    kv_index = lax.axis_index("head") * local_heads // (QH // KVH)
+    kv, offsets = gather_keys(key_cache, value_cache, kv_index)
+    projected = attention(queries, visible_len, kv, offsets, out_weight, residual.shape[0])
     hidden_state, block = norm(residual, projected, norm_gain, expert_ids, route_weights)
     dims = (x, y, z)
     matrices = (w_gate, w_up, w_down)
@@ -389,13 +390,13 @@
     own_c = [swap(p, core) for p in own]
     got_c = [swap(p, core) for p in got]
     top = expert_ids.shape[1]
-    back = expert(where, own_c, matrices, top, BF16)
+    back = expert(own_c, matrices, top, BF16)
     back = swap(back, core)
-    kept = expert(where, own, matrices, top, F32)
+    kept = expert(own, matrices, top, F32)
     kept = kept + back.astype(F32)
-    back = expert(where, got_c, matrices, top, BF16)
+    back = expert(got_c, matrices, top, BF16)
     back = swap(back, core)
-    sent = expert(where, got, matrices, top, F32)
+    sent = expert(got, matrices, top, F32)
     sent = (sent + back.astype(F32)).astype(BF16)
     cuts = [0]
     for p in own:

time: 133 us -> 131 us (0.985)
  waiting for transfers between devices: 62.8 us -> 71.3 us
  starting transfers between devices: 44.8 us -> 38.3 us
  Pallas kernels: 20.6 us -> 15.6 us
  local copies, waits for them, and re-layouts: 1.24 us -> 2.67 us
    ppermute x36, waiting for transfers between devices: 62.8 us -> 71.3 us  [swap(): lax.ppermute(v, axis, [(i, i ^ mask) for i in range(lax.axis_size(axis))])]
    ppermute x36, starting transfers between devices: 44.8 us -> 38.3 us  [swap(): lax.ppermute(v, axis, [(i, i ^ mask) for i in range(lax.axis_size(axis))])]
    pallas_call x6 -> x8, Pallas kernels: 18.1 us -> 15.6 us  [call(): pl.pallas_call(kernel, out_shape=outs, in_specs=specs, out_specs=[pl.Bloc...]
    pallas_call x1 -> x0, Pallas kernels: 2.51 us -> none  [pick(): pl.pallas_call(pick_kernel, out_shape=jax.ShapeDtypeStruct((rows, 2 * HD)...]
  transfers between devices with their start and end apart: 36 -> 36, of which waited for: 19 -> 20; matrix products, arithmetic and copies ran while one was open for 1% -> 1% of each run, Pallas kernels for 10% -> 8%
where the time goes in v1:
time: 131 us; the launch traced here: 130 us
  waiting for transfers between devices  71.3 us (54%)
  starting transfers between devices  38.3 us (29%)
  Pallas kernels  15.6 us (12%)
  local copies, waits for them, and re-layouts  2.67 us (2%)
  other arithmetic  2.07 us (2%)
    ppermute x36, waiting for transfers between devices, swap(): lax.ppermute(v, axis, [(i, i ^ mask) for i in range(lax.axis_size(axis))])  71.3 us
    ppermute x36, starting transfers between devices, swap(): lax.ppermute(v, axis, [(i, i ^ mask) for i in range(lax.axis_size(axis))])  38.3 us
    pallas_call x8, Pallas kernels, call(): pl.pallas_call(kernel, out_shape=outs, in_specs=specs, out_specs=[pl.Bloc...  15.6 us
  transfers between devices with their start and end apart: 36, of which 20 were waited for; matrix products, arithmetic and copies ran while one was open for 1% of the time, Pallas kernels for 8%

profile of v1, /device:TPU:0, one launch (start us, length us, event | category | flops | bytes accessed | tf_op | source)
XLA Modules:
  0.0 130.4 jit_solution(1696823117820546557)
XLA Ops:
  1.0 3.0 %collective-permute-start = (bf16[512,256]{1,0:T(8,128)(2,1)S(1)}, bf16[512,256]{1,0:T(8,128)(2,1)S(1)}, u32[]{:S(2)}, u32[]{:S(2)}) collective-permute-start(bf16[512,256]{1,0:T(8,128)(2,1)S(1)} %pad_maximum_fusion.5.refs_0_), channel_id=1, source_target_pairs={{0,2},{1,3},{2,0},{3,1},{4,6},{5,7},{6,4},{7,5},{8,10},{9,11},{10,... | collective-permute-start | bytes 786440 | tf_op jit(solution)/shard_map/ppermute | solution.py:25
  4.1 6.3 %collective-permute-done.refs_1_ = bf16[512,256]{1,0:T(8,128)(2,1)S(1)} collective-permute-done((bf16[512,256]{1,0:T(8,128)(2,1)S(1)}, bf16[512,256]{1,0:T(8,128)(2,1)S(1)}, u32[]{:S(2)}, u32[]{:S(2)}) %collective-permute-start) | collective-permute-done | bytes 262176 | tf_op jit(solution)/shard_map/ppermute | solution.py:25
  12.6 2.2 %shard_map.119 = (bf16[2,64,1280]{2,1,0:T(8,128)(2,1)S(1)}, bf16[64,768]{1,0:T(8,128)(2,1)S(1)}, f32[64,768]{1,0:T(8,128)S(1)}) custom-call(bf16[256,512]{1,0:T(8,128)(2,1)S(1)} %copy-done.4, f32[256,1]{1,0:T(8,128)S(1)} %shard_map.118.column, bf16[512,256]{1,0:T(8,128)(2,1)S(1)} %pad_maximum_fusion.5.refs_0_, ...), custom_call_target="tpu_custom_call" | custom-call | flops 805306368 | bytes 4031488 | tf_op jit(solution)/shard_map/pallas_call | solution.py:48
  14.9 2.2 %shard_map.120 = (f32[2,64,1280]{2,1,0:T(8,128)S(1)}, bf16[2,64,768]{2,1,0:T(8,128)(2,1)S(1)}, f32[64,768]{1,0:T(8,128)S(1)}) custom-call(bf16[256,512]{1,0:T(8,128)(2,1)S(1)} %copy-done.4, f32[256,1]{1,0:T(8,128)S(1)} %shard_map.118.column, bf16[512,256]{1,0:T(8,128)(2,1)S(1)} %pad_maximum_fusion.5.refs_0_, ...), custom_call_target="tpu_custom_call" | custom-call | flops 805306368 | bytes 4555776 | tf_op jit(solution)/shard_map/pallas_call | solution.py:48
  20.5 4.0 %collective-permute-done.5 = bf16[2,64,768]{2,1,0:T(8,128)(2,1)S(1)} collective-permute-done((bf16[2,64,768]{2,1,0:T(8,128)(2,1)S(1)}, bf16[2,64,768]{2,1,0:T(8,128)(2,1)S(1)}, u32[]{:S(2)}, u32[]{:S(2)}) %collective-permute-start.5) | collective-permute-done | bytes 196640 | tf_op jit(solution)/shard_map/ppermute | solution.py:25
  26.4 3.1 %collective-permute-done.3 = bf16[2,64,1280]{2,1,0:T(8,128)(2,1)S(1)} collective-permute-done((bf16[2,64,1280]{2,1,0:T(8,128)(2,1)S(1)}, bf16[2,64,1280]{2,1,0:T(8,128)(2,1)S(1)}, u32[]{:S(2)}, u32[]{:S(2)}) %collective-permute-start.3) | collective-permute-done | bytes 327712 | tf_op jit(solution)/shard_map/ppermute | solution.py:25
  31.0 4.0 %collective-permute-done.4 = bf16[64,1280]{1,0:T(8,128)(2,1)S(1)} collective-permute-done((bf16[64,1280]{1,0:T(8,128)(2,1)S(1)}, bf16[64,1280]{1,0:T(8,128)(2,1)S(1)}, u32[]{:S(2)}, u32[]{:S(2)}) %collective-permute-start.4) | collective-permute-done | bytes 163872 | tf_op jit(solution)/shard_map/ppermute | solution.py:25
  35.1 3.7 %collective-permute-start.7 = (bf16[32,2048]{1,0:T(8,128)(2,1)S(1)}, bf16[32,2048]{1,0:T(8,128)(2,1)S(1)}, u32[]{:S(2)}, u32[]{:S(2)}) collective-permute-start(bf16[32,2048]{1,0:T(8,128)(2,1)S(1)} %fusion.7), channel_id=1, source_target_pairs={{0,24},{4,28},{8,16},{12,20},{16,8},{20,12},{24,0},{28,4},{1,25},{... | collective-permute-start | bytes 393224 | tf_op jit(solution)/shard_map/ppermute | solution.py:25
  38.7 3.3 %collective-permute-done.7 = bf16[32,2048]{1,0:T(8,128)(2,1)S(1)} collective-permute-done((bf16[32,2048]{1,0:T(8,128)(2,1)S(1)}, bf16[32,2048]{1,0:T(8,128)(2,1)S(1)}, u32[]{:S(2)}, u32[]{:S(2)}) %collective-permute-start.7) | collective-permute-done | bytes 131104 | tf_op jit(solution)/shard_map/ppermute | solution.py:25
  42.2 3.7 %collective-permute-start.10 = (bf16[32,2176]{1,0:T(8,128)(2,1)S(1)}, bf16[32,2176]{1,0:T(8,128)(2,1)S(1)}, u32[]{:S(2)}, u32[]{:S(2)}) collective-permute-start(bf16[32,2176]{1,0:T(8,128)(2,1)S(1)} %get-tuple-element.20), channel_id=1, source_target_pairs={{0,24},{4,28},{8,16},{12,20},{16,8},{20,12},{24,0},{28,4},{1,25},{... | collective-permute-start | bytes 417800 | tf_op jit(solution)/shard_map/ppermute | solution.py:25
  45.9 3.8 %collective-permute-done.10 = bf16[32,2176]{1,0:T(8,128)(2,1)S(1)} collective-permute-done((bf16[32,2176]{1,0:T(8,128)(2,1)S(1)}, bf16[32,2176]{1,0:T(8,128)(2,1)S(1)}, u32[]{:S(2)}, u32[]{:S(2)}) %collective-permute-start.10) | collective-permute-done | bytes 139296 | tf_op jit(solution)/shard_map/ppermute | solution.py:25
  52.4 2.4 %collective-permute-done.13 = bf16[1,1,1,16,2176]{4,3,2,1,0:T(8,128)(2,1)S(1)} collective-permute-done((bf16[1,1,1,16,2176]{4,3,2,1,0:T(8,128)(2,1)S(1)}, bf16[1,1,1,16,2176]{4,3,2,1,0:T(8,128)(2,1)S(1)}, u32[]{:S(2)}, u32[]{:S(2)}) %collective-permute-start.13) | collective-permute-done | bytes 69664 | tf_op jit(solution)/shard_map/ppermute | solution.py:25
  57.9 4.4 %collective-permute-done.12 = bf16[1,2,1,24,2176]{4,3,2,1,0:T(8,128)(2,1)S(1)} collective-permute-done((bf16[1,2,1,24,2176]{4,3,2,1,0:T(8,128)(2,1)S(1)}, bf16[1,2,1,24,2176]{4,3,2,1,0:T(8,128)(2,1)S(1)}, u32[]{:S(2)}, u32[]{:S(2)}) %collective-permute-start.12) | collective-permute-done | bytes 208928 | tf_op jit(solution)/shard_map/ppermute | solution.py:25
  66.3 2.7 %shard_map.123 = bf16[256,2048]{1,0:T(8,128)(2,1)S(1)} custom-call(bf16[96,2176]{1,0:T(8,128)(2,1)S(1)} %collective-permute-done.15.refs_0_, bf16[96,2176]{1,0:T(8,128)(2,1)S(1)} %collective-permute-done.16.refs_1_, bf16[64,2176]{1,0:T(8,128)(2,1)S(1)} %collective-permute-done.17.refs_2_, bf16[1,2048,768]{2,1,0:T(8,128)(2,1)S(1)} %copy-done, ...), custom_call_target="tpu_custom_call" | custom-call | flops 2415919104 | bytes 11599872 | tf_op jit(solution)/shard_map/pallas_call | solution.py:48
  69.9 8.3 %collective-permute-done.21.refs_2_ = bf16[64,2176]{1,0:T(8,128)(2,1)S(1)} collective-permute-done((bf16[64,2176]{1,0:T(8,128)(2,1)S(1)}, bf16[64,2176]{1,0:T(8,128)(2,1)S(1)}, u32[]{:S(2)}, u32[]{:S(2)}) %collective-permute-start.21) | collective-permute-done | bytes 278560 | tf_op jit(solution)/shard_map/ppermute | solution.py:25
  78.7 2.7 %shard_map.122 = f32[256,2048]{1,0:T(8,128)S(1)} custom-call(bf16[96,2176]{1,0:T(8,128)(2,1)S(1)} %bitcast.111, bf16[96,2176]{1,0:T(8,128)(2,1)S(1)} %bitcast.108, bf16[64,2176]{1,0:T(8,128)(2,1)S(1)} %bitcast.114, bf16[1,2048,768]{2,1,0:T(8,128)(2,1)S(1)} %copy-done, bf16[1,2048,768]{2,1,0:T(8,128)(2,1)S(1)} %copy-done.1, bf16[1,768,2048]{2,1,0:T(8,128)(2,1)S(1)} %copy-done.2), custom_call_target="tpu_custom_call" | custom-call | flops 2415919104 | bytes 12648448 | tf_op jit(solution)/shard_map/pallas_call | solution.py:48
  81.4 2.8 %shard_map.124 = f32[256,2048]{1,0:T(8,128)S(1)} custom-call(bf16[96,2176]{1,0:T(8,128)(2,1)S(1)} %collective-permute-done.19.refs_0_, bf16[96,2176]{1,0:T(8,128)(2,1)S(1)} %collective-permute-done.20.refs_1_, bf16[64,2176]{1,0:T(8,128)(2,1)S(1)} %collective-permute-done.21.refs_2_, bf16[1,2048,768]{2,1,0:T(8,128)(2,1)S(1)} %copy-done, ...), custom_call_target="tpu_custom_call" | custom-call | flops 2415919104 | bytes 12648448 | tf_op jit(solution)/shard_map/pallas_call | solution.py:48
  84.3 2.7 %shard_map.125 = bf16[256,2048]{1,0:T(8,128)(2,1)S(1)} custom-call(bf16[96,2176]{1,0:T(8,128)(2,1)S(1)} %collective-permute-done.22.refs_0_, bf16[96,2176]{1,0:T(8,128)(2,1)S(1)} %collective-permute-done.23.refs_1_, bf16[64,2176]{1,0:T(8,128)(2,1)S(1)} %collective-permute-done.24.refs_2_, bf16[1,2048,768]{2,1,0:T(8,128)(2,1)S(1)} %copy-done, ...), custom_call_target="tpu_custom_call" | custom-call | flops 2415919104 | bytes 11599872 | tf_op jit(solution)/shard_map/pallas_call | solution.py:48
  90.9 7.8 %collective-permute-done.32 = bf16[2,2,16,2048]{3,2,1,0:T(8,128)(2,1)S(1)} collective-permute-done((bf16[2,2,16,2048]{3,2,1,0:T(8,128)(2,1)S(1)}, bf16[2,2,16,2048]{3,2,1,0:T(8,128)(2,1)S(1)}, u32[]{:S(2)}, u32[]{:S(2)}) %collective-permute-start.32) | collective-permute-done | bytes 262176 | tf_op jit(solution)/shard_map/ppermute | solution.py:25
  102.3 2.8 %collective-permute-done.33 = bf16[2,16,2048]{2,1,0:T(8,128)(2,1)S(1)} collective-permute-done((bf16[2,16,2048]{2,1,0:T(8,128)(2,1)S(1)}, bf16[2,16,2048]{2,1,0:T(8,128)(2,1)S(1)}, u32[]{:S(2)}, u32[]{:S(2)}) %collective-permute-start.33) | collective-permute-done | bytes 131104 | tf_op jit(solution)/shard_map/ppermute | solution.py:25
  106.7 5.5 %collective-permute-done.29 = bf16[2,2,24,2048]{3,2,1,0:T(8,128)(2,1)S(1)} collective-permute-done((bf16[2,2,24,2048]{3,2,1,0:T(8,128)(2,1)S(1)}, bf16[2,2,24,2048]{3,2,1,0:T(8,128)(2,1)S(1)}, u32[]{:S(2)}, u32[]{:S(2)}) %collective-permute-start.29) | collective-permute-done | bytes 393248 | tf_op jit(solution)/shard_map/ppermute | solution.py:25
  114.5 3.4 %collective-permute-done.30 = bf16[2,24,2048]{2,1,0:T(8,128)(2,1)S(1)} collective-permute-done((bf16[2,24,2048]{2,1,0:T(8,128)(2,1)S(1)}, bf16[2,24,2048]{2,1,0:T(8,128)(2,1)S(1)}, u32[]{:S(2)}, u32[]{:S(2)}) %collective-permute-start.30) | collective-permute-done | bytes 196640 | tf_op jit(solution)/shard_map/ppermute | solution.py:25
  122.7 2.7 %collective-permute-start.35 = (bf16[32,2048]{1,0:T(8,128)(2,1)S(1)}, bf16[32,2048]{1,0:T(8,128)(2,1)S(1)}, u32[]{:S(2)}, u32[]{:S(2)}) collective-permute-start(bf16[32,2048]{1,0:T(8,128)(2,1)S(1)} %pad_maximum_fusion.9), channel_id=1, source_target_pairs={{0,24},{4,28},{8,16},{12,20},{16,8},{20,12},{24,0},{28,4},{1,25},{... | collective-permute-start | bytes 393224 | tf_op jit(solution)/shard_map/ppermute | solution.py:25
  125.5 4.2 %collective-permute-done.35 = bf16[32,2048]{1,0:T(8,128)(2,1)S(1)} collective-permute-done((bf16[32,2048]{1,0:T(8,128)(2,1)S(1)}, bf16[32,2048]{1,0:T(8,128)(2,1)S(1)}, u32[]{:S(2)}, u32[]{:S(2)}) %collective-permute-start.35) | collective-permute-done | bytes 131104 | tf_op jit(solution)/shard_map/ppermute | solution.py:25
  (109 shorter events, 38.2 us)
Async XLA Ops:
  1.0 9.3 %collective-permute-start = (bf16[512,256]{1,0:T(8,128)(2,1)S(1)}, bf16[512,256]{1,0:T(8,128)(2,1)S(1)}, u32[]{:S(2)}, u32[]{:S(2)}) collective-permute-start(bf16[512,256]{1,0:T(8,128)(2,1)S(1)} %pad_maximum_fusion.5.refs_0_), channel_id=1, source_target_pairs={{0,2},{1,3},{2,0},{3,1},{4,6},{5,7},{6,4},{7,5},{8,10},{9,11},{10,... | collective-permute-start | bytes 786440 | tf_op jit(solution)/shard_map/ppermute | solution.py:25
  4.1 7.1 %collective-permute-start.1 = (bf16[512,256]{1,0:T(8,128)(2,1)S(1)}, bf16[512,256]{1,0:T(8,128)(2,1)S(1)}, u32[]{:S(2)}, u32[]{:S(2)}) collective-permute-start(bf16[512,256]{1,0:T(8,128)(2,1)S(1)} %pad_maximum_fusion.5.refs_0_), channel_id=1, source_target_pairs={{0,1},{1,0},{2,3},{3,2},{4,5},{5,4},{6,7},{7,6},{8,9},{9,8},{10,11... | collective-permute-start | bytes 786440 | tf_op jit(solution)/shard_map/ppermute | solution.py:25
  17.1 7.4 %collective-permute-start.5 = (bf16[2,64,768]{2,1,0:T(8,128)(2,1)S(1)}, bf16[2,64,768]{2,1,0:T(8,128)(2,1)S(1)}, u32[]{:S(2)}, u32[]{:S(2)}) collective-permute-start(bf16[2,64,768]{2,1,0:T(8,128)(2,1)S(1)} %get-tuple-element.17), channel_id=1, source_target_pairs={{0,4},{4,0},{8,12},{12,8},{16,20},{20,16},{24,28},{28,24},{1,5},{5... | collective-permute-start | bytes 589832 | tf_op jit(solution)/shard_map/ppermute | solution.py:25
  19.0 10.6 %collective-permute-start.3 = (bf16[2,64,1280]{2,1,0:T(8,128)(2,1)S(1)}, bf16[2,64,1280]{2,1,0:T(8,128)(2,1)S(1)}, u32[]{:S(2)}, u32[]{:S(2)}) collective-permute-start(bf16[2,64,1280]{2,1,0:T(8,128)(2,1)S(1)} %get-tuple-element.15), channel_id=1, source_target_pairs={{0,8},{4,12},{8,0},{12,4},{16,24},{20,28},{24,16},{28,20},{1,9},{5... | collective-permute-start | bytes 983048 | tf_op jit(solution)/shard_map/ppermute | solution.py:25
  24.6 6.3 %collective-permute-start.6 = (bf16[64,768]{1,0:T(8,128)(2,1)S(1)}, bf16[64,768]{1,0:T(8,128)(2,1)S(1)}, u32[]{:S(2)}, u32[]{:S(2)}) collective-permute-start(bf16[64,768]{1,0:T(8,128)(2,1)S(1)} %fusion.21), channel_id=1, source_target_pairs={{0,8},{4,12},{8,0},{12,4},{16,24},{20,28},{24,16},{28,20},{1,9},{5... | collective-permute-start | bytes 294920 | tf_op jit(solution)/shard_map/ppermute | solution.py:25
  35.1 6.9 %collective-permute-start.7 = (bf16[32,2048]{1,0:T(8,128)(2,1)S(1)}, bf16[32,2048]{1,0:T(8,128)(2,1)S(1)}, u32[]{:S(2)}, u32[]{:S(2)}) collective-permute-start(bf16[32,2048]{1,0:T(8,128)(2,1)S(1)} %fusion.7), channel_id=1, source_target_pairs={{0,24},{4,28},{8,16},{12,20},{16,8},{20,12},{24,0},{28,4},{1,25},{... | collective-permute-start | bytes 393224 | tf_op jit(solution)/shard_map/ppermute | solution.py:25
  42.2 7.5 %collective-permute-start.10 = (bf16[32,2176]{1,0:T(8,128)(2,1)S(1)}, bf16[32,2176]{1,0:T(8,128)(2,1)S(1)}, u32[]{:S(2)}, u32[]{:S(2)}) collective-permute-start(bf16[32,2176]{1,0:T(8,128)(2,1)S(1)} %get-tuple-element.20), channel_id=1, source_target_pairs={{0,24},{4,28},{8,16},{12,20},{16,8},{20,12},{24,0},{28,4},{1,25},{... | collective-permute-start | bytes 417800 | tf_op jit(solution)/shard_map/ppermute | solution.py:25
  50.5 5.9 %collective-permute-start.11 = (bf16[1,1,1,24,2176]{4,3,2,1,0:T(8,128)(2,1)S(1)}, bf16[1,1,1,24,2176]{4,3,2,1,0:T(8,128)(2,1)S(1)}, u32[]{:S(2)}, u32[]{:S(2)}) collective-permute-start(bf16[1,1,1,24,2176]{4,3,2,1,0:T(8,128)(2,1)S(1)} %get-tuple-element.35), channel_id=1, source_target_pairs={{0,4},{4,0},{8,12},{12,8},{16,20},{20,16},{24,28},{28,24},{1,5},{5... | collective-permute-start | bytes 313352 | tf_op jit(solution)/shard_map/ppermute | solution.py:25
  51.2 6.5 %collective-permute-start.8 = (bf16[1,1,1,24,2176]{4,3,2,1,0:T(8,128)(2,1)S(1)}, bf16[1,1,1,24,2176]{4,3,2,1,0:T(8,128)(2,1)S(1)}, u32[]{:S(2)}, u32[]{:S(2)}) collective-permute-start(bf16[1,1,1,24,2176]{4,3,2,1,0:T(8,128)(2,1)S(1)} %get-tuple-element.36), channel_id=1, source_target_pairs={{0,2},{1,3},{2,0},{3,1},{4,6},{5,7},{6,4},{7,5},{8,10},{9,11},{10,... | collective-permute-start | bytes 313352 | tf_op jit(solution)/shard_map/ppermute | solution.py:25
  54.8 9.0 %collective-permute-start.14 = (bf16[1,1,2,16,2176]{4,3,2,1,0:T(8,128)(2,1)S(1)}, bf16[1,1,2,16,2176]{4,3,2,1,0:T(8,128)(2,1)S(1)}, u32[]{:S(2)}, u32[]{:S(2)}) collective-permute-start(bf16[1,1,2,16,2176]{4,3,2,1,0:T(8,128)(2,1)S(1)} %pad_maximum_fusion.8), channel_id=1, source_target_pairs={{0,2},{1,3},{2,0},{3,1},{4,6},{5,7},{6,4},{7,5},{8,10},{9,11},{10,... | collective-permute-start | bytes 417800 | tf_op jit(solution)/shard_map/ppermute | solution.py:25
  56.4 5.9 %collective-permute-start.12 = (bf16[1,2,1,24,2176]{4,3,2,1,0:T(8,128)(2,1)S(1)}, bf16[1,2,1,24,2176]{4,3,2,1,0:T(8,128)(2,1)S(1)}, u32[]{:S(2)}, u32[]{:S(2)}) collective-permute-start(bf16[1,2,1,24,2176]{4,3,2,1,0:T(8,128)(2,1)S(1)} %pad_maximum_fusion.7), channel_id=1, source_target_pairs={{0,8},{4,12},{8,0},{12,4},{16,24},{20,28},{24,16},{28,20},{1,9},{5... | collective-permute-start | bytes 626696 | tf_op jit(solution)/shard_map/ppermute | solution.py:25
  64.4 13.7 %collective-permute-start.20 = (bf16[96,2176]{1,0:T(8,128)(2,1)S(1)}, bf16[96,2176]{1,0:T(8,128)(2,1)S(1)}, u32[]{:S(2)}, u32[]{:S(2)}) collective-permute-start(bf16[96,2176]{1,0:T(8,128)(2,1)S(1)} %bitcast.107), channel_id=1, source_target_pairs={{0,2},{1,3},{2,0},{3,1},{4,6},{5,7},{6,4},{7,5},{8,10},{9,11},{10,... | collective-permute-start | bytes 1253384 | tf_op jit(solution)/shard_map/ppermute | solution.py:25
  65.6 13.0 %collective-permute-start.19 = (bf16[96,2176]{1,0:T(8,128)(2,1)S(1)}, bf16[96,2176]{1,0:T(8,128)(2,1)S(1)}, u32[]{:S(2)}, u32[]{:S(2)}) collective-permute-start(bf16[96,2176]{1,0:T(8,128)(2,1)S(1)} %bitcast.110), channel_id=1, source_target_pairs={{0,8},{4,12},{8,0},{12,4},{16,24},{20,28},{24,16},{28,20},{1,9},{5... | collective-permute-start | bytes 1253384 | tf_op jit(solution)/shard_map/ppermute | solution.py:25
  69.0 18.5 %collective-permute-start.18 = (bf16[256,2048]{1,0:T(8,128)(2,1)S(1)}, bf16[256,2048]{1,0:T(8,128)(2,1)S(1)}, u32[]{:S(2)}, u32[]{:S(2)}) collective-permute-start(bf16[256,2048]{1,0:T(8,128)(2,1)S(1)} %shard_map.123), channel_id=1, source_target_pairs={{0,1},{1,0},{2,3},{3,2},{4,5},{5,4},{6,7},{7,6},{8,9},{9,8},{10,11... | collective-permute-start | bytes 3145736 | tf_op jit(solution)/shard_map/ppermute | solution.py:25
  69.1 9.1 %collective-permute-start.21 = (bf16[64,2176]{1,0:T(8,128)(2,1)S(1)}, bf16[64,2176]{1,0:T(8,128)(2,1)S(1)}, u32[]{:S(2)}, u32[]{:S(2)}) collective-permute-start(bf16[64,2176]{1,0:T(8,128)(2,1)S(1)} %bitcast.113), channel_id=1, source_target_pairs={{0,4},{4,0},{8,12},{12,8},{16,20},{20,16},{24,28},{28,24},{1,5},{5... | collective-permute-start | bytes 835592 | tf_op jit(solution)/shard_map/ppermute | solution.py:25
  78.1 6.1 %collective-permute-start.24 = (bf16[64,2176]{1,0:T(8,128)(2,1)S(1)}, bf16[64,2176]{1,0:T(8,128)(2,1)S(1)}, u32[]{:S(2)}, u32[]{:S(2)}) collective-permute-start(bf16[64,2176]{1,0:T(8,128)(2,1)S(1)} %collective-permute-done.21.refs_2_), channel_id=1, source_target_pairs={{0,1},{1,0},{2,3},{3,2},{4,5},{5,4},{6,7},{7,6},{8,9},{9,8},{10,11... | collective-permute-start | bytes 835592 | tf_op jit(solution)/shard_map/ppermute | solution.py:25
  78.1 6.1 %collective-permute-start.23 = (bf16[96,2176]{1,0:T(8,128)(2,1)S(1)}, bf16[96,2176]{1,0:T(8,128)(2,1)S(1)}, u32[]{:S(2)}, u32[]{:S(2)}) collective-permute-start(bf16[96,2176]{1,0:T(8,128)(2,1)S(1)} %collective-permute-done.20.refs_1_), channel_id=1, source_target_pairs={{0,1},{1,0},{2,3},{3,2},{4,5},{5,4},{6,7},{7,6},{8,9},{9,8},{10,11... | collective-permute-start | bytes 1253384 | tf_op jit(solution)/shard_map/ppermute | solution.py:25
  90.1 8.7 %collective-permute-start.32 = (bf16[2,2,16,2048]{3,2,1,0:T(8,128)(2,1)S(1)}, bf16[2,2,16,2048]{3,2,1,0:T(8,128)(2,1)S(1)}, u32[]{:S(2)}, u32[]{:S(2)}) collective-permute-start(bf16[2,2,16,2048]{3,2,1,0:T(8,128)(2,1)S(1)} %bitcast.125), channel_id=1, source_target_pairs={{0,4},{4,0},{8,12},{12,8},{16,20},{20,16},{24,28},{28,24},{1,5},{5... | collective-permute-start | bytes 786440 | tf_op jit(solution)/shard_map/ppermute | solution.py:25
  98.8 6.4 %collective-permute-start.33 = (bf16[2,16,2048]{2,1,0:T(8,128)(2,1)S(1)}, bf16[2,16,2048]{2,1,0:T(8,128)(2,1)S(1)}, u32[]{:S(2)}, u32[]{:S(2)}) collective-permute-start(bf16[2,16,2048]{2,1,0:T(8,128)(2,1)S(1)} %get-tuple-element.33), channel_id=1, source_target_pairs={{0,2},{1,3},{2,0},{3,1},{4,6},{5,7},{6,4},{7,5},{8,10},{9,11},{10,... | collective-permute-start | bytes 393224 | tf_op jit(solution)/shard_map/ppermute | solution.py:25
  99.8 12.4 %collective-permute-start.29 = (bf16[2,2,24,2048]{3,2,1,0:T(8,128)(2,1)S(1)}, bf16[2,2,24,2048]{3,2,1,0:T(8,128)(2,1)S(1)}, u32[]{:S(2)}, u32[]{:S(2)}) collective-permute-start(bf16[2,2,24,2048]{3,2,1,0:T(8,128)(2,1)S(1)} %bitcast.124), channel_id=1, source_target_pairs={{0,2},{1,3},{2,0},{3,1},{4,6},{5,7},{6,4},{7,5},{8,10},{9,11},{10,... | collective-permute-start | bytes 1179656 | tf_op jit(solution)/shard_map/ppermute | solution.py:25
  101.0 12.7 %collective-permute-start.26 = (bf16[2,2,24,2048]{3,2,1,0:T(8,128)(2,1)S(1)}, bf16[2,2,24,2048]{3,2,1,0:T(8,128)(2,1)S(1)}, u32[]{:S(2)}, u32[]{:S(2)}) collective-permute-start(bf16[2,2,24,2048]{3,2,1,0:T(8,128)(2,1)S(1)} %bitcast.123), channel_id=1, source_target_pairs={{0,8},{4,12},{8,0},{12,4},{16,24},{20,28},{24,16},{28,20},{1,9},{5... | collective-permute-start | bytes 1179656 | tf_op jit(solution)/shard_map/ppermute | solution.py:25
  105.2 9.3 %collective-permute-start.34 = (bf16[16,2048]{1,0:T(8,128)(2,1)S(1)}, bf16[16,2048]{1,0:T(8,128)(2,1)S(1)}, u32[]{:S(2)}, u32[]{:S(2)}) collective-permute-start(bf16[16,2048]{1,0:T(8,128)(2,1)S(1)} %fusion.31), channel_id=1, source_target_pairs={{0,8},{4,12},{8,0},{12,4},{16,24},{20,28},{24,16},{28,20},{1,9},{5... | collective-permute-start | bytes 196616 | tf_op jit(solution)/shard_map/ppermute | solution.py:25
  113.8 6.8 %collective-permute-start.27 = (bf16[2,24,2048]{2,1,0:T(8,128)(2,1)S(1)}, bf16[2,24,2048]{2,1,0:T(8,128)(2,1)S(1)}, u32[]{:S(2)}, u32[]{:S(2)}) collective-permute-start(bf16[2,24,2048]{2,1,0:T(8,128)(2,1)S(1)} %get-tuple-element.27), channel_id=1, source_target_pairs={{0,4},{4,0},{8,12},{12,8},{16,20},{20,16},{24,28},{28,24},{1,5},{5... | collective-permute-start | bytes 589832 | tf_op jit(solution)/shard_map/ppermute | solution.py:25
  122.7 6.9 %collective-permute-start.35 = (bf16[32,2048]{1,0:T(8,128)(2,1)S(1)}, bf16[32,2048]{1,0:T(8,128)(2,1)S(1)}, u32[]{:S(2)}, u32[]{:S(2)}) collective-permute-start(bf16[32,2048]{1,0:T(8,128)(2,1)S(1)} %pad_maximum_fusion.9), channel_id=1, source_target_pairs={{0,24},{4,28},{8,16},{12,20},{16,8},{20,12},{24,0},{28,4},{1,25},{... | collective-permute-start | bytes 393224 | tf_op jit(solution)/shard_map/ppermute | solution.py:25
  (22 other events, 196.8 us)

commit v2 on v1

--- a/solution.py
+++ b/solution.py
@@ -57,6 +57,10 @@
 
 
 IN_VMEM = pl.BlockSpec(memory_space=pltpu.VMEM)
+
+
+def spans(first, last):
+    return [(at, min(at + TILE, last)) for at in range(first, last, TILE)]
 
 
 def lens_kernel(lens, column):
@@ -118,18 +122,18 @@
             ]
     a = attended[...]
     cut = cfg["cut"]
-    for col in range(0, out_weight.shape[1], TILE):
-        p = jnp.dot(a, out_weight[:, col : col + TILE], preferred_element_type=F32)
+    for col, end in spans(0, cut) + spans(cut, out_weight.shape[1]):
+        p = jnp.dot(a, out_weight[:, col:end], preferred_element_type=F32)
         for y in (0, 1):
             rows = p[y * near : (y + 1) * near]
             if col < cut:
-                at = slice(col, col + TILE)
+                at = slice(col, end)
                 if cfg["z"]:
                     send_a[y, :, at] = rows.astype(BF16)
                 else:
                     keep_a[y, :, at] = rows
                 continue
-            at = slice(col - cut, col - cut + TILE)
+            at = slice(col - cut, end - cut)
             if not y:
                 keep_b[:, at] = rows
             elif cfg["z"]:
@@ -147,7 +151,7 @@
     blocks = len(order) // 2
     near = blocks // 2 * token_rows
     width = out_weight.shape[1]
-    cut = -(-5 * width // (8 * TILE)) * TILE
+    cut = -(-9 * width // (16 * LANES)) * LANES
     tile = 2 * near
     rows = max(1, TILE // tile) * tile
     keys = kv[0].shape[0] * len(kv)
@@ -236,11 +240,16 @@
     return (0, first * 8, 2 * first * 8, rows)
 
 
-def spread(block, dims, far):
+def spread(block, first, dims, far):
     for link in far:
         block = jnp.concatenate([block, swap(block, link)], axis=0)
     cuts = row_cuts(block.shape[0])
-    parts = [block[cuts[i] : cuts[i + 1]][None, None, None] for i in range(3)]
+    parts = []
+    for i in range(3):
+        part = block[cuts[i] : cuts[i + 1]]
+        if i == 0 and first.shape[0] == cuts[1]:
+            part = first
+        parts.append(part[None, None, None])
     for stage in range(2):
         got = [swap(parts[i], dims[(i + stage) % 3]) for i in range(3)]
         joined = []
@@ -323,7 +332,7 @@
     return fold_far(total, far)
 
 
-def norm_kernel(residual, projected, gain, ids, weights, hidden, block):
+def norm_kernel(residual, projected, gain, ids, weights, hidden, block, first):
     total = residual[...].astype(F32) + projected[...]
     mean_square = jnp.mean(total * total, axis=1, keepdims=True)
     hidden[...] = total
@@ -346,15 +355,17 @@
         eye, table, (((1,), (1,)), ((), ())), preferred_element_type=F32
     )
     block[:, width:] = turned.astype(BF16)
-
-
-def norm(residual, projected, gain, expert_ids, route_weights):
+    first[...] = block[: first.shape[0], :]
+
+
+def norm(residual, projected, gain, expert_ids, route_weights, gathered):
     rows, width = residual.shape
     return call(
         norm_kernel,
         [
             jax.ShapeDtypeStruct((rows, width), F32),
             jax.ShapeDtypeStruct((rows, width + LANES), BF16),
+            jax.ShapeDtypeStruct((min(rows, row_cuts(gathered)[1]), width + LANES), BF16),
         ],
         [residual, projected, gain.reshape(1, width), expert_ids.T, route_weights.T],
         [IN_VMEM] * 5,
@@ -383,10 +394,12 @@
     kv_index = lax.axis_index("head") * local_heads // (QH // KVH)
     kv, offsets = gather_keys(key_cache, value_cache, kv_index)
     projected = attention(queries, visible_len, kv, offsets, out_weight, residual.shape[0])
-    hidden_state, block = norm(residual, projected, norm_gain, expert_ids, route_weights)
     dims = (x, y, z)
+    hidden_state, block, first = norm(
+        residual, projected, norm_gain, expert_ids, route_weights, residual.shape[0] << len(far)
+    )
     matrices = (w_gate, w_up, w_down)
-    own, got = spread(block, dims, far)
+    own, got = spread(block, first, dims, far)
     own_c = [swap(p, core) for p in own]
     got_c = [swap(p, core) for p in got]
     top = expert_ids.shape[1]

time: 131 us -> 128 us (0.977)
  starting transfers between devices: 38.3 us -> 35.4 us
    ppermute x36, starting transfers between devices: 38.3 us -> 35.4 us  [swap(): lax.ppermute(v, axis, [(i, i ^ mask) for i in range(lax.axis_size(axis))])]
  transfers between devices with their start and end apart: 36 -> 36, of which waited for: 20 -> 19; matrix products, arithmetic and copies ran while one was open for 1% -> 1% of each run, Pallas kernels for 8% -> 9%
where the time goes in v2:
time: 128 us
  waiting for transfers between devices  71.9 us (56%)
  starting transfers between devices  35.4 us (28%)
  Pallas kernels  15.6 us (12%)
  local copies, waits for them, and re-layouts  2.7 us (2%)
  other arithmetic  2.18 us (2%)
    ppermute x36, waiting for transfers between devices, swap(): lax.ppermute(v, axis, [(i, i ^ mask) for i in range(lax.axis_size(axis))])  71.9 us
    ppermute x36, starting transfers between devices, swap(): lax.ppermute(v, axis, [(i, i ^ mask) for i in range(lax.axis_size(axis))])  35.4 us
    pallas_call x8, Pallas kernels, call(): pl.pallas_call(kernel, out_shape=outs, in_specs=specs, out_specs=[pl.Bloc...  15.6 us
  transfers between devices with their start and end apart: 36, of which 19 were waited for; matrix products, arithmetic and copies ran while one was open for 1% of the time, Pallas kernels for 9%

profile of v2, /device:TPU:0, one launch (start us, length us, event | category | flops | bytes accessed | tf_op | source)
XLA Modules:
  0.0 128.2 jit_solution(1024663117138641766)
XLA Ops:
  1.0 3.0 %collective-permute-start = (bf16[512,256]{1,0:T(8,128)(2,1)S(1)}, bf16[512,256]{1,0:T(8,128)(2,1)S(1)}, u32[]{:S(2)}, u32[]{:S(2)}) collective-permute-start(bf16[512,256]{1,0:T(8,128)(2,1)S(1)} %pad_maximum_fusion.5.refs_0_), channel_id=1, source_target_pairs={{0,2},{1,3},{2,0},{3,1},{4,6},{5,7},{6,4},{7,5},{8,10},{9,11},{10,... | collective-permute-start | bytes 786440 | tf_op jit(solution)/shard_map/ppermute | solution.py:25
  4.1 6.3 %collective-permute-done.refs_1_ = bf16[512,256]{1,0:T(8,128)(2,1)S(1)} collective-permute-done((bf16[512,256]{1,0:T(8,128)(2,1)S(1)}, bf16[512,256]{1,0:T(8,128)(2,1)S(1)}, u32[]{:S(2)}, u32[]{:S(2)}) %collective-permute-start) | collective-permute-done | bytes 262176 | tf_op jit(solution)/shard_map/ppermute | solution.py:25
  12.6 2.3 %shard_map.119 = (bf16[2,64,1152]{2,1,0:T(8,128)(2,1)S(1)}, bf16[64,896]{1,0:T(8,128)(2,1)S(1)}, f32[64,896]{1,0:T(8,128)S(1)}) custom-call(bf16[256,512]{1,0:T(8,128)(2,1)S(1)} %copy-done.4, f32[256,1]{1,0:T(8,128)S(1)} %shard_map.118.column, bf16[512,256]{1,0:T(8,128)(2,1)S(1)} %pad_maximum_fusion.5.refs_0_, ...), custom_call_target="tpu_custom_call" | custom-call | flops 805306368 | bytes 4047872 | tf_op jit(solution)/shard_map/pallas_call | solution.py:48
  14.9 2.3 %shard_map.120 = (f32[2,64,1152]{2,1,0:T(8,128)S(1)}, bf16[2,64,896]{2,1,0:T(8,128)(2,1)S(1)}, f32[64,896]{1,0:T(8,128)S(1)}) custom-call(bf16[256,512]{1,0:T(8,128)(2,1)S(1)} %copy-done.4, f32[256,1]{1,0:T(8,128)S(1)} %shard_map.118.column, bf16[512,256]{1,0:T(8,128)(2,1)S(1)} %pad_maximum_fusion.5.refs_0_, ...), custom_call_target="tpu_custom_call" | custom-call | flops 805306368 | bytes 4572160 | tf_op jit(solution)/shard_map/pallas_call | solution.py:48
  20.6 4.7 %collective-permute-done.5 = bf16[2,64,896]{2,1,0:T(8,128)(2,1)S(1)} collective-permute-done((bf16[2,64,896]{2,1,0:T(8,128)(2,1)S(1)}, bf16[2,64,896]{2,1,0:T(8,128)(2,1)S(1)}, u32[]{:S(2)}, u32[]{:S(2)}) %collective-permute-start.5) | collective-permute-done | bytes 229408 | tf_op jit(solution)/shard_map/ppermute | solution.py:25
  30.7 3.2 %collective-permute-done.4 = bf16[64,1152]{1,0:T(8,128)(2,1)S(1)} collective-permute-done((bf16[64,1152]{1,0:T(8,128)(2,1)S(1)}, bf16[64,1152]{1,0:T(8,128)(2,1)S(1)}, u32[]{:S(2)}, u32[]{:S(2)}) %collective-permute-start.4) | collective-permute-done | bytes 147488 | tf_op jit(solution)/shard_map/ppermute | solution.py:25
  33.9 3.5 %collective-permute-start.7 = (bf16[32,2048]{1,0:T(8,128)(2,1)S(1)}, bf16[32,2048]{1,0:T(8,128)(2,1)S(1)}, u32[]{:S(2)}, u32[]{:S(2)}) collective-permute-start(bf16[32,2048]{1,0:T(8,128)(2,1)S(1)} %fusion.7), channel_id=1, source_target_pairs={{0,24},{4,28},{8,16},{12,20},{16,8},{20,12},{24,0},{28,4},{1,25},{... | collective-permute-start | bytes 393224 | tf_op jit(solution)/shard_map/ppermute | solution.py:25
  37.4 3.4 %collective-permute-done.7 = bf16[32,2048]{1,0:T(8,128)(2,1)S(1)} collective-permute-done((bf16[32,2048]{1,0:T(8,128)(2,1)S(1)}, bf16[32,2048]{1,0:T(8,128)(2,1)S(1)}, u32[]{:S(2)}, u32[]{:S(2)}) %collective-permute-start.7) | collective-permute-done | bytes 131104 | tf_op jit(solution)/shard_map/ppermute | solution.py:25
  42.5 3.6 %collective-permute-start.10 = (bf16[32,2176]{1,0:T(8,128)(2,1)S(1)}, bf16[32,2176]{1,0:T(8,128)(2,1)S(1)}, u32[]{:S(2)}, u32[]{:S(2)}) collective-permute-start(bf16[32,2176]{1,0:T(8,128)(2,1)S(1)} %get-tuple-element.22), channel_id=1, source_target_pairs={{0,24},{4,28},{8,16},{12,20},{16,8},{20,12},{24,0},{28,4},{1,25},{... | collective-permute-start | bytes 417800 | tf_op jit(solution)/shard_map/ppermute | solution.py:25
  46.5 3.3 %collective-permute-done.10 = bf16[32,2176]{1,0:T(8,128)(2,1)S(1)} collective-permute-done((bf16[32,2176]{1,0:T(8,128)(2,1)S(1)}, bf16[32,2176]{1,0:T(8,128)(2,1)S(1)}, u32[]{:S(2)}, u32[]{:S(2)}) %collective-permute-start.10) | collective-permute-done | bytes 139296 | tf_op jit(solution)/shard_map/ppermute | solution.py:25
  50.5 4.3 %collective-permute-done.13 = bf16[1,1,1,16,2176]{4,3,2,1,0:T(8,128)(2,1)S(1)} collective-permute-done((bf16[1,1,1,16,2176]{4,3,2,1,0:T(8,128)(2,1)S(1)}, bf16[1,1,1,16,2176]{4,3,2,1,0:T(8,128)(2,1)S(1)}, u32[]{:S(2)}, u32[]{:S(2)}) %collective-permute-start.13) | collective-permute-done | bytes 69664 | tf_op jit(solution)/shard_map/ppermute | solution.py:25
  56.8 4.4 %collective-permute-done.12 = bf16[1,2,1,24,2176]{4,3,2,1,0:T(8,128)(2,1)S(1)} collective-permute-done((bf16[1,2,1,24,2176]{4,3,2,1,0:T(8,128)(2,1)S(1)}, bf16[1,2,1,24,2176]{4,3,2,1,0:T(8,128)(2,1)S(1)}, u32[]{:S(2)}, u32[]{:S(2)}) %collective-permute-start.12) | collective-permute-done | bytes 208928 | tf_op jit(solution)/shard_map/ppermute | solution.py:25
  64.1 2.7 %shard_map.123 = bf16[256,2048]{1,0:T(8,128)(2,1)S(1)} custom-call(bf16[96,2176]{1,0:T(8,128)(2,1)S(1)} %collective-permute-done.15.refs_0_, bf16[96,2176]{1,0:T(8,128)(2,1)S(1)} %collective-permute-done.16.refs_1_, bf16[64,2176]{1,0:T(8,128)(2,1)S(1)} %collective-permute-done.17.refs_2_, bf16[1,2048,768]{2,1,0:T(8,128)(2,1)S(1)} %copy-done, ...), custom_call_target="tpu_custom_call" | custom-call | flops 2415919104 | bytes 11599872 | tf_op jit(solution)/shard_map/pallas_call | solution.py:48
  67.1 8.8 %collective-permute-done.21.refs_2_ = bf16[64,2176]{1,0:T(8,128)(2,1)S(1)} collective-permute-done((bf16[64,2176]{1,0:T(8,128)(2,1)S(1)}, bf16[64,2176]{1,0:T(8,128)(2,1)S(1)}, u32[]{:S(2)}, u32[]{:S(2)}) %collective-permute-start.21) | collective-permute-done | bytes 278560 | tf_op jit(solution)/shard_map/ppermute | solution.py:25
  76.5 2.6 %shard_map.122 = f32[256,2048]{1,0:T(8,128)S(1)} custom-call(bf16[96,2176]{1,0:T(8,128)(2,1)S(1)} %bitcast.107, bf16[96,2176]{1,0:T(8,128)(2,1)S(1)} %bitcast.110, bf16[64,2176]{1,0:T(8,128)(2,1)S(1)} %bitcast.113, bf16[1,2048,768]{2,1,0:T(8,128)(2,1)S(1)} %copy-done, bf16[1,2048,768]{2,1,0:T(8,128)(2,1)S(1)} %copy-done.1, bf16[1,768,2048]{2,1,0:T(8,128)(2,1)S(1)} %copy-done.2), custom_call_target="tpu_custom_call" | custom-call | flops 2415919104 | bytes 12648448 | tf_op jit(solution)/shard_map/pallas_call | solution.py:48
  79.1 2.9 %shard_map.124 = f32[256,2048]{1,0:T(8,128)S(1)} custom-call(bf16[96,2176]{1,0:T(8,128)(2,1)S(1)} %collective-permute-done.19.refs_0_, bf16[96,2176]{1,0:T(8,128)(2,1)S(1)} %collective-permute-done.20.refs_1_, bf16[64,2176]{1,0:T(8,128)(2,1)S(1)} %collective-permute-done.21.refs_2_, bf16[1,2048,768]{2,1,0:T(8,128)(2,1)S(1)} %copy-done, ...), custom_call_target="tpu_custom_call" | custom-call | flops 2415919104 | bytes 12648448 | tf_op jit(solution)/shard_map/pallas_call | solution.py:48
  82.0 2.7 %shard_map.125 = bf16[256,2048]{1,0:T(8,128)(2,1)S(1)} custom-call(bf16[96,2176]{1,0:T(8,128)(2,1)S(1)} %collective-permute-done.22.refs_0_, bf16[96,2176]{1,0:T(8,128)(2,1)S(1)} %collective-permute-done.23.refs_1_, bf16[64,2176]{1,0:T(8,128)(2,1)S(1)} %collective-permute-done.24.refs_2_, bf16[1,2048,768]{2,1,0:T(8,128)(2,1)S(1)} %copy-done, ...), custom_call_target="tpu_custom_call" | custom-call | flops 2415919104 | bytes 11599872 | tf_op jit(solution)/shard_map/pallas_call | solution.py:48
  88.2 8.3 %collective-permute-done.32 = bf16[2,2,16,2048]{3,2,1,0:T(8,128)(2,1)S(1)} collective-permute-done((bf16[2,2,16,2048]{3,2,1,0:T(8,128)(2,1)S(1)}, bf16[2,2,16,2048]{3,2,1,0:T(8,128)(2,1)S(1)}, u32[]{:S(2)}, u32[]{:S(2)}) %collective-permute-start.32) | collective-permute-done | bytes 262176 | tf_op jit(solution)/shard_map/ppermute | solution.py:25
  100.3 2.7 %collective-permute-done.33 = bf16[2,16,2048]{2,1,0:T(8,128)(2,1)S(1)} collective-permute-done((bf16[2,16,2048]{2,1,0:T(8,128)(2,1)S(1)}, bf16[2,16,2048]{2,1,0:T(8,128)(2,1)S(1)}, u32[]{:S(2)}, u32[]{:S(2)}) %collective-permute-start.33) | collective-permute-done | bytes 131104 | tf_op jit(solution)/shard_map/ppermute | solution.py:25
  104.6 5.3 %collective-permute-done.29 = bf16[2,2,24,2048]{3,2,1,0:T(8,128)(2,1)S(1)} collective-permute-done((bf16[2,2,24,2048]{3,2,1,0:T(8,128)(2,1)S(1)}, bf16[2,2,24,2048]{3,2,1,0:T(8,128)(2,1)S(1)}, u32[]{:S(2)}, u32[]{:S(2)}) %collective-permute-start.29) | collective-permute-done | bytes 393248 | tf_op jit(solution)/shard_map/ppermute | solution.py:25
  112.1 3.6 %collective-permute-done.30 = bf16[2,24,2048]{2,1,0:T(8,128)(2,1)S(1)} collective-permute-done((bf16[2,24,2048]{2,1,0:T(8,128)(2,1)S(1)}, bf16[2,24,2048]{2,1,0:T(8,128)(2,1)S(1)}, u32[]{:S(2)}, u32[]{:S(2)}) %collective-permute-start.30) | collective-permute-done | bytes 196640 | tf_op jit(solution)/shard_map/ppermute | solution.py:25
  116.1 2.4 %collective-permute-done.27 = bf16[2,24,2048]{2,1,0:T(8,128)(2,1)S(1)} collective-permute-done((bf16[2,24,2048]{2,1,0:T(8,128)(2,1)S(1)}, bf16[2,24,2048]{2,1,0:T(8,128)(2,1)S(1)}, u32[]{:S(2)}, u32[]{:S(2)}) %collective-permute-start.27) | collective-permute-done | bytes 196640 | tf_op jit(solution)/shard_map/ppermute | solution.py:25
  120.5 3.0 %collective-permute-start.35 = (bf16[32,2048]{1,0:T(8,128)(2,1)S(1)}, bf16[32,2048]{1,0:T(8,128)(2,1)S(1)}, u32[]{:S(2)}, u32[]{:S(2)}) collective-permute-start(bf16[32,2048]{1,0:T(8,128)(2,1)S(1)} %pad_maximum_fusion.9), channel_id=1, source_target_pairs={{0,24},{4,28},{8,16},{12,20},{16,8},{20,12},{24,0},{28,4},{1,25},{... | collective-permute-start | bytes 393224 | tf_op jit(solution)/shard_map/ppermute | solution.py:25
  123.6 3.9 %collective-permute-done.35 = bf16[32,2048]{1,0:T(8,128)(2,1)S(1)} collective-permute-done((bf16[32,2048]{1,0:T(8,128)(2,1)S(1)}, bf16[32,2048]{1,0:T(8,128)(2,1)S(1)}, u32[]{:S(2)}, u32[]{:S(2)}) %collective-permute-start.35) | collective-permute-done | bytes 131104 | tf_op jit(solution)/shard_map/ppermute | solution.py:25
  (109 shorter events, 34.7 us)
Async XLA Ops:
  1.0 9.3 %collective-permute-start = (bf16[512,256]{1,0:T(8,128)(2,1)S(1)}, bf16[512,256]{1,0:T(8,128)(2,1)S(1)}, u32[]{:S(2)}, u32[]{:S(2)}) collective-permute-start(bf16[512,256]{1,0:T(8,128)(2,1)S(1)} %pad_maximum_fusion.5.refs_0_), channel_id=1, source_target_pairs={{0,2},{1,3},{2,0},{3,1},{4,6},{5,7},{6,4},{7,5},{8,10},{9,11},{10,... | collective-permute-start | bytes 786440 | tf_op jit(solution)/shard_map/ppermute | solution.py:25
  4.1 7.1 %collective-permute-start.1 = (bf16[512,256]{1,0:T(8,128)(2,1)S(1)}, bf16[512,256]{1,0:T(8,128)(2,1)S(1)}, u32[]{:S(2)}, u32[]{:S(2)}) collective-permute-start(bf16[512,256]{1,0:T(8,128)(2,1)S(1)} %pad_maximum_fusion.5.refs_0_), channel_id=1, source_target_pairs={{0,1},{1,0},{2,3},{3,2},{4,5},{5,4},{6,7},{7,6},{8,9},{9,8},{10,11... | collective-permute-start | bytes 786440 | tf_op jit(solution)/shard_map/ppermute | solution.py:25
  17.2 8.1 %collective-permute-start.5 = (bf16[2,64,896]{2,1,0:T(8,128)(2,1)S(1)}, bf16[2,64,896]{2,1,0:T(8,128)(2,1)S(1)}, u32[]{:S(2)}, u32[]{:S(2)}) collective-permute-start(bf16[2,64,896]{2,1,0:T(8,128)(2,1)S(1)} %get-tuple-element.18), channel_id=1, source_target_pairs={{0,4},{4,0},{8,12},{12,8},{16,20},{20,16},{24,28},{28,24},{1,5},{5... | collective-permute-start | bytes 688136 | tf_op jit(solution)/shard_map/ppermute | solution.py:25
  19.1 9.6 %collective-permute-start.3 = (bf16[2,64,1152]{2,1,0:T(8,128)(2,1)S(1)}, bf16[2,64,1152]{2,1,0:T(8,128)(2,1)S(1)}, u32[]{:S(2)}, u32[]{:S(2)}) collective-permute-start(bf16[2,64,1152]{2,1,0:T(8,128)(2,1)S(1)} %get-tuple-element.16), channel_id=1, source_target_pairs={{0,8},{4,12},{8,0},{12,4},{16,24},{20,28},{24,16},{28,20},{1,9},{5... | collective-permute-start | bytes 884744 | tf_op jit(solution)/shard_map/ppermute | solution.py:25
  33.9 6.9 %collective-permute-start.7 = (bf16[32,2048]{1,0:T(8,128)(2,1)S(1)}, bf16[32,2048]{1,0:T(8,128)(2,1)S(1)}, u32[]{:S(2)}, u32[]{:S(2)}) collective-permute-start(bf16[32,2048]{1,0:T(8,128)(2,1)S(1)} %fusion.7), channel_id=1, source_target_pairs={{0,24},{4,28},{8,16},{12,20},{16,8},{20,12},{24,0},{28,4},{1,25},{... | collective-permute-start | bytes 393224 | tf_op jit(solution)/shard_map/ppermute | solution.py:25
  42.5 7.2 %collective-permute-start.10 = (bf16[32,2176]{1,0:T(8,128)(2,1)S(1)}, bf16[32,2176]{1,0:T(8,128)(2,1)S(1)}, u32[]{:S(2)}, u32[]{:S(2)}) collective-permute-start(bf16[32,2176]{1,0:T(8,128)(2,1)S(1)} %get-tuple-element.22), channel_id=1, source_target_pairs={{0,24},{4,28},{8,16},{12,20},{16,8},{20,12},{24,0},{28,4},{1,25},{... | collective-permute-start | bytes 417800 | tf_op jit(solution)/shard_map/ppermute | solution.py:25
  46.1 10.5 %collective-permute-start.9 = (bf16[2,1,1,24,2176]{4,3,2,1,0:T(8,128)(2,1)S(1)}, bf16[2,1,1,24,2176]{4,3,2,1,0:T(8,128)(2,1)S(1)}, u32[]{:S(2)}, u32[]{:S(2)}) collective-permute-start(bf16[2,1,1,24,2176]{4,3,2,1,0:T(8,128)(2,1)S(1)} %pad_maximum_fusion.6), channel_id=1, source_target_pairs={{0,4},{4,0},{8,12},{12,8},{16,20},{20,16},{24,28},{28,24},{1,5},{5... | collective-permute-start | bytes 626696 | tf_op jit(solution)/shard_map/ppermute | solution.py:25
  54.9 6.5 %collective-permute-start.14 = (bf16[1,1,2,16,2176]{4,3,2,1,0:T(8,128)(2,1)S(1)}, bf16[1,1,2,16,2176]{4,3,2,1,0:T(8,128)(2,1)S(1)}, u32[]{:S(2)}, u32[]{:S(2)}) collective-permute-start(bf16[1,1,2,16,2176]{4,3,2,1,0:T(8,128)(2,1)S(1)} %pad_maximum_fusion.8), channel_id=1, source_target_pairs={{0,2},{1,3},{2,0},{3,1},{4,6},{5,7},{6,4},{7,5},{8,10},{9,11},{10,... | collective-permute-start | bytes 417800 | tf_op jit(solution)/shard_map/ppermute | solution.py:25
  55.3 5.9 %collective-permute-start.12 = (bf16[1,2,1,24,2176]{4,3,2,1,0:T(8,128)(2,1)S(1)}, bf16[1,2,1,24,2176]{4,3,2,1,0:T(8,128)(2,1)S(1)}, u32[]{:S(2)}, u32[]{:S(2)}) collective-permute-start(bf16[1,2,1,24,2176]{4,3,2,1,0:T(8,128)(2,1)S(1)} %pad_maximum_fusion.7), channel_id=1, source_target_pairs={{0,8},{4,12},{8,0},{12,4},{16,24},{20,28},{24,16},{28,20},{1,9},{5... | collective-permute-start | bytes 626696 | tf_op jit(solution)/shard_map/ppermute | solution.py:25
  56.7 7.3 %collective-permute-start.15 = (bf16[96,2176]{1,0:T(8,128)(2,1)S(1)}, bf16[96,2176]{1,0:T(8,128)(2,1)S(1)}, u32[]{:S(2)}, u32[]{:S(2)}) collective-permute-start(bf16[96,2176]{1,0:T(8,128)(2,1)S(1)} %bitcast.105), channel_id=1, source_target_pairs={{0,1},{1,0},{2,3},{3,2},{4,5},{5,4},{6,7},{7,6},{8,9},{9,8},{10,11... | collective-permute-start | bytes 1253384 | tf_op jit(solution)/shard_map/ppermute | solution.py:25
  61.9 14.0 %collective-permute-start.19 = (bf16[96,2176]{1,0:T(8,128)(2,1)S(1)}, bf16[96,2176]{1,0:T(8,128)(2,1)S(1)}, u32[]{:S(2)}, u32[]{:S(2)}) collective-permute-start(bf16[96,2176]{1,0:T(8,128)(2,1)S(1)} %bitcast.106), channel_id=1, source_target_pairs={{0,8},{4,12},{8,0},{12,4},{16,24},{20,28},{24,16},{28,20},{1,9},{5... | collective-permute-start | bytes 1253384 | tf_op jit(solution)/shard_map/ppermute | solution.py:25
  63.2 13.2 %collective-permute-start.20 = (bf16[96,2176]{1,0:T(8,128)(2,1)S(1)}, bf16[96,2176]{1,0:T(8,128)(2,1)S(1)}, u32[]{:S(2)}, u32[]{:S(2)}) collective-permute-start(bf16[96,2176]{1,0:T(8,128)(2,1)S(1)} %bitcast.109), channel_id=1, source_target_pairs={{0,2},{1,3},{2,0},{3,1},{4,6},{5,7},{6,4},{7,5},{8,10},{9,11},{10,... | collective-permute-start | bytes 1253384 | tf_op jit(solution)/shard_map/ppermute | solution.py:25
  66.8 18.5 %collective-permute-start.18 = (bf16[256,2048]{1,0:T(8,128)(2,1)S(1)}, bf16[256,2048]{1,0:T(8,128)(2,1)S(1)}, u32[]{:S(2)}, u32[]{:S(2)}) collective-permute-start(bf16[256,2048]{1,0:T(8,128)(2,1)S(1)} %shard_map.123), channel_id=1, source_target_pairs={{0,1},{1,0},{2,3},{3,2},{4,5},{5,4},{6,7},{7,6},{8,9},{9,8},{10,11... | collective-permute-start | bytes 3145736 | tf_op jit(solution)/shard_map/ppermute | solution.py:25
  66.8 9.1 %collective-permute-start.21 = (bf16[64,2176]{1,0:T(8,128)(2,1)S(1)}, bf16[64,2176]{1,0:T(8,128)(2,1)S(1)}, u32[]{:S(2)}, u32[]{:S(2)}) collective-permute-start(bf16[64,2176]{1,0:T(8,128)(2,1)S(1)} %bitcast.112), channel_id=1, source_target_pairs={{0,4},{4,0},{8,12},{12,8},{16,20},{20,16},{24,28},{28,24},{1,5},{5... | collective-permute-start | bytes 835592 | tf_op jit(solution)/shard_map/ppermute | solution.py:25
  75.9 6.1 %collective-permute-start.24 = (bf16[64,2176]{1,0:T(8,128)(2,1)S(1)}, bf16[64,2176]{1,0:T(8,128)(2,1)S(1)}, u32[]{:S(2)}, u32[]{:S(2)}) collective-permute-start(bf16[64,2176]{1,0:T(8,128)(2,1)S(1)} %collective-permute-done.21.refs_2_), channel_id=1, source_target_pairs={{0,1},{1,0},{2,3},{3,2},{4,5},{5,4},{6,7},{7,6},{8,9},{9,8},{10,11... | collective-permute-start | bytes 835592 | tf_op jit(solution)/shard_map/ppermute | solution.py:25
  75.9 6.1 %collective-permute-start.22 = (bf16[96,2176]{1,0:T(8,128)(2,1)S(1)}, bf16[96,2176]{1,0:T(8,128)(2,1)S(1)}, u32[]{:S(2)}, u32[]{:S(2)}) collective-permute-start(bf16[96,2176]{1,0:T(8,128)(2,1)S(1)} %collective-permute-done.19.refs_0_), channel_id=1, source_target_pairs={{0,1},{1,0},{2,3},{3,2},{4,5},{5,4},{6,7},{7,6},{8,9},{9,8},{10,11... | collective-permute-start | bytes 1253384 | tf_op jit(solution)/shard_map/ppermute | solution.py:25
  87.8 8.7 %collective-permute-start.32 = (bf16[2,2,16,2048]{3,2,1,0:T(8,128)(2,1)S(1)}, bf16[2,2,16,2048]{3,2,1,0:T(8,128)(2,1)S(1)}, u32[]{:S(2)}, u32[]{:S(2)}) collective-permute-start(bf16[2,2,16,2048]{3,2,1,0:T(8,128)(2,1)S(1)} %bitcast.127), channel_id=1, source_target_pairs={{0,4},{4,0},{8,12},{12,8},{16,20},{20,16},{24,28},{28,24},{1,5},{5... | collective-permute-start | bytes 786440 | tf_op jit(solution)/shard_map/ppermute | solution.py:25
  96.5 6.4 %collective-permute-start.33 = (bf16[2,16,2048]{2,1,0:T(8,128)(2,1)S(1)}, bf16[2,16,2048]{2,1,0:T(8,128)(2,1)S(1)}, u32[]{:S(2)}, u32[]{:S(2)}) collective-permute-start(bf16[2,16,2048]{2,1,0:T(8,128)(2,1)S(1)} %get-tuple-element.35), channel_id=1, source_target_pairs={{0,2},{1,3},{2,0},{3,1},{4,6},{5,7},{6,4},{7,5},{8,10},{9,11},{10,... | collective-permute-start | bytes 393224 | tf_op jit(solution)/shard_map/ppermute | solution.py:25
  97.8 12.1 %collective-permute-start.29 = (bf16[2,2,24,2048]{3,2,1,0:T(8,128)(2,1)S(1)}, bf16[2,2,24,2048]{3,2,1,0:T(8,128)(2,1)S(1)}, u32[]{:S(2)}, u32[]{:S(2)}) collective-permute-start(bf16[2,2,24,2048]{3,2,1,0:T(8,128)(2,1)S(1)} %bitcast.126), channel_id=1, source_target_pairs={{0,2},{1,3},{2,0},{3,1},{4,6},{5,7},{6,4},{7,5},{8,10},{9,11},{10,... | collective-permute-start | bytes 1179656 | tf_op jit(solution)/shard_map/ppermute | solution.py:25
  98.7 12.9 %collective-permute-start.26 = (bf16[2,2,24,2048]{3,2,1,0:T(8,128)(2,1)S(1)}, bf16[2,2,24,2048]{3,2,1,0:T(8,128)(2,1)S(1)}, u32[]{:S(2)}, u32[]{:S(2)}) collective-permute-start(bf16[2,2,24,2048]{3,2,1,0:T(8,128)(2,1)S(1)} %bitcast.125), channel_id=1, source_target_pairs={{0,8},{4,12},{8,0},{12,4},{16,24},{20,28},{24,16},{28,20},{1,9},{5... | collective-permute-start | bytes 1179656 | tf_op jit(solution)/shard_map/ppermute | solution.py:25
  103.0 9.1 %collective-permute-start.34 = (bf16[16,2048]{1,0:T(8,128)(2,1)S(1)}, bf16[16,2048]{1,0:T(8,128)(2,1)S(1)}, u32[]{:S(2)}, u32[]{:S(2)}) collective-permute-start(bf16[16,2048]{1,0:T(8,128)(2,1)S(1)} %fusion.31), channel_id=1, source_target_pairs={{0,8},{4,12},{8,0},{12,4},{16,24},{20,28},{24,16},{28,20},{1,9},{5... | collective-permute-start | bytes 196616 | tf_op jit(solution)/shard_map/ppermute | solution.py:25
  110.0 5.7 %collective-permute-start.30 = (bf16[2,24,2048]{2,1,0:T(8,128)(2,1)S(1)}, bf16[2,24,2048]{2,1,0:T(8,128)(2,1)S(1)}, u32[]{:S(2)}, u32[]{:S(2)}) collective-permute-start(bf16[2,24,2048]{2,1,0:T(8,128)(2,1)S(1)} %get-tuple-element.31), channel_id=1, source_target_pairs={{0,8},{4,12},{8,0},{12,4},{16,24},{20,28},{24,16},{28,20},{1,9},{5... | collective-permute-start | bytes 589832 | tf_op jit(solution)/shard_map/ppermute | solution.py:25
  111.7 6.8 %collective-permute-start.27 = (bf16[2,24,2048]{2,1,0:T(8,128)(2,1)S(1)}, bf16[2,24,2048]{2,1,0:T(8,128)(2,1)S(1)}, u32[]{:S(2)}, u32[]{:S(2)}) collective-permute-start(bf16[2,24,2048]{2,1,0:T(8,128)(2,1)S(1)} %get-tuple-element.29), channel_id=1, source_target_pairs={{0,4},{4,0},{8,12},{12,8},{16,20},{20,16},{24,28},{28,24},{1,5},{5... | collective-permute-start | bytes 589832 | tf_op jit(solution)/shard_map/ppermute | solution.py:25
  120.5 6.9 %collective-permute-start.35 = (bf16[32,2048]{1,0:T(8,128)(2,1)S(1)}, bf16[32,2048]{1,0:T(8,128)(2,1)S(1)}, u32[]{:S(2)}, u32[]{:S(2)}) collective-permute-start(bf16[32,2048]{1,0:T(8,128)(2,1)S(1)} %pad_maximum_fusion.9), channel_id=1, source_target_pairs={{0,24},{4,28},{8,16},{12,20},{16,8},{20,12},{24,0},{28,4},{1,25},{... | collective-permute-start | bytes 393224 | tf_op jit(solution)/shard_map/ppermute | solution.py:25
  (22 other events, 186.2 us)

commit v3 on v2

--- a/solution.py
+++ b/solution.py
@@ -261,7 +261,8 @@
 
 
 def expert_kernel(cfg, *refs):
-    parts, (gate, up, down), refs = refs[:3], refs[3:6], refs[6:]
+    count = cfg["parts"]
+    parts, (gate, up, down), refs = refs[:count], refs[count : count + 3], refs[count + 3 :]
     out, hidden = refs
     mine = (lax.axis_index("head") * cfg["blocks"] + lax.axis_index("qblk")).astype(F32)
     top = cfg["top"]
@@ -300,7 +301,7 @@
     width = parts[0].shape[1] - LANES
     rows = sum(p.shape[0] for p in parts)
     hidden = matrices[0].shape[2]
-    cfg = dict(blocks=lax.axis_size("qblk"), top=top, chunk=2 * TILE)
+    cfg = dict(blocks=lax.axis_size("qblk"), top=top, chunk=2 * TILE, parts=len(parts))
     args = [*parts, *matrices]
     return call(
         functools.partial(expert_kernel, cfg),
@@ -403,18 +404,26 @@
     own_c = [swap(p, core) for p in own]
     got_c = [swap(p, core) for p in got]
     top = expert_ids.shape[1]
-    back = expert(own_c, matrices, top, BF16)
-    back = swap(back, core)
-    kept = expert(own, matrices, top, F32)
-    kept = kept + back.astype(F32)
-    back = expert(got_c, matrices, top, BF16)
-    back = swap(back, core)
-    sent = expert(got, matrices, top, F32)
-    sent = (sent + back.astype(F32)).astype(BF16)
-    cuts = [0]
-    for p in own:
-        cuts.append(cuts[-1] + p.shape[0])
-    split = [[v[cuts[i] : cuts[i + 1]] for i in range(3)] for v in (sent, kept)]
+
+    def run(parts, kind):
+        return expert(parts, matrices, top, kind)
+
+    def cut_up(value, parts):
+        pieces, at = [], 0
+        for p in parts:
+            pieces.append(value[at : at + p.shape[0]])
+            at += p.shape[0]
+        return pieces
+
+    back = swap(run(own_c, BF16), core)
+    mine = cut_up(run(own, F32), own)
+    kept = [m + b.astype(F32) for m, b in zip(mine, cut_up(back, own), strict=True)]
+    sent = []
+    for which in (slice(0, 1), slice(1, 3)):
+        mine = run(got[which], F32)
+        back = swap(run(got_c[which], BF16), core)
+        sent += cut_up((mine + back.astype(F32)).astype(BF16), got[which])
+    split = (sent, kept)
     mix = fold(*split, dims, far)
     return (hidden_state + mix).astype(BF16)
 

time: 128 us -> 132 us (1.031)
  starting transfers between devices: 35.4 us -> 38.9 us
  Pallas kernels: 15.6 us -> 17.1 us
    ppermute x36 -> x37, starting transfers between devices: 35.4 us -> 38.9 us  [swap(): lax.ppermute(v, axis, [(i, i ^ mask) for i in range(lax.axis_size(axis))])]
    pallas_call x8 -> x10, Pallas kernels: 15.6 us -> 17.1 us  [call(): pl.pallas_call(kernel, out_shape=outs, in_specs=specs, out_specs=[pl.Bloc...]
    ppermute x36 -> x37, waiting for transfers between devices: 71.9 us -> 70.8 us  [swap(): lax.ppermute(v, axis, [(i, i ^ mask) for i in range(lax.axis_size(axis))])]
  transfers between devices with their start and end apart: 36 -> 37, of which waited for: 19 -> 21; matrix products, arithmetic and copies ran while one was open for 1% -> 1% of each run, Pallas kernels for 9% -> 9%
where the time goes in v3:
time: 132 us
  waiting for transfers between devices  70.8 us (54%)
  starting transfers between devices  38.9 us (29%)
  Pallas kernels  17.1 us (13%)
  local copies, waits for them, and re-layouts  2.53 us (2%)
  other arithmetic  2.09 us (2%)
    ppermute x37, waiting for transfers between devices, swap(): lax.ppermute(v, axis, [(i, i ^ mask) for i in range(lax.axis_size(axis))])  70.8 us
    ppermute x37, starting transfers between devices, swap(): lax.ppermute(v, axis, [(i, i ^ mask) for i in range(lax.axis_size(axis))])  38.9 us
    pallas_call x10, Pallas kernels, call(): pl.pallas_call(kernel, out_shape=outs, in_specs=specs, out_specs=[pl.Bloc...  17.1 us
  transfers between devices with their start and end apart: 37, of which 21 were waited for; matrix products, arithmetic and copies ran while one was open for 1% of the time, Pallas kernels for 9%

profile of v3, /device:TPU:0, one launch (start us, length us, event | category | flops | bytes accessed | tf_op | source)
XLA Modules:
  0.0 131.8 jit_solution(2904844887450466510)
XLA Ops:
  1.0 3.0 %collective-permute-start = (bf16[512,256]{1,0:T(8,128)(2,1)S(1)}, bf16[512,256]{1,0:T(8,128)(2,1)S(1)}, u32[]{:S(2)}, u32[]{:S(2)}) collective-permute-start(bf16[512,256]{1,0:T(8,128)(2,1)S(1)} %pad_maximum_fusion.5.refs_0_), channel_id=1, source_target_pairs={{0,2},{1,3},{2,0},{3,1},{4,6},{5,7},{6,4},{7,5},{8,10},{9,11},{10,... | collective-permute-start | bytes 786440 | tf_op jit(solution)/shard_map/ppermute | solution.py:25
  4.1 6.3 %collective-permute-done.refs_1_ = bf16[512,256]{1,0:T(8,128)(2,1)S(1)} collective-permute-done((bf16[512,256]{1,0:T(8,128)(2,1)S(1)}, bf16[512,256]{1,0:T(8,128)(2,1)S(1)}, u32[]{:S(2)}, u32[]{:S(2)}) %collective-permute-start) | collective-permute-done | bytes 262176 | tf_op jit(solution)/shard_map/ppermute | solution.py:25
  12.6 2.3 %shard_map.119 = (bf16[2,64,1152]{2,1,0:T(8,128)(2,1)S(1)}, bf16[64,896]{1,0:T(8,128)(2,1)S(1)}, f32[64,896]{1,0:T(8,128)S(1)}) custom-call(bf16[256,512]{1,0:T(8,128)(2,1)S(1)} %copy-done.4, f32[256,1]{1,0:T(8,128)S(1)} %shard_map.118.column, bf16[512,256]{1,0:T(8,128)(2,1)S(1)} %pad_maximum_fusion.5.refs_0_, ...), custom_call_target="tpu_custom_call" | custom-call | flops 805306368 | bytes 4047872 | tf_op jit(solution)/shard_map/pallas_call | solution.py:48
  14.9 2.3 %shard_map.120 = (f32[2,64,1152]{2,1,0:T(8,128)S(1)}, bf16[2,64,896]{2,1,0:T(8,128)(2,1)S(1)}, f32[64,896]{1,0:T(8,128)S(1)}) custom-call(bf16[256,512]{1,0:T(8,128)(2,1)S(1)} %copy-done.4, f32[256,1]{1,0:T(8,128)S(1)} %shard_map.118.column, bf16[512,256]{1,0:T(8,128)(2,1)S(1)} %pad_maximum_fusion.5.refs_0_, ...), custom_call_target="tpu_custom_call" | custom-call | flops 805306368 | bytes 4572160 | tf_op jit(solution)/shard_map/pallas_call | solution.py:48
  20.6 4.7 %collective-permute-done.5 = bf16[2,64,896]{2,1,0:T(8,128)(2,1)S(1)} collective-permute-done((bf16[2,64,896]{2,1,0:T(8,128)(2,1)S(1)}, bf16[2,64,896]{2,1,0:T(8,128)(2,1)S(1)}, u32[]{:S(2)}, u32[]{:S(2)}) %collective-permute-start.5) | collective-permute-done | bytes 229408 | tf_op jit(solution)/shard_map/ppermute | solution.py:25
  30.7 3.2 %collective-permute-done.4 = bf16[64,1152]{1,0:T(8,128)(2,1)S(1)} collective-permute-done((bf16[64,1152]{1,0:T(8,128)(2,1)S(1)}, bf16[64,1152]{1,0:T(8,128)(2,1)S(1)}, u32[]{:S(2)}, u32[]{:S(2)}) %collective-permute-start.4) | collective-permute-done | bytes 147488 | tf_op jit(solution)/shard_map/ppermute | solution.py:25
  33.9 3.5 %collective-permute-start.7 = (bf16[32,2048]{1,0:T(8,128)(2,1)S(1)}, bf16[32,2048]{1,0:T(8,128)(2,1)S(1)}, u32[]{:S(2)}, u32[]{:S(2)}) collective-permute-start(bf16[32,2048]{1,0:T(8,128)(2,1)S(1)} %fusion.7), channel_id=1, source_target_pairs={{0,24},{4,28},{8,16},{12,20},{16,8},{20,12},{24,0},{28,4},{1,25},{... | collective-permute-start | bytes 393224 | tf_op jit(solution)/shard_map/ppermute | solution.py:25
  37.4 3.4 %collective-permute-done.7 = bf16[32,2048]{1,0:T(8,128)(2,1)S(1)} collective-permute-done((bf16[32,2048]{1,0:T(8,128)(2,1)S(1)}, bf16[32,2048]{1,0:T(8,128)(2,1)S(1)}, u32[]{:S(2)}, u32[]{:S(2)}) %collective-permute-start.7) | collective-permute-done | bytes 131104 | tf_op jit(solution)/shard_map/ppermute | solution.py:25
  42.5 3.6 %collective-permute-start.10 = (bf16[32,2176]{1,0:T(8,128)(2,1)S(1)}, bf16[32,2176]{1,0:T(8,128)(2,1)S(1)}, u32[]{:S(2)}, u32[]{:S(2)}) collective-permute-start(bf16[32,2176]{1,0:T(8,128)(2,1)S(1)} %get-tuple-element.22), channel_id=1, source_target_pairs={{0,24},{4,28},{8,16},{12,20},{16,8},{20,12},{24,0},{28,4},{1,25},{... | collective-permute-start | bytes 417800 | tf_op jit(solution)/shard_map/ppermute | solution.py:25
  46.5 3.3 %collective-permute-done.10 = bf16[32,2176]{1,0:T(8,128)(2,1)S(1)} collective-permute-done((bf16[32,2176]{1,0:T(8,128)(2,1)S(1)}, bf16[32,2176]{1,0:T(8,128)(2,1)S(1)}, u32[]{:S(2)}, u32[]{:S(2)}) %collective-permute-start.10) | collective-permute-done | bytes 139296 | tf_op jit(solution)/shard_map/ppermute | solution.py:25
  50.5 4.3 %collective-permute-done.13 = bf16[1,1,1,16,2176]{4,3,2,1,0:T(8,128)(2,1)S(1)} collective-permute-done((bf16[1,1,1,16,2176]{4,3,2,1,0:T(8,128)(2,1)S(1)}, bf16[1,1,1,16,2176]{4,3,2,1,0:T(8,128)(2,1)S(1)}, u32[]{:S(2)}, u32[]{:S(2)}) %collective-permute-start.13) | collective-permute-done | bytes 69664 | tf_op jit(solution)/shard_map/ppermute | solution.py:25
  57.6 2.4 %collective-permute-done.14 = bf16[1,1,2,16,2176]{4,3,2,1,0:T(8,128)(2,1)S(1)} collective-permute-done((bf16[1,1,2,16,2176]{4,3,2,1,0:T(8,128)(2,1)S(1)}, bf16[1,1,2,16,2176]{4,3,2,1,0:T(8,128)(2,1)S(1)}, u32[]{:S(2)}, u32[]{:S(2)}) %collective-permute-start.14) | collective-permute-done | bytes 139296 | tf_op jit(solution)/shard_map/ppermute | solution.py:25
  60.1 2.3 %collective-permute-done.12 = bf16[1,2,1,24,2176]{4,3,2,1,0:T(8,128)(2,1)S(1)} collective-permute-done((bf16[1,2,1,24,2176]{4,3,2,1,0:T(8,128)(2,1)S(1)}, bf16[1,2,1,24,2176]{4,3,2,1,0:T(8,128)(2,1)S(1)}, u32[]{:S(2)}, u32[]{:S(2)}) %collective-permute-start.12) | collective-permute-done | bytes 208928 | tf_op jit(solution)/shard_map/ppermute | solution.py:25
  63.0 3.7 %collective-permute-done.26.refs_1_ = bf16[64,2176]{1,0:T(8,128)(2,1)S(1)} collective-permute-done((bf16[64,2176]{1,0:T(8,128)(2,1)S(1)}, bf16[64,2176]{1,0:T(8,128)(2,1)S(1)}, u32[]{:S(2)}, u32[]{:S(2)}) %collective-permute-start.26) | collective-permute-done | bytes 278560 | tf_op jit(solution)/shard_map/ppermute | solution.py:25
  68.9 2.7 %shard_map.123 = bf16[256,2048]{1,0:T(8,128)(2,1)S(1)} custom-call(bf16[96,2176]{1,0:T(8,128)(2,1)S(1)} %collective-permute-done.15.refs_0_, bf16[96,2176]{1,0:T(8,128)(2,1)S(1)} %collective-permute-done.16.refs_1_, bf16[64,2176]{1,0:T(8,128)(2,1)S(1)} %collective-permute-done.17.refs_2_, bf16[1,2048,768]{2,1,0:T(8,128)(2,1)S(1)} %copy-done, ...), custom_call_target="tpu_custom_call" | custom-call | flops 2415919104 | bytes 11599872 | tf_op jit(solution)/shard_map/pallas_call | solution.py:48
  71.7 5.0 %collective-permute-done.25.refs_0_ = bf16[96,2176]{1,0:T(8,128)(2,1)S(1)} collective-permute-done((bf16[96,2176]{1,0:T(8,128)(2,1)S(1)}, bf16[96,2176]{1,0:T(8,128)(2,1)S(1)}, u32[]{:S(2)}, u32[]{:S(2)}) %collective-permute-start.25) | collective-permute-done | bytes 417824 | tf_op jit(solution)/shard_map/ppermute | solution.py:25
  79.0 2.8 %shard_map.122 = f32[256,2048]{1,0:T(8,128)S(1)} custom-call(bf16[96,2176]{1,0:T(8,128)(2,1)S(1)} %bitcast.107, bf16[96,2176]{1,0:T(8,128)(2,1)S(1)} %bitcast.110, bf16[64,2176]{1,0:T(8,128)(2,1)S(1)} %bitcast.113, bf16[1,2048,768]{2,1,0:T(8,128)(2,1)S(1)} %copy-done, bf16[1,2048,768]{2,1,0:T(8,128)(2,1)S(1)} %copy-done.1, bf16[1,768,2048]{2,1,0:T(8,128)(2,1)S(1)} %copy-done.2), custom_call_target="tpu_custom_call" | custom-call | flops 2415919104 | bytes 12648448 | tf_op jit(solution)/shard_map/pallas_call | solution.py:48
  88.5 10.3 %collective-permute-done.22 = bf16[2,2,24,2048]{3,2,1,0:T(8,128)(2,1)S(1)} collective-permute-done((bf16[2,2,24,2048]{3,2,1,0:T(8,128)(2,1)S(1)}, bf16[2,2,24,2048]{3,2,1,0:T(8,128)(2,1)S(1)}, u32[]{:S(2)}, u32[]{:S(2)}) %collective-permute-start.22) | collective-permute-done | bytes 393248 | tf_op jit(solution)/shard_map/ppermute | solution.py:25
  103.0 3.7 %collective-permute-done.23 = bf16[2,24,2048]{2,1,0:T(8,128)(2,1)S(1)} collective-permute-done((bf16[2,24,2048]{2,1,0:T(8,128)(2,1)S(1)}, bf16[2,24,2048]{2,1,0:T(8,128)(2,1)S(1)}, u32[]{:S(2)}, u32[]{:S(2)}) %collective-permute-start.23) | collective-permute-done | bytes 196640 | tf_op jit(solution)/shard_map/ppermute | solution.py:25
  108.5 2.4 %collective-permute-done.33 = bf16[2,2,16,2048]{3,2,1,0:T(8,128)(2,1)S(1)} collective-permute-done((bf16[2,2,16,2048]{3,2,1,0:T(8,128)(2,1)S(1)}, bf16[2,2,16,2048]{3,2,1,0:T(8,128)(2,1)S(1)}, u32[]{:S(2)}, u32[]{:S(2)}) %collective-permute-start.33) | collective-permute-done | bytes 262176 | tf_op jit(solution)/shard_map/ppermute | solution.py:25
  113.8 2.4 %collective-permute-done.34 = bf16[2,16,2048]{2,1,0:T(8,128)(2,1)S(1)} collective-permute-done((bf16[2,16,2048]{2,1,0:T(8,128)(2,1)S(1)}, bf16[2,16,2048]{2,1,0:T(8,128)(2,1)S(1)}, u32[]{:S(2)}, u32[]{:S(2)}) %collective-permute-start.34) | collective-permute-done | bytes 131104 | tf_op jit(solution)/shard_map/ppermute | solution.py:25
  120.6 3.5 %collective-permute-done.32 = bf16[24,2048]{1,0:T(8,128)(2,1)S(1)} collective-permute-done((bf16[24,2048]{1,0:T(8,128)(2,1)S(1)}, bf16[24,2048]{1,0:T(8,128)(2,1)S(1)}, u32[]{:S(2)}, u32[]{:S(2)}) %collective-permute-start.32) | collective-permute-done | bytes 98336 | tf_op jit(solution)/shard_map/ppermute | solution.py:25
  124.1 3.7 %collective-permute-start.36 = (bf16[32,2048]{1,0:T(8,128)(2,1)S(1)}, bf16[32,2048]{1,0:T(8,128)(2,1)S(1)}, u32[]{:S(2)}, u32[]{:S(2)}) collective-permute-start(bf16[32,2048]{1,0:T(8,128)(2,1)S(1)} %pad_maximum_fusion.9), channel_id=1, source_target_pairs={{0,24},{4,28},{8,16},{12,20},{16,8},{20,12},{24,0},{28,4},{1,25},{... | collective-permute-start | bytes 393224 | tf_op jit(solution)/shard_map/ppermute | solution.py:25
  127.9 3.2 %collective-permute-done.36 = bf16[32,2048]{1,0:T(8,128)(2,1)S(1)} collective-permute-done((bf16[32,2048]{1,0:T(8,128)(2,1)S(1)}, bf16[32,2048]{1,0:T(8,128)(2,1)S(1)}, u32[]{:S(2)}, u32[]{:S(2)}) %collective-permute-start.36) | collective-permute-done | bytes 131104 | tf_op jit(solution)/shard_map/ppermute | solution.py:25
  (114 shorter events, 43.5 us)
Async XLA Ops:
  1.0 9.3 %collective-permute-start = (bf16[512,256]{1,0:T(8,128)(2,1)S(1)}, bf16[512,256]{1,0:T(8,128)(2,1)S(1)}, u32[]{:S(2)}, u32[]{:S(2)}) collective-permute-start(bf16[512,256]{1,0:T(8,128)(2,1)S(1)} %pad_maximum_fusion.5.refs_0_), channel_id=1, source_target_pairs={{0,2},{1,3},{2,0},{3,1},{4,6},{5,7},{6,4},{7,5},{8,10},{9,11},{10,... | collective-permute-start | bytes 786440 | tf_op jit(solution)/shard_map/ppermute | solution.py:25
  4.1 7.1 %collective-permute-start.1 = (bf16[512,256]{1,0:T(8,128)(2,1)S(1)}, bf16[512,256]{1,0:T(8,128)(2,1)S(1)}, u32[]{:S(2)}, u32[]{:S(2)}) collective-permute-start(bf16[512,256]{1,0:T(8,128)(2,1)S(1)} %pad_maximum_fusion.5.refs_0_), channel_id=1, source_target_pairs={{0,1},{1,0},{2,3},{3,2},{4,5},{5,4},{6,7},{7,6},{8,9},{9,8},{10,11... | collective-permute-start | bytes 786440 | tf_op jit(solution)/shard_map/ppermute | solution.py:25
  17.2 8.1 %collective-permute-start.5 = (bf16[2,64,896]{2,1,0:T(8,128)(2,1)S(1)}, bf16[2,64,896]{2,1,0:T(8,128)(2,1)S(1)}, u32[]{:S(2)}, u32[]{:S(2)}) collective-permute-start(bf16[2,64,896]{2,1,0:T(8,128)(2,1)S(1)} %get-tuple-element.18), channel_id=1, source_target_pairs={{0,4},{4,0},{8,12},{12,8},{16,20},{20,16},{24,28},{28,24},{1,5},{5... | collective-permute-start | bytes 688136 | tf_op jit(solution)/shard_map/ppermute | solution.py:25
  19.1 9.6 %collective-permute-start.3 = (bf16[2,64,1152]{2,1,0:T(8,128)(2,1)S(1)}, bf16[2,64,1152]{2,1,0:T(8,128)(2,1)S(1)}, u32[]{:S(2)}, u32[]{:S(2)}) collective-permute-start(bf16[2,64,1152]{2,1,0:T(8,128)(2,1)S(1)} %get-tuple-element.16), channel_id=1, source_target_pairs={{0,8},{4,12},{8,0},{12,4},{16,24},{20,28},{24,16},{28,20},{1,9},{5... | collective-permute-start | bytes 884744 | tf_op jit(solution)/shard_map/ppermute | solution.py:25
  33.9 6.9 %collective-permute-start.7 = (bf16[32,2048]{1,0:T(8,128)(2,1)S(1)}, bf16[32,2048]{1,0:T(8,128)(2,1)S(1)}, u32[]{:S(2)}, u32[]{:S(2)}) collective-permute-start(bf16[32,2048]{1,0:T(8,128)(2,1)S(1)} %fusion.7), channel_id=1, source_target_pairs={{0,24},{4,28},{8,16},{12,20},{16,8},{20,12},{24,0},{28,4},{1,25},{... | collective-permute-start | bytes 393224 | tf_op jit(solution)/shard_map/ppermute | solution.py:25
  42.5 7.2 %collective-permute-start.10 = (bf16[32,2176]{1,0:T(8,128)(2,1)S(1)}, bf16[32,2176]{1,0:T(8,128)(2,1)S(1)}, u32[]{:S(2)}, u32[]{:S(2)}) collective-permute-start(bf16[32,2176]{1,0:T(8,128)(2,1)S(1)} %get-tuple-element.22), channel_id=1, source_target_pairs={{0,24},{4,28},{8,16},{12,20},{16,8},{20,12},{24,0},{28,4},{1,25},{... | collective-permute-start | bytes 417800 | tf_op jit(solution)/shard_map/ppermute | solution.py:25
  46.1 10.5 %collective-permute-start.9 = (bf16[2,1,1,24,2176]{4,3,2,1,0:T(8,128)(2,1)S(1)}, bf16[2,1,1,24,2176]{4,3,2,1,0:T(8,128)(2,1)S(1)}, u32[]{:S(2)}, u32[]{:S(2)}) collective-permute-start(bf16[2,1,1,24,2176]{4,3,2,1,0:T(8,128)(2,1)S(1)} %pad_maximum_fusion.6), channel_id=1, source_target_pairs={{0,4},{4,0},{8,12},{12,8},{16,20},{20,16},{24,28},{28,24},{1,5},{5... | collective-permute-start | bytes 626696 | tf_op jit(solution)/shard_map/ppermute | solution.py:25
  55.3 7.1 %collective-permute-start.12 = (bf16[1,2,1,24,2176]{4,3,2,1,0:T(8,128)(2,1)S(1)}, bf16[1,2,1,24,2176]{4,3,2,1,0:T(8,128)(2,1)S(1)}, u32[]{:S(2)}, u32[]{:S(2)}) collective-permute-start(bf16[1,2,1,24,2176]{4,3,2,1,0:T(8,128)(2,1)S(1)} %pad_maximum_fusion.7), channel_id=1, source_target_pairs={{0,8},{4,12},{8,0},{12,4},{16,24},{20,28},{24,16},{28,20},{1,9},{5... | collective-permute-start | bytes 626696 | tf_op jit(solution)/shard_map/ppermute | solution.py:25
  56.7 11.7 %collective-permute-start.19 = (bf16[96,2176]{1,0:T(8,128)(2,1)S(1)}, bf16[96,2176]{1,0:T(8,128)(2,1)S(1)}, u32[]{:S(2)}, u32[]{:S(2)}) collective-permute-start(bf16[96,2176]{1,0:T(8,128)(2,1)S(1)} %bitcast.105), channel_id=1, source_target_pairs={{0,8},{4,12},{8,0},{12,4},{16,24},{20,28},{24,16},{28,20},{1,9},{5... | collective-permute-start | bytes 1253384 | tf_op jit(solution)/shard_map/ppermute | solution.py:25
  57.5 11.4 %collective-permute-start.15 = (bf16[96,2176]{1,0:T(8,128)(2,1)S(1)}, bf16[96,2176]{1,0:T(8,128)(2,1)S(1)}, u32[]{:S(2)}, u32[]{:S(2)}) collective-permute-start(bf16[96,2176]{1,0:T(8,128)(2,1)S(1)} %bitcast.106), channel_id=1, source_target_pairs={{0,1},{1,0},{2,3},{3,2},{4,5},{5,4},{6,7},{7,6},{8,9},{9,8},{10,11... | collective-permute-start | bytes 1253384 | tf_op jit(solution)/shard_map/ppermute | solution.py:25
  60.0 6.7 %collective-permute-start.26 = (bf16[64,2176]{1,0:T(8,128)(2,1)S(1)}, bf16[64,2176]{1,0:T(8,128)(2,1)S(1)}, u32[]{:S(2)}, u32[]{:S(2)}) collective-permute-start(bf16[64,2176]{1,0:T(8,128)(2,1)S(1)} %bitcast.111), channel_id=1, source_target_pairs={{0,4},{4,0},{8,12},{12,8},{16,20},{20,16},{24,28},{28,24},{1,5},{5... | collective-permute-start | bytes 835592 | tf_op jit(solution)/shard_map/ppermute | solution.py:25
  66.7 10.0 %collective-permute-start.25 = (bf16[96,2176]{1,0:T(8,128)(2,1)S(1)}, bf16[96,2176]{1,0:T(8,128)(2,1)S(1)}, u32[]{:S(2)}, u32[]{:S(2)}) collective-permute-start(bf16[96,2176]{1,0:T(8,128)(2,1)S(1)} %bitcast.109), channel_id=1, source_target_pairs={{0,2},{1,3},{2,0},{3,1},{4,6},{5,7},{6,4},{7,5},{8,10},{9,11},{10,... | collective-permute-start | bytes 1253384 | tf_op jit(solution)/shard_map/ppermute | solution.py:25
  68.4 8.3 %collective-permute-start.20 = (bf16[96,2176]{1,0:T(8,128)(2,1)S(1)}, bf16[96,2176]{1,0:T(8,128)(2,1)S(1)}, u32[]{:S(2)}, u32[]{:S(2)}) collective-permute-start(bf16[96,2176]{1,0:T(8,128)(2,1)S(1)} %collective-permute-done.19.refs_0_), channel_id=1, source_target_pairs={{0,1},{1,0},{2,3},{3,2},{4,5},{5,4},{6,7},{7,6},{8,9},{9,8},{10,11... | collective-permute-start | bytes 1253384 | tf_op jit(solution)/shard_map/ppermute | solution.py:25
  68.4 16.8 %collective-permute-start.28 = (bf16[64,2176]{1,0:T(8,128)(2,1)S(1)}, bf16[64,2176]{1,0:T(8,128)(2,1)S(1)}, u32[]{:S(2)}, u32[]{:S(2)}) collective-permute-start(bf16[64,2176]{1,0:T(8,128)(2,1)S(1)} %collective-permute-done.26.refs_1_), channel_id=1, source_target_pairs={{0,1},{1,0},{2,3},{3,2},{4,5},{5,4},{6,7},{7,6},{8,9},{9,8},{10,11... | collective-permute-start | bytes 835592 | tf_op jit(solution)/shard_map/ppermute | solution.py:25
  71.6 16.5 %collective-permute-start.18 = (bf16[256,2048]{1,0:T(8,128)(2,1)S(1)}, bf16[256,2048]{1,0:T(8,128)(2,1)S(1)}, u32[]{:S(2)}, u32[]{:S(2)}) collective-permute-start(bf16[256,2048]{1,0:T(8,128)(2,1)S(1)} %shard_map.123), channel_id=1, source_target_pairs={{0,1},{1,0},{2,3},{3,2},{4,5},{5,4},{6,7},{7,6},{8,9},{9,8},{10,11... | collective-permute-start | bytes 3145736 | tf_op jit(solution)/shard_map/ppermute | solution.py:25
  76.7 8.5 %collective-permute-start.27 = (bf16[96,2176]{1,0:T(8,128)(2,1)S(1)}, bf16[96,2176]{1,0:T(8,128)(2,1)S(1)}, u32[]{:S(2)}, u32[]{:S(2)}) collective-permute-start(bf16[96,2176]{1,0:T(8,128)(2,1)S(1)} %collective-permute-done.25.refs_0_), channel_id=1, source_target_pairs={{0,1},{1,0},{2,3},{3,2},{4,5},{5,4},{6,7},{7,6},{8,9},{9,8},{10,11... | collective-permute-start | bytes 1253384 | tf_op jit(solution)/shard_map/ppermute | solution.py:25
  78.4 8.7 %collective-permute-start.21 = (bf16[96,2048]{1,0:T(8,128)(2,1)S(1)}, bf16[96,2048]{1,0:T(8,128)(2,1)S(1)}, u32[]{:S(2)}, u32[]{:S(2)}) collective-permute-start(bf16[96,2048]{1,0:T(8,128)(2,1)S(1)} %shard_map.125), channel_id=1, source_target_pairs={{0,1},{1,0},{2,3},{3,2},{4,5},{5,4},{6,7},{7,6},{8,9},{9,8},{10,11... | collective-permute-start | bytes 1179656 | tf_op jit(solution)/shard_map/ppermute | solution.py:25
  87.0 12.5 %collective-permute-start.29 = (bf16[160,2048]{1,0:T(8,128)(2,1)S(1)}, bf16[160,2048]{1,0:T(8,128)(2,1)S(1)}, u32[]{:S(2)}, u32[]{:S(2)}) collective-permute-start(bf16[160,2048]{1,0:T(8,128)(2,1)S(1)} %shard_map.127), channel_id=1, source_target_pairs={{0,1},{1,0},{2,3},{3,2},{4,5},{5,4},{6,7},{7,6},{8,9},{9,8},{10,11... | collective-permute-start | bytes 1966088 | tf_op jit(solution)/shard_map/ppermute | solution.py:25
  87.2 11.6 %collective-permute-start.22 = (bf16[2,2,24,2048]{3,2,1,0:T(8,128)(2,1)S(1)}, bf16[2,2,24,2048]{3,2,1,0:T(8,128)(2,1)S(1)}, u32[]{:S(2)}, u32[]{:S(2)}) collective-permute-start(bf16[2,2,24,2048]{3,2,1,0:T(8,128)(2,1)S(1)} %bitcast.126), channel_id=1, source_target_pairs={{0,8},{4,12},{8,0},{12,4},{16,24},{20,28},{24,16},{28,20},{1,9},{5... | collective-permute-start | bytes 1179656 | tf_op jit(solution)/shard_map/ppermute | solution.py:25
  98.8 7.8 %collective-permute-start.23 = (bf16[2,24,2048]{2,1,0:T(8,128)(2,1)S(1)}, bf16[2,24,2048]{2,1,0:T(8,128)(2,1)S(1)}, u32[]{:S(2)}, u32[]{:S(2)}) collective-permute-start(bf16[2,24,2048]{2,1,0:T(8,128)(2,1)S(1)} %get-tuple-element.27), channel_id=1, source_target_pairs={{0,4},{4,0},{8,12},{12,8},{16,20},{20,16},{24,28},{28,24},{1,5},{5... | collective-permute-start | bytes 589832 | tf_op jit(solution)/shard_map/ppermute | solution.py:25
  99.7 11.3 %collective-permute-start.33 = (bf16[2,2,16,2048]{3,2,1,0:T(8,128)(2,1)S(1)}, bf16[2,2,16,2048]{3,2,1,0:T(8,128)(2,1)S(1)}, u32[]{:S(2)}, u32[]{:S(2)}) collective-permute-start(bf16[2,2,16,2048]{3,2,1,0:T(8,128)(2,1)S(1)} %bitcast.127), channel_id=1, source_target_pairs={{0,4},{4,0},{8,12},{12,8},{16,20},{20,16},{24,28},{28,24},{1,5},{5... | collective-permute-start | bytes 786440 | tf_op jit(solution)/shard_map/ppermute | solution.py:25
  101.2 11.6 %collective-permute-start.30 = (bf16[2,2,24,2048]{3,2,1,0:T(8,128)(2,1)S(1)}, bf16[2,2,24,2048]{3,2,1,0:T(8,128)(2,1)S(1)}, u32[]{:S(2)}, u32[]{:S(2)}) collective-permute-start(bf16[2,2,24,2048]{3,2,1,0:T(8,128)(2,1)S(1)} %bitcast.125), channel_id=1, source_target_pairs={{0,2},{1,3},{2,0},{3,1},{4,6},{5,7},{6,4},{7,5},{8,10},{9,11},{10,... | collective-permute-start | bytes 1179656 | tf_op jit(solution)/shard_map/ppermute | solution.py:25
  106.7 21.2 %collective-permute-start.24 = (bf16[24,2048]{1,0:T(8,128)(2,1)S(1)}, bf16[24,2048]{1,0:T(8,128)(2,1)S(1)}, u32[]{:S(2)}, u32[]{:S(2)}) collective-permute-start(bf16[24,2048]{1,0:T(8,128)(2,1)S(1)} %fusion.29), channel_id=1, source_target_pairs={{0,2},{1,3},{2,0},{3,1},{4,6},{5,7},{6,4},{7,5},{8,10},{9,11},{10,... | collective-permute-start | bytes 294920 | tf_op jit(solution)/shard_map/ppermute | solution.py:25
  124.1 6.9 %collective-permute-start.36 = (bf16[32,2048]{1,0:T(8,128)(2,1)S(1)}, bf16[32,2048]{1,0:T(8,128)(2,1)S(1)}, u32[]{:S(2)}, u32[]{:S(2)}) collective-permute-start(bf16[32,2048]{1,0:T(8,128)(2,1)S(1)} %pad_maximum_fusion.9), channel_id=1, source_target_pairs={{0,24},{4,28},{8,16},{12,20},{16,8},{20,12},{24,0},{28,4},{1,25},{... | collective-permute-start | bytes 393224 | tf_op jit(solution)/shard_map/ppermute | solution.py:25
  (23 other events, 215.2 us)

commit v4 on v3

--- a/solution.py
+++ b/solution.py
@@ -234,6 +234,9 @@
     return total
 
 
+SUM_WAYS = ((0, 1, 2), (2, 1, 0), (0, 2, 1))
+
+
 def row_cuts(rows):
     units = rows // 8
     first = -(-units // 3)
@@ -315,21 +318,32 @@
 
 
 def fold(sends, keeps, dims, far):
-    keeps = [k.reshape(2, 2, -1, k.shape[-1]) for k in keeps]
-    sends = [s.reshape(2, 2, -1, s.shape[-1]) for s in sends]
-    got = [swap(sends[i], dims[(i + 2) % 3]) for i in range(3)]
+    sizes = [k.shape[0] // 4 for k in keeps]
+    half = sum(sizes) // 2
+    pieces, at = [], 0
+    for i, size in enumerate(sizes):
+        ends = [0, half - at, size] if 0 < half - at < size else [0, size]
+        pieces += [(i, a, b) for a, b in zip(ends[:-1], ends[1:], strict=True)]
+        at += size
+
+    def cut(values):
+        blocks = [v.reshape(2, 2, -1, v.shape[-1]) for v in values]
+        return [blocks[i][:, :, a:b] for i, a, b in pieces]
+
+    keeps, sends = cut(keeps), cut(sends)
+    ways = [SUM_WAYS[i] for i, _, _ in pieces]
+    got = [swap(s, dims[w[2]]) for s, w in zip(sends, ways, strict=True)]
     for stage in (1, 0):
         nxt = []
-        for i in range(3):
-            axis = (i + stage) % 3
-            left = sorted((i + s) % 3 for s in range(stage + 1))
-            at = left.index(axis)
-            keep = [lax.index_in_dim(keeps[i], k, at, False) for k in (0, 1)]
-            new = [lax.index_in_dim(got[i], k, at, False).astype(F32) for k in (0, 1)]
+        for j, way in enumerate(ways):
+            axis = way[stage]
+            at = sorted(way[: stage + 1]).index(axis)
+            keep = [lax.index_in_dim(keeps[j], k, at, False) for k in (0, 1)]
+            new = [lax.index_in_dim(got[j], k, at, False).astype(F32) for k in (0, 1)]
             sent = (keep[1] + new[1]).astype(BF16)
             nxt.append((keep[0] + new[0], swap(sent, dims[axis])))
         keeps, got = [n[0] for n in nxt], [n[1] for n in nxt]
-    total = jnp.concatenate([keeps[i] + got[i].astype(F32) for i in range(3)], axis=0)
+    total = jnp.concatenate([k + g.astype(F32) for k, g in zip(keeps, got, strict=True)], axis=0)
     return fold_far(total, far)
 
 

time: 132 us -> 130 us (0.985)
  waiting for transfers between devices: 70.8 us -> 64.4 us
  starting transfers between devices: 38.9 us -> 42.9 us
    ppermute x37 -> x40, waiting for transfers between devices: 70.8 us -> 64.4 us  [swap(): lax.ppermute(v, axis, [(i, i ^ mask) for i in range(lax.axis_size(axis))])]
    ppermute x37 -> x40, starting transfers between devices: 38.9 us -> 42.9 us  [swap(): lax.ppermute(v, axis, [(i, i ^ mask) for i in range(lax.axis_size(axis))])]
  transfers between devices with their start and end apart: 37 -> 40, of which waited for: 21 -> 22; matrix products, arithmetic and copies ran while one was open for 1% -> 1% of each run, Pallas kernels for 9% -> 10%
where the time goes in v4:
time: 130 us; the launch traced here: 129 us
  waiting for transfers between devices  64.4 us (50%)
  starting transfers between devices  42.9 us (33%)
  Pallas kernels  17.1 us (13%)
  local copies, waits for them, and re-layouts  2.52 us (2%)
  other arithmetic  2.07 us (2%)
    ppermute x40, waiting for transfers between devices, swap(): lax.ppermute(v, axis, [(i, i ^ mask) for i in range(lax.axis_size(axis))])  64.4 us
    ppermute x40, starting transfers between devices, swap(): lax.ppermute(v, axis, [(i, i ^ mask) for i in range(lax.axis_size(axis))])  42.9 us
    pallas_call x10, Pallas kernels, call(): pl.pallas_call(kernel, out_shape=outs, in_specs=specs, out_specs=[pl.Bloc...  17.1 us
  transfers between devices with their start and end apart: 40, of which 22 were waited for; matrix products, arithmetic and copies ran while one was open for 1% of the time, Pallas kernels for 10%

profile of v4, /device:TPU:0, one launch (start us, length us, event | category | flops | bytes accessed | tf_op | source)
XLA Modules:
  0.0 129.4 jit_solution(8153649788699201050)
XLA Ops:
  1.0 3.0 %collective-permute-start = (bf16[512,256]{1,0:T(8,128)(2,1)S(1)}, bf16[512,256]{1,0:T(8,128)(2,1)S(1)}, u32[]{:S(2)}, u32[]{:S(2)}) collective-permute-start(bf16[512,256]{1,0:T(8,128)(2,1)S(1)} %pad_maximum_fusion.4.refs_0_), channel_id=1, source_target_pairs={{0,2},{1,3},{2,0},{3,1},{4,6},{5,7},{6,4},{7,5},{8,10},{9,11},{10,... | collective-permute-start | bytes 786440 | tf_op jit(solution)/shard_map/ppermute | solution.py:25
  4.1 6.3 %collective-permute-done.refs_1_ = bf16[512,256]{1,0:T(8,128)(2,1)S(1)} collective-permute-done((bf16[512,256]{1,0:T(8,128)(2,1)S(1)}, bf16[512,256]{1,0:T(8,128)(2,1)S(1)}, u32[]{:S(2)}, u32[]{:S(2)}) %collective-permute-start) | collective-permute-done | bytes 262176 | tf_op jit(solution)/shard_map/ppermute | solution.py:25
  14.9 2.3 %shard_map.120 = (f32[2,64,1152]{2,1,0:T(8,128)S(1)}, bf16[2,64,896]{2,1,0:T(8,128)(2,1)S(1)}, f32[64,896]{1,0:T(8,128)S(1)}) custom-call(bf16[256,512]{1,0:T(8,128)(2,1)S(1)} %copy-done.4, f32[256,1]{1,0:T(8,128)S(1)} %shard_map.118.column, bf16[512,256]{1,0:T(8,128)(2,1)S(1)} %pad_maximum_fusion.4.refs_0_, ...), custom_call_target="tpu_custom_call" | custom-call | flops 805306368 | bytes 4572160 | tf_op jit(solution)/shard_map/pallas_call | solution.py:48
  20.6 4.7 %collective-permute-done.5 = bf16[2,64,896]{2,1,0:T(8,128)(2,1)S(1)} collective-permute-done((bf16[2,64,896]{2,1,0:T(8,128)(2,1)S(1)}, bf16[2,64,896]{2,1,0:T(8,128)(2,1)S(1)}, u32[]{:S(2)}, u32[]{:S(2)}) %collective-permute-start.5) | collective-permute-done | bytes 229408 | tf_op jit(solution)/shard_map/ppermute | solution.py:25
  30.7 3.2 %collective-permute-done.4 = bf16[64,1152]{1,0:T(8,128)(2,1)S(1)} collective-permute-done((bf16[64,1152]{1,0:T(8,128)(2,1)S(1)}, bf16[64,1152]{1,0:T(8,128)(2,1)S(1)}, u32[]{:S(2)}, u32[]{:S(2)}) %collective-permute-start.4) | collective-permute-done | bytes 147488 | tf_op jit(solution)/shard_map/ppermute | solution.py:25
  33.9 3.5 %collective-permute-start.7 = (bf16[32,2048]{1,0:T(8,128)(2,1)S(1)}, bf16[32,2048]{1,0:T(8,128)(2,1)S(1)}, u32[]{:S(2)}, u32[]{:S(2)}) collective-permute-start(bf16[32,2048]{1,0:T(8,128)(2,1)S(1)} %fusion.5), channel_id=1, source_target_pairs={{0,24},{4,28},{8,16},{12,20},{16,8},{20,12},{24,0},{28,4},{1,25},{... | collective-permute-start | bytes 393224 | tf_op jit(solution)/shard_map/ppermute | solution.py:25
  37.4 3.4 %collective-permute-done.7 = bf16[32,2048]{1,0:T(8,128)(2,1)S(1)} collective-permute-done((bf16[32,2048]{1,0:T(8,128)(2,1)S(1)}, bf16[32,2048]{1,0:T(8,128)(2,1)S(1)}, u32[]{:S(2)}, u32[]{:S(2)}) %collective-permute-start.7) | collective-permute-done | bytes 131104 | tf_op jit(solution)/shard_map/ppermute | solution.py:25
  42.5 3.6 %collective-permute-start.10 = (bf16[32,2176]{1,0:T(8,128)(2,1)S(1)}, bf16[32,2176]{1,0:T(8,128)(2,1)S(1)}, u32[]{:S(2)}, u32[]{:S(2)}) collective-permute-start(bf16[32,2176]{1,0:T(8,128)(2,1)S(1)} %get-tuple-element.22), channel_id=1, source_target_pairs={{0,24},{4,28},{8,16},{12,20},{16,8},{20,12},{24,0},{28,4},{1,25},{... | collective-permute-start | bytes 417800 | tf_op jit(solution)/shard_map/ppermute | solution.py:25
  46.5 3.3 %collective-permute-done.10 = bf16[32,2176]{1,0:T(8,128)(2,1)S(1)} collective-permute-done((bf16[32,2176]{1,0:T(8,128)(2,1)S(1)}, bf16[32,2176]{1,0:T(8,128)(2,1)S(1)}, u32[]{:S(2)}, u32[]{:S(2)}) %collective-permute-start.10) | collective-permute-done | bytes 139296 | tf_op jit(solution)/shard_map/ppermute | solution.py:25
  50.5 4.3 %collective-permute-done.13 = bf16[1,1,1,16,2176]{4,3,2,1,0:T(8,128)(2,1)S(1)} collective-permute-done((bf16[1,1,1,16,2176]{4,3,2,1,0:T(8,128)(2,1)S(1)}, bf16[1,1,1,16,2176]{4,3,2,1,0:T(8,128)(2,1)S(1)}, u32[]{:S(2)}, u32[]{:S(2)}) %collective-permute-start.13) | collective-permute-done | bytes 69664 | tf_op jit(solution)/shard_map/ppermute | solution.py:25
  57.6 2.4 %collective-permute-done.14 = bf16[1,1,2,16,2176]{4,3,2,1,0:T(8,128)(2,1)S(1)} collective-permute-done((bf16[1,1,2,16,2176]{4,3,2,1,0:T(8,128)(2,1)S(1)}, bf16[1,1,2,16,2176]{4,3,2,1,0:T(8,128)(2,1)S(1)}, u32[]{:S(2)}, u32[]{:S(2)}) %collective-permute-start.14) | collective-permute-done | bytes 139296 | tf_op jit(solution)/shard_map/ppermute | solution.py:25
  60.1 2.3 %collective-permute-done.12 = bf16[1,2,1,24,2176]{4,3,2,1,0:T(8,128)(2,1)S(1)} collective-permute-done((bf16[1,2,1,24,2176]{4,3,2,1,0:T(8,128)(2,1)S(1)}, bf16[1,2,1,24,2176]{4,3,2,1,0:T(8,128)(2,1)S(1)}, u32[]{:S(2)}, u32[]{:S(2)}) %collective-permute-start.12) | collective-permute-done | bytes 208928 | tf_op jit(solution)/shard_map/ppermute | solution.py:25
  63.0 3.7 %collective-permute-done.26.refs_1_ = bf16[64,2176]{1,0:T(8,128)(2,1)S(1)} collective-permute-done((bf16[64,2176]{1,0:T(8,128)(2,1)S(1)}, bf16[64,2176]{1,0:T(8,128)(2,1)S(1)}, u32[]{:S(2)}, u32[]{:S(2)}) %collective-permute-start.26) | collective-permute-done | bytes 278560 | tf_op jit(solution)/shard_map/ppermute | solution.py:25
  68.9 2.7 %shard_map.123 = bf16[256,2048]{1,0:T(8,128)(2,1)S(1)} custom-call(bf16[96,2176]{1,0:T(8,128)(2,1)S(1)} %collective-permute-done.15.refs_0_, bf16[96,2176]{1,0:T(8,128)(2,1)S(1)} %collective-permute-done.16.refs_1_, bf16[64,2176]{1,0:T(8,128)(2,1)S(1)} %collective-permute-done.17.refs_2_, bf16[1,2048,768]{2,1,0:T(8,128)(2,1)S(1)} %copy-done, ...), custom_call_target="tpu_custom_call" | custom-call | flops 2415919104 | bytes 11599872 | tf_op jit(solution)/shard_map/pallas_call | solution.py:48
  71.7 5.0 %collective-permute-done.25.refs_0_ = bf16[96,2176]{1,0:T(8,128)(2,1)S(1)} collective-permute-done((bf16[96,2176]{1,0:T(8,128)(2,1)S(1)}, bf16[96,2176]{1,0:T(8,128)(2,1)S(1)}, u32[]{:S(2)}, u32[]{:S(2)}) %collective-permute-start.25) | collective-permute-done | bytes 417824 | tf_op jit(solution)/shard_map/ppermute | solution.py:25
  79.0 2.8 %shard_map.122 = f32[256,2048]{1,0:T(8,128)S(1)} custom-call(bf16[96,2176]{1,0:T(8,128)(2,1)S(1)} %bitcast.142, bf16[96,2176]{1,0:T(8,128)(2,1)S(1)} %bitcast.145, bf16[64,2176]{1,0:T(8,128)(2,1)S(1)} %bitcast.148, bf16[1,2048,768]{2,1,0:T(8,128)(2,1)S(1)} %copy-done, bf16[1,2048,768]{2,1,0:T(8,128)(2,1)S(1)} %copy-done.1, bf16[1,768,2048]{2,1,0:T(8,128)(2,1)S(1)} %copy-done.2), custom_call_target="tpu_custom_call" | custom-call | flops 2415919104 | bytes 12648448 | tf_op jit(solution)/shard_map/pallas_call | solution.py:48
  91.2 3.7 %collective-permute-done.30 = bf16[2,2,8,2048]{3,2,1,0:T(8,128)(2,1)S(1)} collective-permute-done((bf16[2,2,8,2048]{3,2,1,0:T(8,128)(2,1)S(1)}, bf16[2,2,8,2048]{3,2,1,0:T(8,128)(2,1)S(1)}, u32[]{:S(2)}, u32[]{:S(2)}) %collective-permute-start.30) | collective-permute-done | bytes 131104 | tf_op jit(solution)/shard_map/ppermute | solution.py:25
  95.6 3.1 %collective-permute-done.22 = bf16[2,2,24,2048]{3,2,1,0:T(8,128)(2,1)S(1)} collective-permute-done((bf16[2,2,24,2048]{3,2,1,0:T(8,128)(2,1)S(1)}, bf16[2,2,24,2048]{3,2,1,0:T(8,128)(2,1)S(1)}, u32[]{:S(2)}, u32[]{:S(2)}) %collective-permute-start.22) | collective-permute-done | bytes 393248 | tf_op jit(solution)/shard_map/ppermute | solution.py:25
  103.7 3.0 %collective-permute-done.23 = bf16[2,24,2048]{2,1,0:T(8,128)(2,1)S(1)} collective-permute-done((bf16[2,24,2048]{2,1,0:T(8,128)(2,1)S(1)}, bf16[2,24,2048]{2,1,0:T(8,128)(2,1)S(1)}, u32[]{:S(2)}, u32[]{:S(2)}) %collective-permute-start.23) | collective-permute-done | bytes 196640 | tf_op jit(solution)/shard_map/ppermute | solution.py:25
  109.8 2.5 %collective-permute-done.36 = bf16[2,2,16,2048]{3,2,1,0:T(8,128)(2,1)S(1)} collective-permute-done((bf16[2,2,16,2048]{3,2,1,0:T(8,128)(2,1)S(1)}, bf16[2,2,16,2048]{3,2,1,0:T(8,128)(2,1)S(1)}, u32[]{:S(2)}, u32[]{:S(2)}) %collective-permute-start.36) | collective-permute-done | bytes 262176 | tf_op jit(solution)/shard_map/ppermute | solution.py:25
  114.7 2.6 %collective-permute-done.37 = bf16[2,16,2048]{2,1,0:T(8,128)(2,1)S(1)} collective-permute-done((bf16[2,16,2048]{2,1,0:T(8,128)(2,1)S(1)}, bf16[2,16,2048]{2,1,0:T(8,128)(2,1)S(1)}, u32[]{:S(2)}, u32[]{:S(2)}) %collective-permute-start.37) | collective-permute-done | bytes 131104 | tf_op jit(solution)/shard_map/ppermute | solution.py:25
  119.2 2.5 %collective-permute-done.38 = bf16[16,2048]{1,0:T(8,128)(2,1)S(1)} collective-permute-done((bf16[16,2048]{1,0:T(8,128)(2,1)S(1)}, bf16[16,2048]{1,0:T(8,128)(2,1)S(1)}, u32[]{:S(2)}, u32[]{:S(2)}) %collective-permute-start.38) | collective-permute-done | bytes 65568 | tf_op jit(solution)/shard_map/ppermute | solution.py:25
  121.8 3.7 %collective-permute-start.39 = (bf16[32,2048]{1,0:T(8,128)(2,1)S(1)}, bf16[32,2048]{1,0:T(8,128)(2,1)S(1)}, u32[]{:S(2)}, u32[]{:S(2)}) collective-permute-start(bf16[32,2048]{1,0:T(8,128)(2,1)S(1)} %pad_maximum_fusion.8), channel_id=1, source_target_pairs={{0,24},{4,28},{8,16},{12,20},{16,8},{20,12},{24,0},{28,4},{1,25},{... | collective-permute-start | bytes 393224 | tf_op jit(solution)/shard_map/ppermute | solution.py:25
  125.5 3.2 %collective-permute-done.39 = bf16[32,2048]{1,0:T(8,128)(2,1)S(1)} collective-permute-done((bf16[32,2048]{1,0:T(8,128)(2,1)S(1)}, bf16[32,2048]{1,0:T(8,128)(2,1)S(1)}, u32[]{:S(2)}, u32[]{:S(2)}) %collective-permute-start.39) | collective-permute-done | bytes 131104 | tf_op jit(solution)/shard_map/ppermute | solution.py:25
  (124 shorter events, 48.2 us)
Async XLA Ops:
  1.0 9.3 %collective-permute-start = (bf16[512,256]{1,0:T(8,128)(2,1)S(1)}, bf16[512,256]{1,0:T(8,128)(2,1)S(1)}, u32[]{:S(2)}, u32[]{:S(2)}) collective-permute-start(bf16[512,256]{1,0:T(8,128)(2,1)S(1)} %pad_maximum_fusion.4.refs_0_), channel_id=1, source_target_pairs={{0,2},{1,3},{2,0},{3,1},{4,6},{5,7},{6,4},{7,5},{8,10},{9,11},{10,... | collective-permute-start | bytes 786440 | tf_op jit(solution)/shard_map/ppermute | solution.py:25
  4.1 7.1 %collective-permute-start.1 = (bf16[512,256]{1,0:T(8,128)(2,1)S(1)}, bf16[512,256]{1,0:T(8,128)(2,1)S(1)}, u32[]{:S(2)}, u32[]{:S(2)}) collective-permute-start(bf16[512,256]{1,0:T(8,128)(2,1)S(1)} %pad_maximum_fusion.4.refs_0_), channel_id=1, source_target_pairs={{0,1},{1,0},{2,3},{3,2},{4,5},{5,4},{6,7},{7,6},{8,9},{9,8},{10,11... | collective-permute-start | bytes 786440 | tf_op jit(solution)/shard_map/ppermute | solution.py:25
  17.2 8.1 %collective-permute-start.5 = (bf16[2,64,896]{2,1,0:T(8,128)(2,1)S(1)}, bf16[2,64,896]{2,1,0:T(8,128)(2,1)S(1)}, u32[]{:S(2)}, u32[]{:S(2)}) collective-permute-start(bf16[2,64,896]{2,1,0:T(8,128)(2,1)S(1)} %get-tuple-element.18), channel_id=1, source_target_pairs={{0,4},{4,0},{8,12},{12,8},{16,20},{20,16},{24,28},{28,24},{1,5},{5... | collective-permute-start | bytes 688136 | tf_op jit(solution)/shard_map/ppermute | solution.py:25
  19.1 9.6 %collective-permute-start.3 = (bf16[2,64,1152]{2,1,0:T(8,128)(2,1)S(1)}, bf16[2,64,1152]{2,1,0:T(8,128)(2,1)S(1)}, u32[]{:S(2)}, u32[]{:S(2)}) collective-permute-start(bf16[2,64,1152]{2,1,0:T(8,128)(2,1)S(1)} %get-tuple-element.16), channel_id=1, source_target_pairs={{0,8},{4,12},{8,0},{12,4},{16,24},{20,28},{24,16},{28,20},{1,9},{5... | collective-permute-start | bytes 884744 | tf_op jit(solution)/shard_map/ppermute | solution.py:25
  33.9 6.9 %collective-permute-start.7 = (bf16[32,2048]{1,0:T(8,128)(2,1)S(1)}, bf16[32,2048]{1,0:T(8,128)(2,1)S(1)}, u32[]{:S(2)}, u32[]{:S(2)}) collective-permute-start(bf16[32,2048]{1,0:T(8,128)(2,1)S(1)} %fusion.5), channel_id=1, source_target_pairs={{0,24},{4,28},{8,16},{12,20},{16,8},{20,12},{24,0},{28,4},{1,25},{... | collective-permute-start | bytes 393224 | tf_op jit(solution)/shard_map/ppermute | solution.py:25
  42.5 7.2 %collective-permute-start.10 = (bf16[32,2176]{1,0:T(8,128)(2,1)S(1)}, bf16[32,2176]{1,0:T(8,128)(2,1)S(1)}, u32[]{:S(2)}, u32[]{:S(2)}) collective-permute-start(bf16[32,2176]{1,0:T(8,128)(2,1)S(1)} %get-tuple-element.22), channel_id=1, source_target_pairs={{0,24},{4,28},{8,16},{12,20},{16,8},{20,12},{24,0},{28,4},{1,25},{... | collective-permute-start | bytes 417800 | tf_op jit(solution)/shard_map/ppermute | solution.py:25
  46.1 10.5 %collective-permute-start.9 = (bf16[2,1,1,24,2176]{4,3,2,1,0:T(8,128)(2,1)S(1)}, bf16[2,1,1,24,2176]{4,3,2,1,0:T(8,128)(2,1)S(1)}, u32[]{:S(2)}, u32[]{:S(2)}) collective-permute-start(bf16[2,1,1,24,2176]{4,3,2,1,0:T(8,128)(2,1)S(1)} %pad_maximum_fusion.5), channel_id=1, source_target_pairs={{0,4},{4,0},{8,12},{12,8},{16,20},{20,16},{24,28},{28,24},{1,5},{5... | collective-permute-start | bytes 626696 | tf_op jit(solution)/shard_map/ppermute | solution.py:25
  55.3 7.1 %collective-permute-start.12 = (bf16[1,2,1,24,2176]{4,3,2,1,0:T(8,128)(2,1)S(1)}, bf16[1,2,1,24,2176]{4,3,2,1,0:T(8,128)(2,1)S(1)}, u32[]{:S(2)}, u32[]{:S(2)}) collective-permute-start(bf16[1,2,1,24,2176]{4,3,2,1,0:T(8,128)(2,1)S(1)} %pad_maximum_fusion.6), channel_id=1, source_target_pairs={{0,8},{4,12},{8,0},{12,4},{16,24},{20,28},{24,16},{28,20},{1,9},{5... | collective-permute-start | bytes 626696 | tf_op jit(solution)/shard_map/ppermute | solution.py:25
  56.7 11.7 %collective-permute-start.19 = (bf16[96,2176]{1,0:T(8,128)(2,1)S(1)}, bf16[96,2176]{1,0:T(8,128)(2,1)S(1)}, u32[]{:S(2)}, u32[]{:S(2)}) collective-permute-start(bf16[96,2176]{1,0:T(8,128)(2,1)S(1)} %bitcast.140), channel_id=1, source_target_pairs={{0,8},{4,12},{8,0},{12,4},{16,24},{20,28},{24,16},{28,20},{1,9},{5... | collective-permute-start | bytes 1253384 | tf_op jit(solution)/shard_map/ppermute | solution.py:25
  57.5 11.4 %collective-permute-start.15 = (bf16[96,2176]{1,0:T(8,128)(2,1)S(1)}, bf16[96,2176]{1,0:T(8,128)(2,1)S(1)}, u32[]{:S(2)}, u32[]{:S(2)}) collective-permute-start(bf16[96,2176]{1,0:T(8,128)(2,1)S(1)} %bitcast.141), channel_id=1, source_target_pairs={{0,1},{1,0},{2,3},{3,2},{4,5},{5,4},{6,7},{7,6},{8,9},{9,8},{10,11... | collective-permute-start | bytes 1253384 | tf_op jit(solution)/shard_map/ppermute | solution.py:25
  60.0 6.7 %collective-permute-start.26 = (bf16[64,2176]{1,0:T(8,128)(2,1)S(1)}, bf16[64,2176]{1,0:T(8,128)(2,1)S(1)}, u32[]{:S(2)}, u32[]{:S(2)}) collective-permute-start(bf16[64,2176]{1,0:T(8,128)(2,1)S(1)} %bitcast.146), channel_id=1, source_target_pairs={{0,4},{4,0},{8,12},{12,8},{16,20},{20,16},{24,28},{28,24},{1,5},{5... | collective-permute-start | bytes 835592 | tf_op jit(solution)/shard_map/ppermute | solution.py:25
  66.7 10.0 %collective-permute-start.25 = (bf16[96,2176]{1,0:T(8,128)(2,1)S(1)}, bf16[96,2176]{1,0:T(8,128)(2,1)S(1)}, u32[]{:S(2)}, u32[]{:S(2)}) collective-permute-start(bf16[96,2176]{1,0:T(8,128)(2,1)S(1)} %bitcast.144), channel_id=1, source_target_pairs={{0,2},{1,3},{2,0},{3,1},{4,6},{5,7},{6,4},{7,5},{8,10},{9,11},{10,... | collective-permute-start | bytes 1253384 | tf_op jit(solution)/shard_map/ppermute | solution.py:25
  68.4 8.3 %collective-permute-start.20 = (bf16[96,2176]{1,0:T(8,128)(2,1)S(1)}, bf16[96,2176]{1,0:T(8,128)(2,1)S(1)}, u32[]{:S(2)}, u32[]{:S(2)}) collective-permute-start(bf16[96,2176]{1,0:T(8,128)(2,1)S(1)} %collective-permute-done.19.refs_0_), channel_id=1, source_target_pairs={{0,1},{1,0},{2,3},{3,2},{4,5},{5,4},{6,7},{7,6},{8,9},{9,8},{10,11... | collective-permute-start | bytes 1253384 | tf_op jit(solution)/shard_map/ppermute | solution.py:25
  68.4 16.8 %collective-permute-start.28 = (bf16[64,2176]{1,0:T(8,128)(2,1)S(1)}, bf16[64,2176]{1,0:T(8,128)(2,1)S(1)}, u32[]{:S(2)}, u32[]{:S(2)}) collective-permute-start(bf16[64,2176]{1,0:T(8,128)(2,1)S(1)} %collective-permute-done.26.refs_1_), channel_id=1, source_target_pairs={{0,1},{1,0},{2,3},{3,2},{4,5},{5,4},{6,7},{7,6},{8,9},{9,8},{10,11... | collective-permute-start | bytes 835592 | tf_op jit(solution)/shard_map/ppermute | solution.py:25
  71.6 16.5 %collective-permute-start.18 = (bf16[256,2048]{1,0:T(8,128)(2,1)S(1)}, bf16[256,2048]{1,0:T(8,128)(2,1)S(1)}, u32[]{:S(2)}, u32[]{:S(2)}) collective-permute-start(bf16[256,2048]{1,0:T(8,128)(2,1)S(1)} %shard_map.123), channel_id=1, source_target_pairs={{0,1},{1,0},{2,3},{3,2},{4,5},{5,4},{6,7},{7,6},{8,9},{9,8},{10,11... | collective-permute-start | bytes 3145736 | tf_op jit(solution)/shard_map/ppermute | solution.py:25
  76.7 8.5 %collective-permute-start.27 = (bf16[96,2176]{1,0:T(8,128)(2,1)S(1)}, bf16[96,2176]{1,0:T(8,128)(2,1)S(1)}, u32[]{:S(2)}, u32[]{:S(2)}) collective-permute-start(bf16[96,2176]{1,0:T(8,128)(2,1)S(1)} %collective-permute-done.25.refs_0_), channel_id=1, source_target_pairs={{0,1},{1,0},{2,3},{3,2},{4,5},{5,4},{6,7},{7,6},{8,9},{9,8},{10,11... | collective-permute-start | bytes 1253384 | tf_op jit(solution)/shard_map/ppermute | solution.py:25
  78.4 8.7 %collective-permute-start.21 = (bf16[96,2048]{1,0:T(8,128)(2,1)S(1)}, bf16[96,2048]{1,0:T(8,128)(2,1)S(1)}, u32[]{:S(2)}, u32[]{:S(2)}) collective-permute-start(bf16[96,2048]{1,0:T(8,128)(2,1)S(1)} %shard_map.125), channel_id=1, source_target_pairs={{0,1},{1,0},{2,3},{3,2},{4,5},{5,4},{6,7},{7,6},{8,9},{9,8},{10,11... | collective-permute-start | bytes 1179656 | tf_op jit(solution)/shard_map/ppermute | solution.py:25
  87.2 11.6 %collective-permute-start.22 = (bf16[2,2,24,2048]{3,2,1,0:T(8,128)(2,1)S(1)}, bf16[2,2,24,2048]{3,2,1,0:T(8,128)(2,1)S(1)}, u32[]{:S(2)}, u32[]{:S(2)}) collective-permute-start(bf16[2,2,24,2048]{3,2,1,0:T(8,128)(2,1)S(1)} %bitcast.162), channel_id=1, source_target_pairs={{0,8},{4,12},{8,0},{12,4},{16,24},{20,28},{24,16},{28,20},{1,9},{5... | collective-permute-start | bytes 1179656 | tf_op jit(solution)/shard_map/ppermute | solution.py:25
  95.0 7.8 %collective-permute-start.31 = (bf16[2,8,2048]{2,1,0:T(8,128)(2,1)S(1)}, bf16[2,8,2048]{2,1,0:T(8,128)(2,1)S(1)}, u32[]{:S(2)}, u32[]{:S(2)}) collective-permute-start(bf16[2,8,2048]{2,1,0:T(8,128)(2,1)S(1)} %get-tuple-element.29), channel_id=1, source_target_pairs={{0,4},{4,0},{8,12},{12,8},{16,20},{20,16},{24,28},{28,24},{1,5},{5... | collective-permute-start | bytes 196616 | tf_op jit(solution)/shard_map/ppermute | solution.py:25
  98.8 7.8 %collective-permute-start.23 = (bf16[2,24,2048]{2,1,0:T(8,128)(2,1)S(1)}, bf16[2,24,2048]{2,1,0:T(8,128)(2,1)S(1)}, u32[]{:S(2)}, u32[]{:S(2)}) collective-permute-start(bf16[2,24,2048]{2,1,0:T(8,128)(2,1)S(1)} %get-tuple-element.25), channel_id=1, source_target_pairs={{0,4},{4,0},{8,12},{12,8},{16,20},{20,16},{24,28},{28,24},{1,5},{5... | collective-permute-start | bytes 589832 | tf_op jit(solution)/shard_map/ppermute | solution.py:25
  99.5 9.0 %collective-permute-start.33 = (bf16[2,2,16,2048]{3,2,1,0:T(8,128)(2,1)S(1)}, bf16[2,2,16,2048]{3,2,1,0:T(8,128)(2,1)S(1)}, u32[]{:S(2)}, u32[]{:S(2)}) collective-permute-start(bf16[2,2,16,2048]{3,2,1,0:T(8,128)(2,1)S(1)} %slice.281), channel_id=1, source_target_pairs={{0,2},{1,3},{2,0},{3,1},{4,6},{5,7},{6,4},{7,5},{8,10},{9,11},{10,... | collective-permute-start | bytes 786440 | tf_op jit(solution)/shard_map/ppermute | solution.py:25
  101.3 11.0 %collective-permute-start.36 = (bf16[2,2,16,2048]{3,2,1,0:T(8,128)(2,1)S(1)}, bf16[2,2,16,2048]{3,2,1,0:T(8,128)(2,1)S(1)}, u32[]{:S(2)}, u32[]{:S(2)}) collective-permute-start(bf16[2,2,16,2048]{3,2,1,0:T(8,128)(2,1)S(1)} %bitcast.163), channel_id=1, source_target_pairs={{0,4},{4,0},{8,12},{12,8},{16,20},{20,16},{24,28},{28,24},{1,5},{5... | collective-permute-start | bytes 786440 | tf_op jit(solution)/shard_map/ppermute | solution.py:25
  106.7 18.8 %collective-permute-start.24 = (bf16[24,2048]{1,0:T(8,128)(2,1)S(1)}, bf16[24,2048]{1,0:T(8,128)(2,1)S(1)}, u32[]{:S(2)}, u32[]{:S(2)}) collective-permute-start(bf16[24,2048]{1,0:T(8,128)(2,1)S(1)} %fusion.33), channel_id=1, source_target_pairs={{0,2},{1,3},{2,0},{3,1},{4,6},{5,7},{6,4},{7,5},{8,10},{9,11},{10,... | collective-permute-start | bytes 294920 | tf_op jit(solution)/shard_map/ppermute | solution.py:25
  121.8 6.9 %collective-permute-start.39 = (bf16[32,2048]{1,0:T(8,128)(2,1)S(1)}, bf16[32,2048]{1,0:T(8,128)(2,1)S(1)}, u32[]{:S(2)}, u32[]{:S(2)}) collective-permute-start(bf16[32,2048]{1,0:T(8,128)(2,1)S(1)} %pad_maximum_fusion.8), channel_id=1, source_target_pairs={{0,24},{4,28},{8,16},{12,20},{16,8},{20,12},{24,0},{28,4},{1,25},{... | collective-permute-start | bytes 393224 | tf_op jit(solution)/shard_map/ppermute | solution.py:25
  (26 other events, 228.0 us)
